TPU v7x, 128 devices: a whole 4x4x4 slice. The times are simulated.
128 devices in a mesh: basis: 16 (over x, z_lo, core), orb: 8 (over z_hi, y).
Axes of the slice: x: 4, y: 4, z: 4 (z_hi: 2, z_lo: 2; z = z_hi * 2 + z_lo), core: 2. Of those that a mesh axis runs over, the one named last changes fastest.
Arguments:
- cont_orbitals: bfloat16 [65536, 2048], P('basis', 'orb'), may hold values from -6 to 6
- target_orbitals: bfloat16 [65536, 1024], P('basis'), may hold values from -0.09375 to 0.09375
- margin_blocks: bfloat16 [256, 4, 256, 256], P('basis'), may hold values from -0.1875 to 0.1875
- dipole_blocks: bfloat16 [256, 4, 256, 256], P('basis'), may hold values from -0.1875 to 0.1875
- band_offsets: int32 [256, 4], P('basis'), may hold values from -2 to 2, as said below
Outputs:
- cont_orth: bfloat16 [65536, 2048], P('basis', 'orb')
- dipole_mo: bfloat16 [1024, 2048], P('basis', 'orb')
Inputs may be any that keep to these rules, and one draw needn't show every extreme that they name: `band_offsets`: each block row names 4 different offsets.
All inputs are finite; a program needn't handle non-finite values.
Results may differ from a plain program's by a relative error of at most 0.012.
Values may be sent and summed in bfloat16 or wider, within the bound.
A program may use at most 128 MiB of HBM per device.

v0:
```python
import jax
import jax.numpy as jnp
from jax import lax
from jax.sharding import PartitionSpec as P

BK = 256
KB = 4


def padded_2(block, sides, width):
    for axis, dim in sides:
        count = lax.axis_size(axis)
        forward = [(i, i + 1) for i in range(count - 1)]
        backward = [(target, source) for source, target in forward]
        low = lax.ppermute(
            lax.slice_in_dim(block, block.shape[dim] - width, None, axis=dim), axis, forward
        )
        high = lax.ppermute(lax.slice_in_dim(block, 0, width, axis=dim), axis, backward)
        block = jnp.concatenate([low, block, high], axis=dim)
    return block


def band_local(blocks, offsets, padded):
    nblk = blocks.shape[0]
    width = padded.shape[1]
    stacked = padded.reshape(nblk + 4, BK, width)
    total = jnp.zeros((nblk, BK, width), jnp.float32)
    for k in range(KB):
        index = jnp.arange(nblk, dtype=jnp.int32) + 2 + offsets[:, k]
        taken = stacked[index]
        total = total + jnp.einsum(
            "bij,bjc->bic", blocks[:, k], taken, preferred_element_type=jnp.float32
        )
    return total.reshape(nblk * BK, width)


def on_device(cont_orbitals, target_orbitals, margin_blocks, dipole_blocks, band_offsets):
    cont_padded = padded_2(cont_orbitals, (("basis", 0),), 2 * BK)
    margin_cont = band_local(margin_blocks, band_offsets, cont_padded).astype(jnp.bfloat16)
    partial_proj = lax.dot_general(
        target_orbitals, margin_cont, (((0,), (0,)), ((), ())), preferred_element_type=jnp.float32
    )
    projection = lax.psum(partial_proj, "basis")
    projection_b = projection.astype(jnp.bfloat16)
    removed = jnp.dot(target_orbitals, projection_b, preferred_element_type=jnp.float32)
    cont_orth = (cont_orbitals.astype(jnp.float32) - removed).astype(jnp.bfloat16)
    squares = jnp.sum(jnp.square(cont_orth.astype(jnp.float32)), axis=0)
    orth_padded = padded_2(cont_orth, (("basis", 0),), 2 * BK)
    total_squares = lax.psum(squares, "basis")
    col_norm = 1.0 / jnp.sqrt(
        total_squares / (band_offsets.shape[0] * BK * lax.axis_size("basis")) + 1e-06
    )
    dipole_cont = band_local(dipole_blocks, band_offsets, orth_padded).astype(jnp.bfloat16)
    dipole_raw = lax.psum_scatter(
        lax.dot_general(
            target_orbitals,
            dipole_cont,
            (((0,), (0,)), ((), ())),
            preferred_element_type=jnp.float32,
        ),
        "basis",
        scatter_dimension=0,
        tiled=True,
    )
    dipole_mo = (dipole_raw * col_norm[None, :]).astype(jnp.bfloat16)
    return (cont_orth, dipole_mo)


def solution(mesh):
    return jax.shard_map(
        on_device,
        mesh=mesh,
        in_specs=(
            P("basis", "orb"),
            P("basis", None),
            P("basis", None, None, None),
            P("basis", None, None, None),
            P("basis", None),
        ),
        out_specs=(P("basis", "orb"), P("basis", "orb")),
        check_vma=False,
    )
```

profile of v0, /device:TPU:1, one launch (start us, length us, event | category | flops | bytes accessed | tf_op | source)
XLA Modules:
  0.0 219.4 jit_solution(11804426336611701205)
XLA Ops:
  7.2 0.0 reduce-scatter.4.cloned.1.call-start
  7.2 1.1 fusion.30
  8.3 4.9 %collective-permute-start = (bf16[512,256]{1,0:T(8,128)(2,1)S(1)}, bf16[512,256]{1,0:T(8,128)(2,1)S(1)}, u32[]{:S(2)}, u32[]{:S(2)}) collective-permute-start(bf16[512,256]{1,0:T(8,128)(2,1)S(1)} %get-tuple-element.10), channel_id=1, source_target_pairs={{0,8},{8,16},{16,24},{24,32},{32,40},{40,48},{48,56},{56,64},{64,7... | collective-permute-start | bytes 786440 | tf_op jit(solution)/shard_map/ppermute | solution.py:15
  13.2 1.9 collective-permute-start.1
  15.2 0.8 fusion.28
  16.0 4.1 %copy.30 = bf16[4096,256]{0,1:T(8,128)(2,1)} copy(bf16[4096,256]{1,0:T(8,128)(2,1)} %param.5) | data formatting | bytes 4194304 | tf_op args[0]
  20.1 0.0 collective-permute-done
  20.1 0.8 collective-permute-done.1
  20.9 1.8 pad_maximum_fusion
  22.7 2.0 gather_fusion.3
  24.7 2.0 gather_fusion.2
  26.7 2.0 gather_fusion.1
  28.7 2.0 gather_fusion
  30.8 3.1 %fusion.10 = f32[16,256,256]{1,2,0:T(8,128)S(1)} fusion(bf16[16,256,256]{2,1,0:T(8,128)(2,1)} %gather_fusion.2, bf16[16,4,256,256]{3,2,1,0:T(8,128)(2,1)} %param.7), kind=kOutput, calls=%fused_computation.24 | convolution fusion | flops 536870912 | bytes 8388608 | tf_op jit(solution)/shard_map/bij,bjc->bic/dot_general | solution.py:31
  33.8 0.0 copy-done.7
  33.9 0.0 copy-start.5
  33.9 2.5 %fusion.14 = f32[16,256,256]{1,2,0:T(8,128)S(1)} fusion(bf16[16,256,256]{2,1,0:T(8,128)(2,1)S(1)} %copy-done.7, bf16[16,4,256,256]{3,2,1,0:T(8,128)(2,1)} %param.7), kind=kOutput, calls=%fused_computation.28 | convolution fusion | flops 536870912 | bytes 8388608 | tf_op jit(solution)/shard_map/bij,bjc->bic/dot_general | solution.py:31
  36.3 0.0 copy-done.5
  36.3 0.0 copy-start.3
  36.4 0.0 slice-start
  36.4 2.5 %fusion.12 = f32[16,256,256]{1,2,0:T(8,128)S(1)} fusion(bf16[16,256,256]{2,1,0:T(8,128)(2,1)S(1)} %copy-done.5, bf16[16,4,256,256]{3,2,1,0:T(8,128)(2,1)} %param.7), kind=kOutput, calls=%fused_computation.26 | convolution fusion | flops 536870912 | bytes 8388608 | tf_op jit(solution)/shard_map/bij,bjc->bic/dot_general | solution.py:31
  38.8 0.0 copy-done.3
  38.9 0.0 slice-start.1
  38.9 3.0 %add_convert_fusion.1 = bf16[16,256,256]{1,2,0:T(8,128)(2,1)S(1)} fusion(f32[16,256,256]{1,2,0:T(8,128)S(1)} %fusion.10, f32[16,256,256]{1,2,0:T(8,128)S(1)} %fusion.14, f32[16,256,256]{1,2,0:T(8,128)S(1)} %fusion.12, bf16[16,256,256]{2,1,0:T(8,128)(2,1)S(1)} %copy-done.3, bf16[16,4,256,256]{3,2,1,0:T(8,128)(2,1)} %param.7), kind=kOutput, calls=%fused_computation.13 | convolution fusion | flops 541065216 | bytes 18874368 | tf_op jit(solution)/shard_map/bij,bjc->bic/dot_general | solution.py:31
  41.8 0.0 slice-done
  41.8 0.1 slice-done.1
  41.9 2.3 %convolution_bitcast_fusion.2 = f32[1024,256]{0,1:T(8,128)S(1)} fusion(bf16[4096,256]{1,0:T(8,128)(2,1)S(1)} %bitcast.93, bf16[4096,1024]{1,0:T(8,128)(2,1)S(1)} %bitcast.82), kind=kOutput, calls=%fused_computation.39 | convolution fusion | flops 2147483648 | bytes 11534336 | tf_op jit(solution)/shard_map/dot_general | solution.py:40
  44.3 62.0 %all-reduce.1 = bf16[1024,256]{0,1:T(8,128)(2,1)} all-reduce(f32[1024,256]{0,1:T(8,128)S(1)} %convolution_bitcast_fusion.2), channel_id=1, replica_groups=mesh['basis'=16,'orb'=8] {'basis'}, use_global_device_ids=true, to_apply=%region_0.0 | all-reduce | flops 262144 | bytes 1572864 | tf_op jit(solution)/shard_map/psum | solution.py:43
  106.3 0.0 copy-done.8
  106.3 6.2 %multiply_reduce_fusion = (f32[256]{0:T(256)S(1)}, bf16[4096,256]{0,1:T(8,128)(2,1)S(1)}) fusion(bf16[1024,256]{0,1:T(8,128)(2,1)} %all-reduce.1, bf16[4096,1024]{1,0:T(8,128)(2,1)} %param.6, bf16[4096,256]{0,1:T(8,128)(2,1)S(1)} %copy-done.8), kind=kOutput, calls=%fused_computation.11 | convolution fusion | flops 2153774848 | bytes 13108224 | tf_op jit(solution)/shard_map/dot_general | solution.py:45
  112.5 0.0 copy-start
  112.5 3.3 %collective-permute-start.2 = (bf16[512,256]{0,1:T(8,128)(2,1)S(1)}, bf16[512,256]{0,1:T(8,128)(2,1)S(1)}, u32[]{:S(2)}, u32[]{:S(2)}) collective-permute-start(bf16[512,256]{0,1:T(8,128)(2,1)S(1)} %get-tuple-element.8), channel_id=1, source_target_pairs={{0,8},{8,16},{16,24},{24,32},{32,40},{40,48},{48,56},{56,64},{64,7... | collective-permute-start | bytes 786440 | tf_op jit(solution)/shard_map/ppermute | solution.py:15
  115.9 4.8 %collective-permute-start.3 = (bf16[512,256]{0,1:T(8,128)(2,1)S(1)}, bf16[512,256]{0,1:T(8,128)(2,1)S(1)}, u32[]{:S(2)}, u32[]{:S(2)}) collective-permute-start(bf16[512,256]{0,1:T(8,128)(2,1)S(1)} %get-tuple-element.9), channel_id=1, source_target_pairs={{8,0},{16,8},{24,16},{32,24},{40,32},{48,40},{56,48},{64,56},{72,6... | collective-permute-start | bytes 786440 | tf_op jit(solution)/shard_map/ppermute | solution.py:18
  120.7 1.3 collective-permute-done.2
  122.0 1.6 collective-permute-done.3
  123.6 0.0 copy-done
  123.6 1.7 pad_maximum_fusion.1
  125.3 3.0 %copy.35 = bf16[5120,256]{1,0:T(8,128)(2,1)S(1)} copy(bf16[5120,256]{0,1:T(8,128)(2,1)} %pad_maximum_fusion.1) | data formatting | bytes 5242880 | tf_op jit(solution)/shard_map/concatenate | solution.py:19
  128.3 2.0 gather_fusion.7
  130.3 2.0 gather_fusion.6
  132.3 2.0 gather_fusion.5
  134.3 2.0 gather_fusion.4
  136.4 3.1 %fusion.7 = f32[16,256,256]{1,2,0:T(8,128)S(1)} fusion(bf16[16,256,256]{2,1,0:T(8,128)(2,1)} %gather_fusion.4, bf16[16,4,256,256]{3,2,1,0:T(8,128)(2,1)} %param.8), kind=kOutput, calls=%fused_computation.21 | convolution fusion | flops 536870912 | bytes 8388608 | tf_op jit(solution)/shard_map/bij,bjc->bic/dot_general | solution.py:31
  139.5 0.0 copy-done.6
  139.5 0.0 copy-start.4
  139.5 2.5 %fusion.5 = f32[16,256,256]{1,2,0:T(8,128)S(1)} fusion(bf16[16,256,256]{2,1,0:T(8,128)(2,1)S(1)} %copy-done.6, bf16[16,4,256,256]{3,2,1,0:T(8,128)(2,1)} %param.8), kind=kOutput, calls=%fused_computation.19 | convolution fusion | flops 536870912 | bytes 8388608 | tf_op jit(solution)/shard_map/bij,bjc->bic/dot_general | solution.py:31
  142.0 0.0 copy-done.4
  142.0 0.0 copy-start.2
  142.0 0.0 slice-start.2
  142.0 2.5 %fusion.3 = f32[16,256,256]{1,2,0:T(8,128)S(1)} fusion(bf16[16,256,256]{2,1,0:T(8,128)(2,1)S(1)} %copy-done.4, bf16[16,4,256,256]{3,2,1,0:T(8,128)(2,1)} %param.8), kind=kOutput, calls=%fused_computation.17 | convolution fusion | flops 536870912 | bytes 8388608 | tf_op jit(solution)/shard_map/bij,bjc->bic/dot_general | solution.py:31
  144.5 0.0 slice-start.3
  144.5 3.0 %add_convert_fusion = bf16[16,256,256]{1,2,0:T(8,128)(2,1)S(1)} fusion(f32[16,256,256]{1,2,0:T(8,128)S(1)} %fusion.3, f32[16,256,256]{1,2,0:T(8,128)S(1)} %fusion.7, f32[16,256,256]{1,2,0:T(8,128)S(1)} %fusion.5, bf16[16,256,256]{2,1,0:T(8,128)(2,1)S(1)} %copy-done.2, bf16[16,4,256,256]{3,2,1,0:T(8,128)(2,1)} %param.8), kind=kOutput, calls=%fused_computation.12 | convolution fusion | flops 541065216 | bytes 18874368 | tf_op jit(solution)/shard_map/bij,bjc->bic/dot_general | solution.py:31
  147.5 0.1 slice-done.3
  147.5 2.3 %convolution_bitcast_fusion.1 = f32[1024,256]{0,1:T(8,128)S(1)} fusion(bf16[4096,256]{1,0:T(8,128)(2,1)S(1)} %bitcast.94, bf16[4096,1024]{1,0:T(8,128)(2,1)S(1)} %bitcast.84), kind=kOutput, calls=%fused_computation.38 | convolution fusion | flops 2147483648 | bytes 11534336 | tf_op jit(solution)/shard_map/dot_general | solution.py:55
  149.9 0.0 copy-start.1
  149.9 1.3 copy.42
  151.2 0.0 reduce-scatter.4.cloned.1.call-update
  151.2 0.6 copy-done.1
  151.9 2.4 %copy.40 = bf16[4096,256]{1,0:T(8,128)(2,1)} copy(bf16[4096,256]{0,1:T(8,128)(2,1)S(1)} %copy-done.1) | data formatting | bytes 4194304
  154.3 25.4 %psum.15 = f32[256]{0:T(256)S(1)} all-reduce(f32[256]{0:T(256)S(1)} %get-tuple-element.16), channel_id=1, replica_groups=mesh['basis'=16,'orb'=8] {'basis'}, use_global_device_ids=true, to_apply=%region_3.0 | all-reduce | flops 256 | bytes 2048 | tf_op jit(solution)/shard_map/psum | solution.py:49
  179.7 31.1 %reduce-scatter.4.cloned.1.call-done = f32[64,256]{1,0:T(8,128)} async-done(((f32[1024,256]{1,0:T(8,128)}), f32[64,256]{1,0:T(8,128)}) %reduce-scatter.4.cloned.1.call-update) | async-done | bytes 65552
  210.8 0.9 copy.43
  211.7 0.1 multiply_convert_fusion
  211.9 0.7 copy.41
  (11 shorter events, 0.1 us)
Async XLA Ops:
  7.2 203.6 %reduce-scatter.4.cloned.1.call-start = ((), (), s32[]{:S(2)}) async-start(), calls=%async_computation.1 | async-start | bytes 1114112
  8.3 11.8 %collective-permute-start = (bf16[512,256]{1,0:T(8,128)(2,1)S(1)}, bf16[512,256]{1,0:T(8,128)(2,1)S(1)}, u32[]{:S(2)}, u32[]{:S(2)}) collective-permute-start(bf16[512,256]{1,0:T(8,128)(2,1)S(1)} %get-tuple-element.10), channel_id=1, source_target_pairs={{0,8},{8,16},{16,24},{24,32},{32,40},{40,48},{48,56},{56,64},{64,7... | collective-permute-start | bytes 786440 | tf_op jit(solution)/shard_map/ppermute | solution.py:15
  13.2 7.7 %collective-permute-start.1 = (bf16[512,256]{1,0:T(8,128)(2,1)S(1)}, bf16[512,256]{1,0:T(8,128)(2,1)S(1)}, u32[]{:S(2)}, u32[]{:S(2)}) collective-permute-start(bf16[512,256]{1,0:T(8,128)(2,1)S(1)} %get-tuple-element.11), channel_id=1, source_target_pairs={{8,0},{16,8},{24,16},{32,24},{40,32},{48,40},{56,48},{64,56},{72,6... | collective-permute-start | bytes 786440 | tf_op jit(solution)/shard_map/ppermute | solution.py:18
  30.8 3.1 %copy-start.7 = (bf16[16,256,256]{2,1,0:T(8,128)(2,1)S(1)}, bf16[16,256,256]{2,1,0:T(8,128)(2,1)}, u32[]{:S(2)}) copy-start(bf16[16,256,256]{2,1,0:T(8,128)(2,1)} %gather_fusion) | copy-start | bytes 6291460
  33.9 2.5 %copy-start.5 = (bf16[16,256,256]{2,1,0:T(8,128)(2,1)S(1)}, bf16[16,256,256]{2,1,0:T(8,128)(2,1)}, u32[]{:S(2)}) copy-start(bf16[16,256,256]{2,1,0:T(8,128)(2,1)} %gather_fusion.1) | copy-start | bytes 6291460
  36.3 2.5 %copy-start.3 = (bf16[16,256,256]{2,1,0:T(8,128)(2,1)S(1)}, bf16[16,256,256]{2,1,0:T(8,128)(2,1)}, u32[]{:S(2)}) copy-start(bf16[16,256,256]{2,1,0:T(8,128)(2,1)} %gather_fusion.3) | copy-start | bytes 6291460
  36.4 5.5 %slice-start = ((s8[8388608]{0:T(1024)(128)(4,1)}), s8[4194304]{0:T(1024)(128)(4,1)S(1)}, s32[]{:S(2)}) async-start(s8[8388608]{0:T(1024)(128)(4,1)} %bitcast.81), calls=%async_computation.2 | async-start | bytes 8388608
  38.9 3.1 %slice-start.1 = ((s8[8388608]{0:T(1024)(128)(4,1)}), s8[4194304]{0:T(1024)(128)(4,1)S(1)}, s32[]{:S(2)}) async-start(s8[8388608]{0:T(1024)(128)(4,1)} %bitcast.81), calls=%async_computation.3 | async-start | bytes 8388608
  41.9 64.3 %copy-start.8 = (bf16[4096,256]{0,1:T(8,128)(2,1)S(1)}, bf16[4096,256]{0,1:T(8,128)(2,1)}, u32[]{:S(2)}) copy-start(bf16[4096,256]{0,1:T(8,128)(2,1)} %copy.30) | copy-start | bytes 6291460
  112.5 11.1 %copy-start = (bf16[4096,256]{0,1:T(8,128)(2,1)}, bf16[4096,256]{0,1:T(8,128)(2,1)S(1)}, u32[]{:S(2)}) copy-start(bf16[4096,256]{0,1:T(8,128)(2,1)S(1)} %get-tuple-element.17) | copy-start | bytes 6291460
  112.5 9.4 %collective-permute-start.2 = (bf16[512,256]{0,1:T(8,128)(2,1)S(1)}, bf16[512,256]{0,1:T(8,128)(2,1)S(1)}, u32[]{:S(2)}, u32[]{:S(2)}) collective-permute-start(bf16[512,256]{0,1:T(8,128)(2,1)S(1)} %get-tuple-element.8), channel_id=1, source_target_pairs={{0,8},{8,16},{16,24},{24,32},{32,40},{40,48},{48,56},{56,64},{64,7... | collective-permute-start | bytes 786440 | tf_op jit(solution)/shard_map/ppermute | solution.py:15
  115.9 7.7 %collective-permute-start.3 = (bf16[512,256]{0,1:T(8,128)(2,1)S(1)}, bf16[512,256]{0,1:T(8,128)(2,1)S(1)}, u32[]{:S(2)}, u32[]{:S(2)}) collective-permute-start(bf16[512,256]{0,1:T(8,128)(2,1)S(1)} %get-tuple-element.9), channel_id=1, source_target_pairs={{8,0},{16,8},{24,16},{32,24},{40,32},{48,40},{56,48},{64,56},{72,6... | collective-permute-start | bytes 786440 | tf_op jit(solution)/shard_map/ppermute | solution.py:18
  136.4 3.1 %copy-start.6 = (bf16[16,256,256]{2,1,0:T(8,128)(2,1)S(1)}, bf16[16,256,256]{2,1,0:T(8,128)(2,1)}, u32[]{:S(2)}) copy-start(bf16[16,256,256]{2,1,0:T(8,128)(2,1)} %gather_fusion.5) | copy-start | bytes 6291460
  139.5 2.5 %copy-start.4 = (bf16[16,256,256]{2,1,0:T(8,128)(2,1)S(1)}, bf16[16,256,256]{2,1,0:T(8,128)(2,1)}, u32[]{:S(2)}) copy-start(bf16[16,256,256]{2,1,0:T(8,128)(2,1)} %gather_fusion.6) | copy-start | bytes 6291460
  142.0 2.5 %copy-start.2 = (bf16[16,256,256]{2,1,0:T(8,128)(2,1)S(1)}, bf16[16,256,256]{2,1,0:T(8,128)(2,1)}, u32[]{:S(2)}) copy-start(bf16[16,256,256]{2,1,0:T(8,128)(2,1)} %gather_fusion.7) | copy-start | bytes 6291460
  142.0 5.5 %slice-start.2 = ((s8[8388608]{0:T(1024)(128)(4,1)}), s8[4194304]{0:T(1024)(128)(4,1)S(1)}, s32[]{:S(2)}) async-start(s8[8388608]{0:T(1024)(128)(4,1)} %bitcast.83), calls=%async_computation.4 | async-start | bytes 8388608
  144.5 3.1 %slice-start.3 = ((s8[8388608]{0:T(1024)(128)(4,1)}), s8[4194304]{0:T(1024)(128)(4,1)S(1)}, s32[]{:S(2)}) async-start(s8[8388608]{0:T(1024)(128)(4,1)} %bitcast.83), calls=%async_computation.5 | async-start | bytes 8388608
  149.9 2.0 copy-start.1
Sparse Core Ops, SparseCore 0:
  151.4 59.4 reduce-scatter.3
where the time goes:
time: 223 us; the launch traced here: 219 us
  blocking collectives  87.4 us (39%)
  waiting for transfers between devices  34.8 us (16%)
  matrix products  32.8 us (15%)
  local copies, waits for them, and re-layouts  30.6 us (14%)
  starting transfers between devices  15 us (7%)
  between operations  14.3 us (6%)
  other arithmetic  4.46 us (2%)
    psum x1, blocking collectives, on_device(): projection = lax.psum(partial_proj, 'basis')  62 us
    unnamed x2, waiting for transfers between devices  31.1 us
    psum x1, blocking collectives, on_device(): total_squares = lax.psum(squares, 'basis')  25.4 us
    dot_general x8, matrix products, band_local(): jnp.einsum('bij,bjc->bic', blocks[:, k], taken, preferred_element_type=jn...  21.9 us
    gather x8, local copies, waits for them, and re-layouts, band_local(): taken = stacked[index]  16.2 us
    unnamed x31, local copies, waits for them, and re-layouts  10.3 us
    ppermute x2, starting transfers between devices, padded_2(): lax.ppermute(lax.slice_in_dim(block, block.shape[dim] - width, None, axis...  8.26 us
    ppermute x2, starting transfers between devices, padded_2(): lax.ppermute(lax.slice_in_dim(block, 0, width, axis=dim), axis, backward)  6.72 us
  transfers between devices with their start and end apart: 5, of which 4 were waited for; matrix products, arithmetic and copies ran while one was open for 3% of the time, Pallas kernels for 0%

commit v1 on v0

--- a/solution.py
+++ b/solution.py
@@ -1,10 +1,15 @@
+import functools
+
 import jax
 import jax.numpy as jnp
 from jax import lax
+from jax.experimental import pallas as pl
+from jax.experimental.pallas import tpu as pltpu
 from jax.sharding import PartitionSpec as P
 
 BK = 256
 KB = 4
+MESH = pl.DeviceIdType.MESH
 
 
 def padded_2(block, sides, width):
@@ -34,35 +39,156 @@
     return total.reshape(nblk * BK, width)
 
 
+def _barrier_all(n, me, orb):
+    barrier = pltpu.get_barrier_semaphore()
+    for j in range(1, n):
+        peer = lax.rem(me + j, n)
+        pl.semaphore_signal(barrier, inc=1, device_id=(peer, orb), device_id_type=MESH)
+    pl.semaphore_wait(barrier, n - 1)
+
+
+def _scatter_sum(n, me, orb, x_ref, recv, send_sem, recv_sem):
+    sends = []
+    for j in range(1, n):
+        peer = lax.rem(me + j, n)
+        c = pltpu.make_async_remote_copy(
+            src_ref=x_ref.at[peer],
+            dst_ref=recv.at[me],
+            send_sem=send_sem.at[j],
+            recv_sem=recv_sem.at[me],
+            device_id=(peer, orb),
+            device_id_type=MESH,
+        )
+        c.start()
+        sends.append(c)
+    acc = x_ref[me]
+    for j in range(1, n):
+        src = lax.rem(me + n - j, n)
+        pltpu.make_async_remote_copy(
+            src_ref=x_ref.at[src],
+            dst_ref=recv.at[src],
+            send_sem=send_sem.at[j],
+            recv_sem=recv_sem.at[src],
+            device_id=(src, orb),
+            device_id_type=MESH,
+        ).wait_recv()
+        acc = acc + recv[src]
+    for c in sends:
+        c.wait_send()
+    return acc
+
+
+def allreduce_kernel(n, x_ref, out_ref, recv, sendbuf, gath, rs_send, rs_recv, ag_send, ag_recv):
+    me = lax.axis_index("basis")
+    orb = lax.axis_index("orb")
+    _barrier_all(n, me, orb)
+    total = _scatter_sum(n, me, orb, x_ref, recv, rs_send, rs_recv)
+    rounded = total.astype(out_ref.dtype)
+    sendbuf[...] = rounded
+    out_ref[me] = rounded
+    sends = []
+    for j in range(1, n):
+        peer = lax.rem(me + j, n)
+        c = pltpu.make_async_remote_copy(
+            src_ref=sendbuf,
+            dst_ref=gath.at[me],
+            send_sem=ag_send.at[j],
+            recv_sem=ag_recv.at[me],
+            device_id=(peer, orb),
+            device_id_type=MESH,
+        )
+        c.start()
+        sends.append(c)
+    for j in range(1, n):
+        src = lax.rem(me + n - j, n)
+        pltpu.make_async_remote_copy(
+            src_ref=sendbuf,
+            dst_ref=gath.at[src],
+            send_sem=ag_send.at[j],
+            recv_sem=ag_recv.at[src],
+            device_id=(src, orb),
+            device_id_type=MESH,
+        ).wait_recv()
+        out_ref[src] = gath[src]
+    for c in sends:
+        c.wait_send()
+
+
+def allreduce_to_bf16(partial, n):
+    rows, cols = partial.shape
+    chunk = rows // n
+    x = partial.reshape(n, chunk, cols)
+    out = pl.pallas_call(
+        functools.partial(allreduce_kernel, n),
+        out_shape=jax.ShapeDtypeStruct((n, chunk, cols), jnp.bfloat16),
+        in_specs=[pl.BlockSpec(memory_space=pltpu.VMEM)],
+        out_specs=pl.BlockSpec(memory_space=pltpu.VMEM),
+        scratch_shapes=[
+            pltpu.VMEM((n, chunk, cols), jnp.float32),
+            pltpu.VMEM((chunk, cols), jnp.bfloat16),
+            pltpu.VMEM((n, chunk, cols), jnp.bfloat16),
+            pltpu.SemaphoreType.DMA((n,)),
+            pltpu.SemaphoreType.DMA((n,)),
+            pltpu.SemaphoreType.DMA((n,)),
+            pltpu.SemaphoreType.DMA((n,)),
+        ],
+        compiler_params=pltpu.CompilerParams(collective_id=0, has_side_effects=True),
+    )(x)
+    return out.reshape(rows, cols)
+
+
+def dipole_kernel(n, chunk, count, x_ref, out_ref, recv, rs_send, rs_recv):
+    me = lax.axis_index("basis")
+    orb = lax.axis_index("orb")
+    _barrier_all(n, me, orb)
+    total = _scatter_sum(n, me, orb, x_ref, recv, rs_send, rs_recv)
+    squares = total[chunk:chunk + 1, :]
+    col_norm = 1.0 / jnp.sqrt(squares / count + 1e-06)
+    out_ref[...] = (total[:chunk, :] * col_norm).astype(out_ref.dtype)
+
+
+def dipole_scatter(partial, squares, n, count):
+    rows, cols = partial.shape
+    chunk = rows // n
+    x = jnp.concatenate(
+        [partial.reshape(n, chunk, cols), jnp.broadcast_to(squares[None, None, :], (n, 8, cols))],
+        axis=1,
+    )
+    return pl.pallas_call(
+        functools.partial(dipole_kernel, n, chunk, count),
+        out_shape=jax.ShapeDtypeStruct((chunk, cols), jnp.bfloat16),
+        in_specs=[pl.BlockSpec(memory_space=pltpu.VMEM)],
+        out_specs=pl.BlockSpec(memory_space=pltpu.VMEM),
+        scratch_shapes=[
+            pltpu.VMEM((n, chunk + 8, cols), jnp.float32),
+            pltpu.SemaphoreType.DMA((n,)),
+            pltpu.SemaphoreType.DMA((n,)),
+        ],
+        compiler_params=pltpu.CompilerParams(collective_id=1, has_side_effects=True),
+    )(x)
+
+
 def on_device(cont_orbitals, target_orbitals, margin_blocks, dipole_blocks, band_offsets):
+    n = lax.axis_size("basis")
+    count = band_offsets.shape[0] * BK * n
     cont_padded = padded_2(cont_orbitals, (("basis", 0),), 2 * BK)
     margin_cont = band_local(margin_blocks, band_offsets, cont_padded).astype(jnp.bfloat16)
     partial_proj = lax.dot_general(
         target_orbitals, margin_cont, (((0,), (0,)), ((), ())), preferred_element_type=jnp.float32
     )
-    projection = lax.psum(partial_proj, "basis")
-    projection_b = projection.astype(jnp.bfloat16)
+    projection_b = allreduce_to_bf16(partial_proj, n)
     removed = jnp.dot(target_orbitals, projection_b, preferred_element_type=jnp.float32)
     cont_orth = (cont_orbitals.astype(jnp.float32) - removed).astype(jnp.bfloat16)
     squares = jnp.sum(jnp.square(cont_orth.astype(jnp.float32)), axis=0)
     orth_padded = padded_2(cont_orth, (("basis", 0),), 2 * BK)
-    total_squares = lax.psum(squares, "basis")
-    col_norm = 1.0 / jnp.sqrt(
-        total_squares / (band_offsets.shape[0] * BK * lax.axis_size("basis")) + 1e-06
-    )
     dipole_cont = band_local(dipole_blocks, band_offsets, orth_padded).astype(jnp.bfloat16)
-    dipole_raw = lax.psum_scatter(
-        lax.dot_general(
-            target_orbitals,
-            dipole_cont,
-            (((0,), (0,)), ((), ())),
-            preferred_element_type=jnp.float32,
-        ),
-        "basis",
-        scatter_dimension=0,
-        tiled=True,
-    )
-    dipole_mo = (dipole_raw * col_norm[None, :]).astype(jnp.bfloat16)
+    partial_dip = lax.dot_general(
+        target_orbitals,
+        dipole_cont,
+        (((0,), (0,)), ((), ())),
+        preferred_element_type=jnp.float32,
+    )
+    dipole_mo = dipole_scatter(partial_dip, squares, n, count)
     return (cont_orth, dipole_mo)
 
 

time: 223 us -> 139 us (0.62)
  blocking collectives: 87.4 us -> 0 us
  Pallas kernels: 0 us -> 51.2 us
  waiting for transfers between devices: 34.8 us -> 3.95 us
  between operations: 14.3 us -> 0.91 us
  starting transfers between devices: 15 us -> 12.4 us
    psum x2 -> x0, blocking collectives: 87.4 us -> none  [the longest x1 62 us: on_device(): projection = lax.psum(partial_proj, 'basis')]
    pallas_call x0 -> x2, Pallas kernels: none -> 51.2 us  [the longest x1 31.2 us: allreduce_to_bf16(): pl.pallas_call(functools.partial(allreduce_kernel, n), out_shape=jax.Shap...]
    unnamed x2 -> x0, waiting for transfers between devices: 31.1 us -> none
    ppermute x2, starting transfers between devices: 6.72 us -> 4.02 us  [padded_2(): lax.ppermute(lax.slice_in_dim(block, 0, width, axis=dim), axis, backward)]
    unnamed x31 -> x23, local copies, waits for them, and re-layouts: 10.3 us -> 8.12 us
  transfers between devices with their start and end apart: 5 -> 4, of which waited for: 4 -> 2; matrix products, arithmetic and copies ran while one was open for 3% -> 5% of each run, Pallas kernels for 0% -> 0%
where the time goes in v1:
time: 139 us; the launch traced here: 137 us
  Pallas kernels  51.2 us (37%)
  matrix products  33.5 us (24%)
  local copies, waits for them, and re-layouts  30 us (22%)
  starting transfers between devices  12.4 us (9%)
  other arithmetic  5.47 us (4%)
  waiting for transfers between devices  3.95 us (3%)
    pallas_call x1, Pallas kernels, allreduce_to_bf16(): pl.pallas_call(functools.partial(allreduce_kernel, n), out_shape=jax.Shap...  31.2 us
    dot_general x8, matrix products, band_local(): jnp.einsum('bij,bjc->bic', blocks[:, k], taken, preferred_element_type=jn...  21.9 us
    pallas_call x1, Pallas kernels, dipole_scatter(): pl.pallas_call(functools.partial(dipole_kernel, n, chunk, count), out_sha...  19.9 us
    gather x8, local copies, waits for them, and re-layouts, band_local(): taken = stacked[index]  16.1 us
    ppermute x2, starting transfers between devices, padded_2(): lax.ppermute(lax.slice_in_dim(block, block.shape[dim] - width, None, axis...  8.4 us
    unnamed x23, local copies, waits for them, and re-layouts  8.12 us
    dot_general x1, matrix products, on_device(): jnp.dot(target_orbitals, projection_b, preferred_element_type=jnp.float32)  6.87 us
    ppermute x2, starting transfers between devices, padded_2(): lax.ppermute(lax.slice_in_dim(block, 0, width, axis=dim), axis, backward)  4.02 us
  transfers between devices with their start and end apart: 4, of which 2 were waited for; matrix products, arithmetic and copies ran while one was open for 5% of the time, Pallas kernels for 0%

profile of v1, /device:TPU:1, one launch (start us, length us, event | category | flops | bytes accessed | tf_op | source)
XLA Modules:
  0.0 137.4 jit_solution(5481509026290228014)
XLA Ops:
  0.6 1.1 fusion.29
  1.7 4.9 %collective-permute-start = (bf16[512,256]{1,0:T(8,128)(2,1)S(1)}, bf16[512,256]{1,0:T(8,128)(2,1)S(1)}, u32[]{:S(2)}, u32[]{:S(2)}) collective-permute-start(bf16[512,256]{1,0:T(8,128)(2,1)S(1)} %get-tuple-element.8), channel_id=1, source_target_pairs={{0,8},{8,16},{16,24},{24,32},{32,40},{40,48},{48,56},{56,64},{64,7... | collective-permute-start | bytes 786440 | tf_op jit(solution)/shard_map/ppermute | solution.py:20
  6.6 1.9 %collective-permute-start.1 = (bf16[512,256]{1,0:T(8,128)(2,1)S(1)}, bf16[512,256]{1,0:T(8,128)(2,1)S(1)}, u32[]{:S(2)}, u32[]{:S(2)}) collective-permute-start(bf16[512,256]{1,0:T(8,128)(2,1)S(1)} %get-tuple-element.9), channel_id=1, source_target_pairs={{8,0},{16,8},{24,16},{32,24},{40,32},{48,40},{56,48},{64,56},{72,6... | collective-permute-start | bytes 786440 | tf_op jit(solution)/shard_map/ppermute | solution.py:23
  8.6 0.8 fusion.27
  9.4 4.1 %copy.19 = bf16[4096,256]{0,1:T(8,128)(2,1)} copy(bf16[4096,256]{1,0:T(8,128)(2,1)} %param.5) | data formatting | bytes 4194304 | tf_op args[0]
  13.5 0.0 collective-permute-done
  13.5 0.8 collective-permute-done.1
  14.3 1.8 %pad_maximum_fusion = bf16[5120,256]{1,0:T(8,128)(2,1)S(1)} fusion(bf16[512,256]{1,0:T(8,128)(2,1)S(1)} %collective-permute-done.1, bf16[4096,256]{1,0:T(8,128)(2,1)} %param.5, bf16[512,256]{1,0:T(8,128)(2,1)S(1)} %collective-permute-done), kind=kLoop, calls=%fused_computation.14 | loop fusion | flops 7864320 | bytes 5242880 | tf_op jit(solution)/shard_map/concatenate | solution.py:24
  16.1 2.0 %gather_fusion.3 = bf16[16,256,256]{2,1,0:T(8,128)(2,1)} fusion(bf16[20,256,256]{2,1,0:T(8,128)(2,1)S(1)} %bitcast.91, s32[1024]{0:T(1024)S(1)} %get-tuple-element.16), kind=kCustom, calls=%fused_computation.3 | custom fusion | bytes 4194368 | tf_op jit(solution)/shard_map/gather | solution.py:35
  18.1 2.0 %gather_fusion.2 = bf16[16,256,256]{2,1,0:T(8,128)(2,1)} fusion(bf16[20,256,256]{2,1,0:T(8,128)(2,1)S(1)} %bitcast.92, s32[1024]{0:T(1024)S(1)} %get-tuple-element.17), kind=kCustom, calls=%fused_computation.2 | custom fusion | bytes 4194368 | tf_op jit(solution)/shard_map/gather | solution.py:35
  20.1 2.0 %gather_fusion.1 = bf16[16,256,256]{2,1,0:T(8,128)(2,1)} fusion(bf16[20,256,256]{2,1,0:T(8,128)(2,1)S(1)} %bitcast.93, s32[1024]{0:T(1024)S(1)} %get-tuple-element.18), kind=kCustom, calls=%fused_computation.1 | custom fusion | bytes 4194368 | tf_op jit(solution)/shard_map/gather | solution.py:35
  22.1 2.0 %gather_fusion = bf16[16,256,256]{2,1,0:T(8,128)(2,1)} fusion(bf16[20,256,256]{2,1,0:T(8,128)(2,1)S(1)} %bitcast.94, s32[1024]{0:T(1024)S(1)} %get-tuple-element.19), kind=kCustom, calls=%fused_computation | custom fusion | bytes 4194368 | tf_op jit(solution)/shard_map/gather | solution.py:35
  24.2 0.0 copy-start.5
  24.2 3.1 %fusion.10 = f32[16,256,256]{1,2,0:T(8,128)S(1)} fusion(bf16[16,256,256]{2,1,0:T(8,128)(2,1)} %gather_fusion.2, bf16[16,4,256,256]{3,2,1,0:T(8,128)(2,1)} %param.7), kind=kOutput, calls=%fused_computation.24 | convolution fusion | flops 536870912 | bytes 8388608 | tf_op jit(solution)/shard_map/bij,bjc->bic/dot_general | solution.py:36
  27.2 0.0 copy-done.5
  27.3 0.0 copy-start.3
  27.3 2.5 %fusion.14 = f32[16,256,256]{1,2,0:T(8,128)S(1)} fusion(bf16[16,256,256]{2,1,0:T(8,128)(2,1)S(1)} %copy-done.5, bf16[16,4,256,256]{3,2,1,0:T(8,128)(2,1)} %param.7), kind=kOutput, calls=%fused_computation.28 | convolution fusion | flops 536870912 | bytes 8388608 | tf_op jit(solution)/shard_map/bij,bjc->bic/dot_general | solution.py:36
  29.7 0.0 copy-done.3
  29.7 0.0 copy-start.1
  29.8 0.0 slice-start
  29.8 2.5 %fusion.12 = f32[16,256,256]{1,2,0:T(8,128)S(1)} fusion(bf16[16,256,256]{2,1,0:T(8,128)(2,1)S(1)} %copy-done.3, bf16[16,4,256,256]{3,2,1,0:T(8,128)(2,1)} %param.7), kind=kOutput, calls=%fused_computation.26 | convolution fusion | flops 536870912 | bytes 8388608 | tf_op jit(solution)/shard_map/bij,bjc->bic/dot_general | solution.py:36
  32.2 0.0 copy-done.1
  32.3 0.0 slice-start.1
  32.3 3.0 %add_convert_fusion.1 = bf16[16,256,256]{1,2,0:T(8,128)(2,1)S(1)} fusion(f32[16,256,256]{1,2,0:T(8,128)S(1)} %fusion.10, f32[16,256,256]{1,2,0:T(8,128)S(1)} %fusion.14, f32[16,256,256]{1,2,0:T(8,128)S(1)} %fusion.12, bf16[16,256,256]{2,1,0:T(8,128)(2,1)S(1)} %copy-done.1, bf16[16,4,256,256]{3,2,1,0:T(8,128)(2,1)} %param.7), kind=kOutput, calls=%fused_computation.13 | convolution fusion | flops 541065216 | bytes 18874368 | tf_op jit(solution)/shard_map/bij,bjc->bic/dot_general | solution.py:36
  35.2 0.0 slice-done
  35.2 0.1 slice-done.1
  35.3 2.3 %convolution_bitcast_fusion.2 = f32[1024,256]{0,1:T(8,128)S(1)} fusion(bf16[4096,256]{1,0:T(8,128)(2,1)S(1)} %bitcast.95, bf16[4096,1024]{1,0:T(8,128)(2,1)S(1)} %bitcast.84), kind=kOutput, calls=%fused_computation.39 | convolution fusion | flops 2147483648 | bytes 11534336 | tf_op jit(solution)/shard_map/dot_general | solution.py:176
  37.7 1.3 copy.24
  39.0 31.2 %shard_map.68 = bf16[16,64,256]{2,1,0:T(8,128)(2,1)} custom-call(f32[16,64,256]{2,1,0:T(8,128)} %bitcast.98), custom_call_target="tpu_custom_call" | custom-call | tf_op jit(solution)/shard_map/pallas_call | solution.py:121
  70.2 6.9 %multiply_reduce_fusion = (f32[256]{0:T(256)S(1)}, bf16[4096,256]{0,1:T(8,128)(2,1)S(1)}) fusion(bf16[1024,256]{1,0:T(8,128)(2,1)} %bitcast.99, bf16[4096,1024]{1,0:T(8,128)(2,1)} %param.6, bf16[4096,256]{0,1:T(8,128)(2,1)} %copy.19), kind=kOutput, calls=%fused_computation.11 | convolution fusion | flops 2153774848 | bytes 13108224 | tf_op jit(solution)/shard_map/dot_general | solution.py:180
  77.1 3.5 %collective-permute-start.2 = (bf16[512,256]{0,1:T(8,128)(2,1)S(1)}, bf16[512,256]{0,1:T(8,128)(2,1)S(1)}, u32[]{:S(2)}, u32[]{:S(2)}) collective-permute-start(bf16[512,256]{0,1:T(8,128)(2,1)S(1)} %get-tuple-element.6), channel_id=1, source_target_pairs={{0,8},{8,16},{16,24},{24,32},{32,40},{40,48},{48,56},{56,64},{64,7... | collective-permute-start | bytes 786440 | tf_op jit(solution)/shard_map/ppermute | solution.py:20
  80.6 2.1 %collective-permute-start.3 = (bf16[512,256]{0,1:T(8,128)(2,1)S(1)}, bf16[512,256]{0,1:T(8,128)(2,1)S(1)}, u32[]{:S(2)}, u32[]{:S(2)}) collective-permute-start(bf16[512,256]{0,1:T(8,128)(2,1)S(1)} %get-tuple-element.7), channel_id=1, source_target_pairs={{8,0},{16,8},{24,16},{32,24},{40,32},{48,40},{56,48},{64,56},{72,6... | collective-permute-start | bytes 786440 | tf_op jit(solution)/shard_map/ppermute | solution.py:23
  82.7 2.5 %copy.31 = bf16[4096,256]{1,0:T(8,128)(2,1)} copy(bf16[4096,256]{0,1:T(8,128)(2,1)S(1)} %get-tuple-element.15) | data formatting | bytes 4194304
  85.2 0.0 collective-permute-done.2
  85.2 3.1 %collective-permute-done.3 = bf16[512,256]{0,1:T(8,128)(2,1)S(1)} collective-permute-done((bf16[512,256]{0,1:T(8,128)(2,1)S(1)}, bf16[512,256]{0,1:T(8,128)(2,1)S(1)}, u32[]{:S(2)}, u32[]{:S(2)}) %collective-permute-start.3) | collective-permute-done | bytes 262176 | tf_op jit(solution)/shard_map/ppermute | solution.py:23
  88.3 1.7 %pad_maximum_fusion.1 = bf16[5120,256]{0,1:T(8,128)(2,1)} fusion(bf16[512,256]{0,1:T(8,128)(2,1)S(1)} %collective-permute-done.3, bf16[4096,256]{0,1:T(8,128)(2,1)S(1)} %get-tuple-element.15, bf16[512,256]{0,1:T(8,128)(2,1)S(1)} %collective-permute-done.2), kind=kLoop, calls=%fused_computation.15 | loop fusion | flops 7864320 | bytes 5242880 | tf_op jit(solution)/shard_map/concatenate | solution.py:24
  90.0 3.0 %copy.25 = bf16[5120,256]{1,0:T(8,128)(2,1)S(1)} copy(bf16[5120,256]{0,1:T(8,128)(2,1)} %pad_maximum_fusion.1) | data formatting | bytes 5242880 | tf_op jit(solution)/shard_map/concatenate | solution.py:24
  93.0 2.0 %gather_fusion.7 = bf16[16,256,256]{2,1,0:T(8,128)(2,1)} fusion(bf16[20,256,256]{2,1,0:T(8,128)(2,1)S(1)} %bitcast.87, s32[1024]{0:T(1024)S(1)} %get-tuple-element.16), kind=kCustom, calls=%fused_computation.7 | custom fusion | bytes 4194368 | tf_op jit(solution)/shard_map/gather | solution.py:35
  95.0 2.0 %gather_fusion.6 = bf16[16,256,256]{2,1,0:T(8,128)(2,1)} fusion(bf16[20,256,256]{2,1,0:T(8,128)(2,1)S(1)} %bitcast.88, s32[1024]{0:T(1024)S(1)} %get-tuple-element.17), kind=kCustom, calls=%fused_computation.6 | custom fusion | bytes 4194368 | tf_op jit(solution)/shard_map/gather | solution.py:35
  97.0 2.0 %gather_fusion.5 = bf16[16,256,256]{2,1,0:T(8,128)(2,1)} fusion(bf16[20,256,256]{2,1,0:T(8,128)(2,1)S(1)} %bitcast.89, s32[1024]{0:T(1024)S(1)} %get-tuple-element.18), kind=kCustom, calls=%fused_computation.5 | custom fusion | bytes 4194368 | tf_op jit(solution)/shard_map/gather | solution.py:35
  99.0 2.0 %gather_fusion.4 = bf16[16,256,256]{2,1,0:T(8,128)(2,1)} fusion(bf16[20,256,256]{2,1,0:T(8,128)(2,1)S(1)} %bitcast.90, s32[1024]{0:T(1024)S(1)} %get-tuple-element.19), kind=kCustom, calls=%fused_computation.4 | custom fusion | bytes 4194368 | tf_op jit(solution)/shard_map/gather | solution.py:35
  101.1 0.0 copy-start.4
  101.1 3.1 %fusion.7 = f32[16,256,256]{1,2,0:T(8,128)S(1)} fusion(bf16[16,256,256]{2,1,0:T(8,128)(2,1)} %gather_fusion.4, bf16[16,4,256,256]{3,2,1,0:T(8,128)(2,1)} %param.8), kind=kOutput, calls=%fused_computation.21 | convolution fusion | flops 536870912 | bytes 8388608 | tf_op jit(solution)/shard_map/bij,bjc->bic/dot_general | solution.py:36
  104.1 0.0 copy-done.4
  104.2 0.0 copy-start.2
  104.2 2.5 %fusion.5 = f32[16,256,256]{1,2,0:T(8,128)S(1)} fusion(bf16[16,256,256]{2,1,0:T(8,128)(2,1)S(1)} %copy-done.4, bf16[16,4,256,256]{3,2,1,0:T(8,128)(2,1)} %param.8), kind=kOutput, calls=%fused_computation.19 | convolution fusion | flops 536870912 | bytes 8388608 | tf_op jit(solution)/shard_map/bij,bjc->bic/dot_general | solution.py:36
  106.6 0.0 copy-done.2
  106.7 0.0 copy-start
  106.7 0.0 slice-start.2
  106.7 2.5 %fusion.3 = f32[16,256,256]{1,2,0:T(8,128)S(1)} fusion(bf16[16,256,256]{2,1,0:T(8,128)(2,1)S(1)} %copy-done.2, bf16[16,4,256,256]{3,2,1,0:T(8,128)(2,1)} %param.8), kind=kOutput, calls=%fused_computation.17 | convolution fusion | flops 536870912 | bytes 8388608 | tf_op jit(solution)/shard_map/bij,bjc->bic/dot_general | solution.py:36
  109.2 0.0 copy-done
  109.2 0.0 slice-start.3
  109.2 3.0 %add_convert_fusion = bf16[16,256,256]{1,2,0:T(8,128)(2,1)S(1)} fusion(f32[16,256,256]{1,2,0:T(8,128)S(1)} %fusion.3, f32[16,256,256]{1,2,0:T(8,128)S(1)} %fusion.7, f32[16,256,256]{1,2,0:T(8,128)S(1)} %fusion.5, bf16[16,256,256]{2,1,0:T(8,128)(2,1)S(1)} %copy-done, bf16[16,4,256,256]{3,2,1,0:T(8,128)(2,1)} %param.8), kind=kOutput, calls=%fused_computation.12 | convolution fusion | flops 541065216 | bytes 18874368 | tf_op jit(solution)/shard_map/bij,bjc->bic/dot_general | solution.py:36
  112.1 0.0 slice-done.2
  112.1 0.1 slice-done.3
  112.2 2.3 %convolution_bitcast_fusion.1 = f32[1024,256]{0,1:T(8,128)S(1)} fusion(bf16[4096,256]{1,0:T(8,128)(2,1)S(1)} %bitcast.96, bf16[4096,1024]{1,0:T(8,128)(2,1)S(1)} %bitcast.86), kind=kOutput, calls=%fused_computation.38 | convolution fusion | flops 2147483648 | bytes 11534336 | tf_op jit(solution)/shard_map/dot_general | solution.py:185
  114.6 0.3 copy.30
  114.9 1.2 pad_maximum_fusion.2.x_ref
  116.1 19.9 %shard_map.69 = bf16[64,256]{1,0:T(8,128)(2,1)} custom-call(f32[16,72,256]{2,1,0:T(8,128)} %pad_maximum_fusion.2.x_ref), custom_call_target="tpu_custom_call" | custom-call | tf_op jit(solution)/shard_map/pallas_call | solution.py:157
  136.0 1.4 %copy.41 = bf16[64,256]{1,0:T(8,128)(2,1)} copy(bf16[64,256]{1,0:T(8,128)(2,1)} %shard_map.69) | data formatting | bytes 65536
  (6 shorter events, 0.1 us)
Async XLA Ops:
  1.7 11.8 %collective-permute-start = (bf16[512,256]{1,0:T(8,128)(2,1)S(1)}, bf16[512,256]{1,0:T(8,128)(2,1)S(1)}, u32[]{:S(2)}, u32[]{:S(2)}) collective-permute-start(bf16[512,256]{1,0:T(8,128)(2,1)S(1)} %get-tuple-element.8), channel_id=1, source_target_pairs={{0,8},{8,16},{16,24},{24,32},{32,40},{40,48},{48,56},{56,64},{64,7... | collective-permute-start | bytes 786440 | tf_op jit(solution)/shard_map/ppermute | solution.py:20
  6.6 7.7 %collective-permute-start.1 = (bf16[512,256]{1,0:T(8,128)(2,1)S(1)}, bf16[512,256]{1,0:T(8,128)(2,1)S(1)}, u32[]{:S(2)}, u32[]{:S(2)}) collective-permute-start(bf16[512,256]{1,0:T(8,128)(2,1)S(1)} %get-tuple-element.9), channel_id=1, source_target_pairs={{8,0},{16,8},{24,16},{32,24},{40,32},{48,40},{56,48},{64,56},{72,6... | collective-permute-start | bytes 786440 | tf_op jit(solution)/shard_map/ppermute | solution.py:23
  24.2 3.1 %copy-start.5 = (bf16[16,256,256]{2,1,0:T(8,128)(2,1)S(1)}, bf16[16,256,256]{2,1,0:T(8,128)(2,1)}, u32[]{:S(2)}) copy-start(bf16[16,256,256]{2,1,0:T(8,128)(2,1)} %gather_fusion) | copy-start | bytes 6291460
  27.3 2.5 %copy-start.3 = (bf16[16,256,256]{2,1,0:T(8,128)(2,1)S(1)}, bf16[16,256,256]{2,1,0:T(8,128)(2,1)}, u32[]{:S(2)}) copy-start(bf16[16,256,256]{2,1,0:T(8,128)(2,1)} %gather_fusion.1) | copy-start | bytes 6291460
  29.7 2.5 %copy-start.1 = (bf16[16,256,256]{2,1,0:T(8,128)(2,1)S(1)}, bf16[16,256,256]{2,1,0:T(8,128)(2,1)}, u32[]{:S(2)}) copy-start(bf16[16,256,256]{2,1,0:T(8,128)(2,1)} %gather_fusion.3) | copy-start | bytes 6291460
  29.8 5.5 %slice-start = ((s8[8388608]{0:T(1024)(128)(4,1)}), s8[4194304]{0:T(1024)(128)(4,1)S(1)}, s32[]{:S(2)}) async-start(s8[8388608]{0:T(1024)(128)(4,1)} %bitcast.83), calls=%async_computation | async-start | bytes 8388608
  32.3 3.1 %slice-start.1 = ((s8[8388608]{0:T(1024)(128)(4,1)}), s8[4194304]{0:T(1024)(128)(4,1)S(1)}, s32[]{:S(2)}) async-start(s8[8388608]{0:T(1024)(128)(4,1)} %bitcast.83), calls=%async_computation.1 | async-start | bytes 8388608
  77.1 8.0 %collective-permute-start.2 = (bf16[512,256]{0,1:T(8,128)(2,1)S(1)}, bf16[512,256]{0,1:T(8,128)(2,1)S(1)}, u32[]{:S(2)}, u32[]{:S(2)}) collective-permute-start(bf16[512,256]{0,1:T(8,128)(2,1)S(1)} %get-tuple-element.6), channel_id=1, source_target_pairs={{0,8},{8,16},{16,24},{24,32},{32,40},{40,48},{48,56},{56,64},{64,7... | collective-permute-start | bytes 786440 | tf_op jit(solution)/shard_map/ppermute | solution.py:20
  80.6 7.7 %collective-permute-start.3 = (bf16[512,256]{0,1:T(8,128)(2,1)S(1)}, bf16[512,256]{0,1:T(8,128)(2,1)S(1)}, u32[]{:S(2)}, u32[]{:S(2)}) collective-permute-start(bf16[512,256]{0,1:T(8,128)(2,1)S(1)} %get-tuple-element.7), channel_id=1, source_target_pairs={{8,0},{16,8},{24,16},{32,24},{40,32},{48,40},{56,48},{64,56},{72,6... | collective-permute-start | bytes 786440 | tf_op jit(solution)/shard_map/ppermute | solution.py:23
  101.1 3.1 %copy-start.4 = (bf16[16,256,256]{2,1,0:T(8,128)(2,1)S(1)}, bf16[16,256,256]{2,1,0:T(8,128)(2,1)}, u32[]{:S(2)}) copy-start(bf16[16,256,256]{2,1,0:T(8,128)(2,1)} %gather_fusion.5) | copy-start | bytes 6291460
  104.2 2.5 %copy-start.2 = (bf16[16,256,256]{2,1,0:T(8,128)(2,1)S(1)}, bf16[16,256,256]{2,1,0:T(8,128)(2,1)}, u32[]{:S(2)}) copy-start(bf16[16,256,256]{2,1,0:T(8,128)(2,1)} %gather_fusion.6) | copy-start | bytes 6291460
  106.7 2.5 %copy-start = (bf16[16,256,256]{2,1,0:T(8,128)(2,1)S(1)}, bf16[16,256,256]{2,1,0:T(8,128)(2,1)}, u32[]{:S(2)}) copy-start(bf16[16,256,256]{2,1,0:T(8,128)(2,1)} %gather_fusion.7) | copy-start | bytes 6291460
  106.7 5.5 %slice-start.2 = ((s8[8388608]{0:T(1024)(128)(4,1)}), s8[4194304]{0:T(1024)(128)(4,1)S(1)}, s32[]{:S(2)}) async-start(s8[8388608]{0:T(1024)(128)(4,1)} %bitcast.85), calls=%async_computation.2 | async-start | bytes 8388608
  109.2 3.1 %slice-start.3 = ((s8[8388608]{0:T(1024)(128)(4,1)}), s8[4194304]{0:T(1024)(128)(4,1)S(1)}, s32[]{:S(2)}) async-start(s8[8388608]{0:T(1024)(128)(4,1)} %bitcast.85), calls=%async_computation.3 | async-start | bytes 8388608

commit v2 on v1

--- a/solution.py
+++ b/solution.py
@@ -25,18 +25,39 @@
     return block
 
 
+def band_kernel(off_ref, blk_ref, field_ref, out_ref):
+    b = pl.program_id(0)
+    acc = None
+    for k in range(KB):
+        start = pl.multiple_of((b + 2 + off_ref[b, k]) * BK, BK)
+        term = jnp.dot(
+            blk_ref[0, k], field_ref[pl.ds(start, BK), :], preferred_element_type=jnp.float32
+        )
+        acc = term if acc is None else acc + term
+    out_ref[...] = acc.astype(out_ref.dtype)
+
+
 def band_local(blocks, offsets, padded):
     nblk = blocks.shape[0]
-    width = padded.shape[1]
-    stacked = padded.reshape(nblk + 4, BK, width)
-    total = jnp.zeros((nblk, BK, width), jnp.float32)
-    for k in range(KB):
-        index = jnp.arange(nblk, dtype=jnp.int32) + 2 + offsets[:, k]
-        taken = stacked[index]
-        total = total + jnp.einsum(
-            "bij,bjc->bic", blocks[:, k], taken, preferred_element_type=jnp.float32
-        )
-    return total.reshape(nblk * BK, width)
+    rows, width = padded.shape
+    return pl.pallas_call(
+        band_kernel,
+        out_shape=jax.ShapeDtypeStruct((nblk * BK, width), jnp.bfloat16),
+        grid_spec=pltpu.PrefetchScalarGridSpec(
+            num_scalar_prefetch=1,
+            grid=(nblk,),
+            in_specs=[
+                pl.BlockSpec((1, KB, BK, BK), lambda b, off: (b, 0, 0, 0)),
+                pl.BlockSpec((rows, width), lambda b, off: (0, 0)),
+            ],
+            out_specs=pl.BlockSpec((BK, width), lambda b, off: (b, 0)),
+        ),
+        cost_estimate=pl.CostEstimate(
+            flops=2 * nblk * KB * BK * BK * width,
+            bytes_accessed=blocks.size * 2 + padded.size * 2 + nblk * BK * width * 2,
+            transcendentals=0,
+        ),
+    )(offsets, blocks, padded)
 
 
 def _barrier_all(n, me, orb):
@@ -172,7 +193,7 @@
     n = lax.axis_size("basis")
     count = band_offsets.shape[0] * BK * n
     cont_padded = padded_2(cont_orbitals, (("basis", 0),), 2 * BK)
-    margin_cont = band_local(margin_blocks, band_offsets, cont_padded).astype(jnp.bfloat16)
+    margin_cont = band_local(margin_blocks, band_offsets, cont_padded)
     partial_proj = lax.dot_general(
         target_orbitals, margin_cont, (((0,), (0,)), ((), ())), preferred_element_type=jnp.float32
     )
@@ -181,7 +202,7 @@
     cont_orth = (cont_orbitals.astype(jnp.float32) - removed).astype(jnp.bfloat16)
     squares = jnp.sum(jnp.square(cont_orth.astype(jnp.float32)), axis=0)
     orth_padded = padded_2(cont_orth, (("basis", 0),), 2 * BK)
-    dipole_cont = band_local(dipole_blocks, band_offsets, orth_padded).astype(jnp.bfloat16)
+    dipole_cont = band_local(dipole_blocks, band_offsets, orth_padded)
     partial_dip = lax.dot_general(
         target_orbitals,
         dipole_cont,

time: 139 us -> 135 us (0.971)
  Pallas kernels: 51.2 us -> 79.9 us
  local copies, waits for them, and re-layouts: 30 us -> 5.5 us
  matrix products: 33.5 us -> 18.6 us
  waiting for transfers between devices: 3.95 us -> 10.2 us
    pallas_call x0 -> x2, Pallas kernels: none -> 28.8 us  [band_local(): pl.pallas_call(band_kernel, out_shape=jax.ShapeDtypeStruct((nblk * BK, wi...]
    dot_general x8 -> x0, matrix products: 21.9 us -> none  [band_local(): jnp.einsum('bij,bjc->bic', blocks[:, k], taken, preferred_element_type=jn...]
    gather x8 -> x0, local copies, waits for them, and re-layouts: 16.1 us -> none  [band_local(): taken = stacked[index]]
    unnamed x23 -> x6, local copies, waits for them, and re-layouts: 8.12 us -> 2.75 us
    ppermute x2, waiting for transfers between devices: 3.94 us -> 8.79 us  [padded_2(): lax.ppermute(lax.slice_in_dim(block, 0, width, axis=dim), axis, backward)]
    dot_general x1, matrix products: 2.34 us -> 6.37 us  [on_device(): lax.dot_general(target_orbitals, margin_cont, (((0,), (0,)), ((), ())), p...]
    dot_general x1, matrix products: 2.34 us -> 6.37 us  [on_device(): lax.dot_general(target_orbitals, dipole_cont, (((0,), (0,)), ((), ())), p...]
    concatenate x1 -> x0, local copies, waits for them, and re-layouts: 2.96 us -> none  [padded_2(): block = jnp.concatenate([low, block, high], axis=dim)]
  transfers between devices with their start and end apart: 4 -> 4, of which waited for: 2 -> 3; matrix products, arithmetic and copies ran while one was open for 5% -> 1% of each run, Pallas kernels for 0% -> 0%
where the time goes in v2:
time: 135 us; the launch traced here: 133 us
  Pallas kernels  79.9 us (59%)
  matrix products  18.6 us (14%)
  starting transfers between devices  12.2 us (9%)
  waiting for transfers between devices  10.2 us (8%)
  other arithmetic  6.11 us (5%)
  local copies, waits for them, and re-layouts  5.5 us (4%)
    pallas_call x1, Pallas kernels, allreduce_to_bf16(): pl.pallas_call(functools.partial(allreduce_kernel, n), out_shape=jax.Shap...  31.2 us
    pallas_call x2, Pallas kernels, band_local(): pl.pallas_call(band_kernel, out_shape=jax.ShapeDtypeStruct((nblk * BK, wi...  28.8 us
    pallas_call x1, Pallas kernels, dipole_scatter(): pl.pallas_call(functools.partial(dipole_kernel, n, chunk, count), out_sha...  19.9 us
    ppermute x2, waiting for transfers between devices, padded_2(): lax.ppermute(lax.slice_in_dim(block, 0, width, axis=dim), axis, backward)  8.79 us
    ppermute x2, starting transfers between devices, padded_2(): lax.ppermute(lax.slice_in_dim(block, block.shape[dim] - width, None, axis...  8.4 us
    dot_general x1, matrix products, on_device(): lax.dot_general(target_orbitals, margin_cont, (((0,), (0,)), ((), ())), p...  6.37 us
    dot_general x1, matrix products, on_device(): lax.dot_general(target_orbitals, dipole_cont, (((0,), (0,)), ((), ())), p...  6.37 us
    dot_general x1, matrix products, on_device(): jnp.dot(target_orbitals, projection_b, preferred_element_type=jnp.float32)  5.89 us
  transfers between devices with their start and end apart: 4, of which 3 were waited for; matrix products, arithmetic and copies ran while one was open for 1% of the time, Pallas kernels for 0%

profile of v2, /device:TPU:1, one launch (start us, length us, event | category | flops | bytes accessed | tf_op | source)
XLA Modules:
  0.0 133.3 jit_solution(10666628738505642809)
XLA Ops:
  0.6 1.1 fusion.3
  1.7 4.9 %collective-permute-start = (bf16[512,256]{1,0:T(8,128)(2,1)S(1)}, bf16[512,256]{1,0:T(8,128)(2,1)S(1)}, u32[]{:S(2)}, u32[]{:S(2)}) collective-permute-start(bf16[512,256]{1,0:T(8,128)(2,1)S(1)} %get-tuple-element.4), channel_id=1, source_target_pairs={{0,8},{8,16},{16,24},{24,32},{32,40},{40,48},{48,56},{56,64},{64,7... | collective-permute-start | bytes 786440 | tf_op jit(solution)/shard_map/ppermute | solution.py:20
  6.6 1.9 %collective-permute-start.1 = (bf16[512,256]{1,0:T(8,128)(2,1)S(1)}, bf16[512,256]{1,0:T(8,128)(2,1)S(1)}, u32[]{:S(2)}, u32[]{:S(2)}) collective-permute-start(bf16[512,256]{1,0:T(8,128)(2,1)S(1)} %get-tuple-element.5), channel_id=1, source_target_pairs={{8,0},{16,8},{24,16},{32,24},{40,32},{48,40},{56,48},{64,56},{72,6... | collective-permute-start | bytes 786440 | tf_op jit(solution)/shard_map/ppermute | solution.py:23
  8.6 1.4 %copy.7.off_ref = s32[16,4]{1,0:T(8,128)} copy(s32[16,4]{0,1:T(4,128)} %param.9) | data formatting | bytes 512 | tf_op args[4]
  9.9 0.0 collective-permute-done
  9.9 4.4 %collective-permute-done.1 = bf16[512,256]{1,0:T(8,128)(2,1)S(1)} collective-permute-done((bf16[512,256]{1,0:T(8,128)(2,1)S(1)}, bf16[512,256]{1,0:T(8,128)(2,1)S(1)}, u32[]{:S(2)}, u32[]{:S(2)}) %collective-permute-start.1) | collective-permute-done | bytes 262176 | tf_op jit(solution)/shard_map/ppermute | solution.py:23
  14.3 3.3 %pad_maximum_fusion.field_ref = bf16[5120,256]{1,0:T(8,128)(2,1)} fusion(bf16[512,256]{1,0:T(8,128)(2,1)S(1)} %collective-permute-done.1, bf16[4096,256]{1,0:T(8,128)(2,1)} %param.5, bf16[512,256]{1,0:T(8,128)(2,1)S(1)} %collective-permute-done), kind=kLoop, calls=%fused_computation.4 | loop fusion | flops 7864320 | bytes 5242880 | tf_op jit(solution)/shard_map/concatenate | solution.py:24
  17.6 14.4 %shard_map.68 = bf16[4096,256]{1,0:T(8,128)(2,1)} custom-call(s32[16,4]{1,0:T(8,128)} %copy.7.off_ref, bf16[16,4,256,256]{3,2,1,0:T(8,128)(2,1)} %blk_ref.2, bf16[5120,256]{1,0:T(8,128)(2,1)} %pad_maximum_fusion.field_ref), custom_call_target="tpu_custom_call" | custom-call | flops 2147483648 | bytes 13107200 | tf_op jit(solution)/shard_map/pallas_call | solution.py:43
  32.0 6.4 %convolution_bitcast_fusion.2 = f32[1024,256]{0,1:T(8,128)S(1)} fusion(bf16[4096,256]{1,0:T(8,128)(2,1)} %shard_map.68, bf16[4096,1024]{1,0:T(8,128)(2,1)} %param.6), kind=kOutput, calls=%fused_computation.7 | convolution fusion | flops 2147483648 | bytes 11534336 | tf_op jit(solution)/shard_map/dot_general | solution.py:197
  38.4 0.0 copy-start
  38.4 1.3 copy.8
  39.7 31.2 %shard_map.69 = bf16[16,64,256]{2,1,0:T(8,128)(2,1)} custom-call(f32[16,64,256]{2,1,0:T(8,128)} %bitcast.20), custom_call_target="tpu_custom_call" | custom-call | tf_op jit(solution)/shard_map/pallas_call | solution.py:142
  71.0 0.0 copy-done
  71.0 5.9 %multiply_reduce_fusion = (f32[256]{0:T(256)S(1)}, bf16[4096,256]{1,0:T(8,128)(2,1)S(1)}) fusion(bf16[4096,1024]{1,0:T(8,128)(2,1)} %param.6, bf16[1024,256]{1,0:T(8,128)(2,1)} %bitcast.21, bf16[4096,256]{1,0:T(8,128)(2,1)S(1)} %copy-done), kind=kOutput, calls=%fused_computation.3 | convolution fusion | flops 2153774848 | bytes 13108224 | tf_op jit(solution)/shard_map/dot_general | solution.py:201
  76.9 0.0 copy-start.1
  76.9 3.5 %collective-permute-start.2 = (bf16[512,256]{1,0:T(8,128)(2,1)S(1)}, bf16[512,256]{1,0:T(8,128)(2,1)S(1)}, u32[]{:S(2)}, u32[]{:S(2)}) collective-permute-start(bf16[512,256]{1,0:T(8,128)(2,1)S(1)} %get-tuple-element.2), channel_id=1, source_target_pairs={{0,8},{8,16},{16,24},{24,32},{32,40},{40,48},{48,56},{56,64},{64,7... | collective-permute-start | bytes 786440 | tf_op jit(solution)/shard_map/ppermute | solution.py:20
  80.4 1.9 %collective-permute-start.3 = (bf16[512,256]{1,0:T(8,128)(2,1)S(1)}, bf16[512,256]{1,0:T(8,128)(2,1)S(1)}, u32[]{:S(2)}, u32[]{:S(2)}) collective-permute-start(bf16[512,256]{1,0:T(8,128)(2,1)S(1)} %get-tuple-element.3), channel_id=1, source_target_pairs={{8,0},{16,8},{24,16},{32,24},{40,32},{48,40},{56,48},{64,56},{72,6... | collective-permute-start | bytes 786440 | tf_op jit(solution)/shard_map/ppermute | solution.py:23
  82.3 1.4 %collective-permute-done.2 = bf16[512,256]{1,0:T(8,128)(2,1)S(1)} collective-permute-done((bf16[512,256]{1,0:T(8,128)(2,1)S(1)}, bf16[512,256]{1,0:T(8,128)(2,1)S(1)}, u32[]{:S(2)}, u32[]{:S(2)}) %collective-permute-start.2) | collective-permute-done | bytes 262176 | tf_op jit(solution)/shard_map/ppermute | solution.py:20
  83.7 4.4 %collective-permute-done.3 = bf16[512,256]{1,0:T(8,128)(2,1)S(1)} collective-permute-done((bf16[512,256]{1,0:T(8,128)(2,1)S(1)}, bf16[512,256]{1,0:T(8,128)(2,1)S(1)}, u32[]{:S(2)}, u32[]{:S(2)}) %collective-permute-start.3) | collective-permute-done | bytes 262176 | tf_op jit(solution)/shard_map/ppermute | solution.py:23
  88.1 0.0 copy-done.1
  88.1 1.7 %pad_maximum_fusion.1.field_ref = bf16[5120,256]{1,0:T(8,128)(2,1)} fusion(bf16[512,256]{1,0:T(8,128)(2,1)S(1)} %collective-permute-done.3, bf16[4096,256]{1,0:T(8,128)(2,1)S(1)} %get-tuple-element.10, bf16[512,256]{1,0:T(8,128)(2,1)S(1)} %collective-permute-done.2), kind=kLoop, calls=%fused_computation.5 | loop fusion | flops 7864320 | bytes 5242880 | tf_op jit(solution)/shard_map/concatenate | solution.py:24
  89.8 14.4 %shard_map.70 = bf16[4096,256]{1,0:T(8,128)(2,1)} custom-call(s32[16,4]{1,0:T(8,128)} %copy.7.off_ref, bf16[16,4,256,256]{3,2,1,0:T(8,128)(2,1)} %blk_ref.3, bf16[5120,256]{1,0:T(8,128)(2,1)} %pad_maximum_fusion.1.field_ref), custom_call_target="tpu_custom_call" | custom-call | flops 2147483648 | bytes 13107200 | tf_op jit(solution)/shard_map/pallas_call | solution.py:43
  104.2 6.4 %convolution_bitcast_fusion.1 = f32[1024,256]{0,1:T(8,128)S(1)} fusion(bf16[4096,256]{1,0:T(8,128)(2,1)} %shard_map.70, bf16[4096,1024]{1,0:T(8,128)(2,1)} %param.6), kind=kOutput, calls=%fused_computation.6 | convolution fusion | flops 2147483648 | bytes 11534336 | tf_op jit(solution)/shard_map/dot_general | solution.py:206
  110.5 0.3 copy.11
  110.9 1.1 pad_maximum_fusion.2.x_ref
  112.0 19.9 %shard_map.71 = bf16[64,256]{1,0:T(8,128)(2,1)} custom-call(f32[16,72,256]{2,1,0:T(8,128)} %pad_maximum_fusion.2.x_ref), custom_call_target="tpu_custom_call" | custom-call | tf_op jit(solution)/shard_map/pallas_call | solution.py:178
  132.0 1.4 %copy.14 = bf16[64,256]{1,0:T(8,128)(2,1)} copy(bf16[64,256]{1,0:T(8,128)(2,1)} %shard_map.71) | data formatting | bytes 65536
  (2 shorter events, 0.0 us)
Async XLA Ops:
  1.7 8.2 %collective-permute-start = (bf16[512,256]{1,0:T(8,128)(2,1)S(1)}, bf16[512,256]{1,0:T(8,128)(2,1)S(1)}, u32[]{:S(2)}, u32[]{:S(2)}) collective-permute-start(bf16[512,256]{1,0:T(8,128)(2,1)S(1)} %get-tuple-element.4), channel_id=1, source_target_pairs={{0,8},{8,16},{16,24},{24,32},{32,40},{40,48},{48,56},{56,64},{64,7... | collective-permute-start | bytes 786440 | tf_op jit(solution)/shard_map/ppermute | solution.py:20
  6.6 7.7 %collective-permute-start.1 = (bf16[512,256]{1,0:T(8,128)(2,1)S(1)}, bf16[512,256]{1,0:T(8,128)(2,1)S(1)}, u32[]{:S(2)}, u32[]{:S(2)}) collective-permute-start(bf16[512,256]{1,0:T(8,128)(2,1)S(1)} %get-tuple-element.5), channel_id=1, source_target_pairs={{8,0},{16,8},{24,16},{32,24},{40,32},{48,40},{56,48},{64,56},{72,6... | collective-permute-start | bytes 786440 | tf_op jit(solution)/shard_map/ppermute | solution.py:23
  38.4 32.6 %copy-start = (bf16[4096,256]{1,0:T(8,128)(2,1)S(1)}, bf16[4096,256]{1,0:T(8,128)(2,1)}, u32[]{:S(2)}) copy-start(bf16[4096,256]{1,0:T(8,128)(2,1)} %param.5) | copy-start | bytes 6291460
  76.9 11.2 %copy-start.1 = (bf16[4096,256]{1,0:T(8,128)(2,1)}, bf16[4096,256]{1,0:T(8,128)(2,1)S(1)}, u32[]{:S(2)}) copy-start(bf16[4096,256]{1,0:T(8,128)(2,1)S(1)} %get-tuple-element.10) | copy-start | bytes 6291460
  76.9 6.8 %collective-permute-start.2 = (bf16[512,256]{1,0:T(8,128)(2,1)S(1)}, bf16[512,256]{1,0:T(8,128)(2,1)S(1)}, u32[]{:S(2)}, u32[]{:S(2)}) collective-permute-start(bf16[512,256]{1,0:T(8,128)(2,1)S(1)} %get-tuple-element.2), channel_id=1, source_target_pairs={{0,8},{8,16},{16,24},{24,32},{32,40},{40,48},{48,56},{56,64},{64,7... | collective-permute-start | bytes 786440 | tf_op jit(solution)/shard_map/ppermute | solution.py:20
  80.4 7.7 %collective-permute-start.3 = (bf16[512,256]{1,0:T(8,128)(2,1)S(1)}, bf16[512,256]{1,0:T(8,128)(2,1)S(1)}, u32[]{:S(2)}, u32[]{:S(2)}) collective-permute-start(bf16[512,256]{1,0:T(8,128)(2,1)S(1)} %get-tuple-element.3), channel_id=1, source_target_pairs={{8,0},{16,8},{24,16},{32,24},{40,32},{48,40},{56,48},{64,56},{72,6... | collective-permute-start | bytes 786440 | tf_op jit(solution)/shard_map/ppermute | solution.py:23

commit v3 on v2

v3 whole, which is shorter than its diff:
```python
import functools

import jax
import jax.numpy as jnp
from jax import lax
from jax.experimental import pallas as pl
from jax.experimental.pallas import tpu as pltpu
from jax.sharding import PartitionSpec as P

BK = 256
KB = 4
MESH = pl.DeviceIdType.MESH


def padded_2(block, sides, width):
    for axis, dim in sides:
        count = lax.axis_size(axis)
        forward = [(i, i + 1) for i in range(count - 1)]
        backward = [(target, source) for source, target in forward]
        low = lax.ppermute(
            lax.slice_in_dim(block, block.shape[dim] - width, None, axis=dim), axis, forward
        )
        high = lax.ppermute(lax.slice_in_dim(block, 0, width, axis=dim), axis, backward)
        block = jnp.concatenate([low, block, high], axis=dim)
    return block


def band_kernel(off_ref, blk_ref, field_ref, out_ref):
    b = pl.program_id(0)
    acc = None
    for k in range(KB):
        start = pl.multiple_of((b + 2 + off_ref[b, k]) * BK, BK)
        term = jnp.dot(
            blk_ref[0, k], field_ref[pl.ds(start, BK), :], preferred_element_type=jnp.float32
        )
        acc = term if acc is None else acc + term
    out_ref[...] = acc.astype(out_ref.dtype)


def band_local(blocks, offsets, padded):
    nblk = blocks.shape[0]
    rows, width = padded.shape
    return pl.pallas_call(
        band_kernel,
        out_shape=jax.ShapeDtypeStruct((nblk * BK, width), jnp.bfloat16),
        grid_spec=pltpu.PrefetchScalarGridSpec(
            num_scalar_prefetch=1,
            grid=(nblk,),
            in_specs=[
                pl.BlockSpec((1, KB, BK, BK), lambda b, off: (b, 0, 0, 0)),
                pl.BlockSpec((rows, width), lambda b, off: (0, 0)),
            ],
            out_specs=pl.BlockSpec((BK, width), lambda b, off: (b, 0)),
        ),
        cost_estimate=pl.CostEstimate(
            flops=2 * nblk * KB * BK * BK * width,
            bytes_accessed=blocks.size * 2 + padded.size * 2 + nblk * BK * width * 2,
            transcendentals=0,
        ),
    )(offsets, blocks, padded)


def _place():
    me = lax.axis_index("basis")
    orb = lax.axis_index("orb")
    core = lax.rem(me, 2)
    partner = me + 1 - 2 * core
    chip = lax.div(me, 2)
    return orb, core, partner, chip


def _barrier_group(nchip, orb, core, partner, chip):
    barrier = pltpu.get_barrier_semaphore()
    pl.semaphore_signal(barrier, inc=1, device_id=(partner, orb), device_id_type=MESH)
    for j in range(1, nchip):
        peer = 2 * lax.rem(chip + j, nchip) + core
        pl.semaphore_signal(barrier, inc=1, device_id=(peer, orb), device_id_type=MESH)
    pl.semaphore_wait(barrier, nchip)


def _remote(src, dst, ssem, rsem, device, orb):
    return pltpu.make_async_remote_copy(
        src_ref=src, dst_ref=dst, send_sem=ssem, recv_sem=rsem,
        device_id=(device, orb), device_id_type=MESH,
    )


def _two_level_sum(nchip, x_ref, pair_recv, part, chip_recv, p_send, p_recv, c_send, c_recv):
    orb, core, partner, chip = _place()
    _barrier_group(nchip, orb, core, partner, chip)
    pair = []
    for i in range(nchip):
        cp = _remote(x_ref.at[i, 1 - core], pair_recv.at[i], p_send.at[i], p_recv.at[i], partner, orb)
        cp.start()
        pair.append(cp)
    for i in range(nchip):
        pair[i].wait_recv()
        part[i] = x_ref[i, core] + pair_recv[i]
    sends = []
    for j in range(1, nchip):
        dst = lax.rem(chip + j, nchip)
        cp = _remote(part.at[dst], chip_recv.at[chip], c_send.at[j], c_recv.at[chip], 2 * dst + core, orb)
        cp.start()
        sends.append(cp)
    total = part[chip]
    for j in range(1, nchip):
        src = lax.rem(chip + nchip - j, nchip)
        _remote(part.at[src], chip_recv.at[src], c_send.at[j], c_recv.at[src], 2 * src + core, orb).wait_recv()
        total = total + chip_recv[src]
    for cp in pair + sends:
        cp.wait_send()
    return total


def allreduce_kernel(nchip, x_ref, out_ref, pair_recv, part, chip_recv, sendbuf, half, other,
                     p_send, p_recv, c_send, c_recv, g_send, g_recv, h_send, h_recv):
    total = _two_level_sum(nchip, x_ref, pair_recv, part, chip_recv, p_send, p_recv, c_send, c_recv)
    orb, core, partner, chip = _place()
    rounded = total.astype(sendbuf.dtype)
    sendbuf[...] = rounded
    half[chip] = rounded
    sends = []
    for j in range(1, nchip):
        dst = lax.rem(chip + j, nchip)
        cp = _remote(sendbuf, half.at[chip], g_send.at[j], g_recv.at[chip], 2 * dst + core, orb)
        cp.start()
        sends.append(cp)
    for j in range(1, nchip):
        src = lax.rem(chip + nchip - j, nchip)
        _remote(sendbuf, half.at[src], g_send.at[j], g_recv.at[src], 2 * src + core, orb).wait_recv()
    for cp in sends:
        cp.wait_send()
    cp = _remote(half, other, h_send.at[0], h_recv.at[0], partner, orb)
    cp.start()
    cp.wait_recv()
    for i in range(nchip):
        out_ref[i, core] = half[i]
        out_ref[i, 1 - core] = other[i]
    cp.wait_send()


def _two_level_scratch(nchip, rows, cols):
    return [
        pltpu.VMEM((nchip, rows, cols), jnp.float32),
        pltpu.VMEM((nchip, rows, cols), jnp.float32),
        pltpu.VMEM((nchip, rows, cols), jnp.float32),
    ]


def allreduce_to_bf16(partial, n):
    rows, cols = partial.shape
    nchip = n // 2
    chunk = rows // n
    x = partial.reshape(nchip, 2, chunk, cols)
    out = pl.pallas_call(
        functools.partial(allreduce_kernel, nchip),
        out_shape=jax.ShapeDtypeStruct((nchip, 2, chunk, cols), jnp.bfloat16),
        in_specs=[pl.BlockSpec(memory_space=pltpu.VMEM)],
        out_specs=pl.BlockSpec(memory_space=pltpu.VMEM),
        scratch_shapes=_two_level_scratch(nchip, chunk, cols) + [
            pltpu.VMEM((chunk, cols), jnp.bfloat16),
            pltpu.VMEM((nchip, chunk, cols), jnp.bfloat16),
            pltpu.VMEM((nchip, chunk, cols), jnp.bfloat16),
        ] + [pltpu.SemaphoreType.DMA((nchip,))] * 6 + [pltpu.SemaphoreType.DMA((1,))] * 2,
        compiler_params=pltpu.CompilerParams(collective_id=0, has_side_effects=True),
    )(x)
    return out.reshape(rows, cols)


def dipole_kernel(nchip, chunk, count, x_ref, out_ref, pair_recv, part, chip_recv,
                  p_send, p_recv, c_send, c_recv):
    total = _two_level_sum(nchip, x_ref, pair_recv, part, chip_recv, p_send, p_recv, c_send, c_recv)
    squares = total[chunk:chunk + 1, :]
    col_norm = 1.0 / jnp.sqrt(squares / count + 1e-06)
    out_ref[...] = (total[:chunk, :] * col_norm).astype(out_ref.dtype)


def dipole_scatter(partial, squares, n, count):
    rows, cols = partial.shape
    nchip = n // 2
    chunk = rows // n
    x = jnp.concatenate(
        [
            partial.reshape(nchip, 2, chunk, cols),
            jnp.broadcast_to(squares[None, None, None, :], (nchip, 2, 8, cols)),
        ],
        axis=2,
    )
    return pl.pallas_call(
        functools.partial(dipole_kernel, nchip, chunk, count),
        out_shape=jax.ShapeDtypeStruct((chunk, cols), jnp.bfloat16),
        in_specs=[pl.BlockSpec(memory_space=pltpu.VMEM)],
        out_specs=pl.BlockSpec(memory_space=pltpu.VMEM),
        scratch_shapes=_two_level_scratch(nchip, chunk + 8, cols)
        + [pltpu.SemaphoreType.DMA((nchip,))] * 4,
        compiler_params=pltpu.CompilerParams(collective_id=1, has_side_effects=True),
    )(x)


def on_device(cont_orbitals, target_orbitals, margin_blocks, dipole_blocks, band_offsets):
    n = lax.axis_size("basis")
    count = band_offsets.shape[0] * BK * n
    cont_padded = padded_2(cont_orbitals, (("basis", 0),), 2 * BK)
    margin_cont = band_local(margin_blocks, band_offsets, cont_padded)
    partial_proj = lax.dot_general(
        target_orbitals, margin_cont, (((0,), (0,)), ((), ())), preferred_element_type=jnp.float32
    )
    projection_b = allreduce_to_bf16(partial_proj, n)
    removed = jnp.dot(target_orbitals, projection_b, preferred_element_type=jnp.float32)
    cont_orth = (cont_orbitals.astype(jnp.float32) - removed).astype(jnp.bfloat16)
    squares = jnp.sum(jnp.square(cont_orth.astype(jnp.float32)), axis=0)
    orth_padded = padded_2(cont_orth, (("basis", 0),), 2 * BK)
    dipole_cont = band_local(dipole_blocks, band_offsets, orth_padded)
    partial_dip = lax.dot_general(
        target_orbitals,
        dipole_cont,
        (((0,), (0,)), ((), ())),
        preferred_element_type=jnp.float32,
    )
    dipole_mo = dipole_scatter(partial_dip, squares, n, count)
    return (cont_orth, dipole_mo)


def solution(mesh):
    return jax.shard_map(
        on_device,
        mesh=mesh,
        in_specs=(
            P("basis", "orb"),
            P("basis", None),
            P("basis", None, None, None),
            P("basis", None, None, None),
            P("basis", None),
        ),
        out_specs=(P("basis", "orb"), P("basis", "orb")),
        check_vma=False,
    )
```

time: 135 us -> 118 us (0.87)
  Pallas kernels: 79.9 us -> 63.2 us
    pallas_call x2, Pallas kernels: 51.1 us -> 34.4 us  [the longest x1 21.7 us: allreduce_to_bf16(): pl.pallas_call(functools.partial(allreduce_kernel, nchip), out_shape=jax....]
where the time goes in v3:
time: 118 us; the launch traced here: 116 us
  Pallas kernels  63.2 us (54%)
  matrix products  18.6 us (16%)
  starting transfers between devices  11.3 us (10%)
  waiting for transfers between devices  10.2 us (9%)
  other arithmetic  6.11 us (5%)
  local copies, waits for them, and re-layouts  5.5 us (5%)
    pallas_call x2, Pallas kernels, band_local(): pl.pallas_call(band_kernel, out_shape=jax.ShapeDtypeStruct((nblk * BK, wi...  28.8 us
    pallas_call x1, Pallas kernels, allreduce_to_bf16(): pl.pallas_call(functools.partial(allreduce_kernel, nchip), out_shape=jax....  21.7 us
    pallas_call x1, Pallas kernels, dipole_scatter(): pl.pallas_call(functools.partial(dipole_kernel, nchip, chunk, count), out...  12.6 us
    ppermute x2, waiting for transfers between devices, padded_2(): lax.ppermute(lax.slice_in_dim(block, 0, width, axis=dim), axis, backward)  8.79 us
    ppermute x2, starting transfers between devices, padded_2(): lax.ppermute(lax.slice_in_dim(block, block.shape[dim] - width, None, axis...  7.46 us
    dot_general x1, matrix products, on_device(): lax.dot_general(target_orbitals, dipole_cont, (((0,), (0,)), ((), ())), p...  6.37 us
    dot_general x1, matrix products, on_device(): lax.dot_general(target_orbitals, margin_cont, (((0,), (0,)), ((), ())), p...  6.37 us
    dot_general x1, matrix products, on_device(): jnp.dot(target_orbitals, projection_b, preferred_element_type=jnp.float32)  5.88 us
  transfers between devices with their start and end apart: 4, of which 3 were waited for; matrix products, arithmetic and copies ran while one was open for 1% of the time, Pallas kernels for 0%

profile of v3, /device:TPU:1, one launch (start us, length us, event | category | flops | bytes accessed | tf_op | source)
XLA Modules:
  0.0 115.6 jit_solution(17124751452435889695)
XLA Ops:
  0.6 1.1 fusion.3
  1.7 4.9 %collective-permute-start = (bf16[512,256]{1,0:T(8,128)(2,1)S(1)}, bf16[512,256]{1,0:T(8,128)(2,1)S(1)}, u32[]{:S(2)}, u32[]{:S(2)}) collective-permute-start(bf16[512,256]{1,0:T(8,128)(2,1)S(1)} %get-tuple-element.4), channel_id=1, source_target_pairs={{0,8},{8,16},{16,24},{24,32},{32,40},{40,48},{48,56},{56,64},{64,7... | collective-permute-start | bytes 786440 | tf_op jit(solution)/shard_map/ppermute | solution.py:20
  6.6 1.9 %collective-permute-start.1 = (bf16[512,256]{1,0:T(8,128)(2,1)S(1)}, bf16[512,256]{1,0:T(8,128)(2,1)S(1)}, u32[]{:S(2)}, u32[]{:S(2)}) collective-permute-start(bf16[512,256]{1,0:T(8,128)(2,1)S(1)} %get-tuple-element.5), channel_id=1, source_target_pairs={{8,0},{16,8},{24,16},{32,24},{40,32},{48,40},{56,48},{64,56},{72,6... | collective-permute-start | bytes 786440 | tf_op jit(solution)/shard_map/ppermute | solution.py:23
  8.6 1.4 %copy.7.off_ref = s32[16,4]{1,0:T(8,128)} copy(s32[16,4]{0,1:T(4,128)} %param.9) | data formatting | bytes 512 | tf_op args[4]
  9.9 0.0 collective-permute-done
  9.9 4.4 %collective-permute-done.1 = bf16[512,256]{1,0:T(8,128)(2,1)S(1)} collective-permute-done((bf16[512,256]{1,0:T(8,128)(2,1)S(1)}, bf16[512,256]{1,0:T(8,128)(2,1)S(1)}, u32[]{:S(2)}, u32[]{:S(2)}) %collective-permute-start.1) | collective-permute-done | bytes 262176 | tf_op jit(solution)/shard_map/ppermute | solution.py:23
  14.3 3.3 %pad_maximum_fusion.field_ref = bf16[5120,256]{1,0:T(8,128)(2,1)} fusion(bf16[512,256]{1,0:T(8,128)(2,1)S(1)} %collective-permute-done.1, bf16[4096,256]{1,0:T(8,128)(2,1)} %param.5, bf16[512,256]{1,0:T(8,128)(2,1)S(1)} %collective-permute-done), kind=kLoop, calls=%fused_computation.4 | loop fusion | flops 7864320 | bytes 5242880 | tf_op jit(solution)/shard_map/concatenate | solution.py:24
  17.6 14.4 %shard_map.68 = bf16[4096,256]{1,0:T(8,128)(2,1)} custom-call(s32[16,4]{1,0:T(8,128)} %copy.7.off_ref, bf16[16,4,256,256]{3,2,1,0:T(8,128)(2,1)} %blk_ref.2, bf16[5120,256]{1,0:T(8,128)(2,1)} %pad_maximum_fusion.field_ref), custom_call_target="tpu_custom_call" | custom-call | flops 2147483648 | bytes 13107200 | tf_op jit(solution)/shard_map/pallas_call | solution.py:43
  32.0 6.4 %convolution_bitcast_fusion.2 = f32[1024,256]{0,1:T(8,128)S(1)} fusion(bf16[4096,256]{1,0:T(8,128)(2,1)} %shard_map.68, bf16[4096,1024]{1,0:T(8,128)(2,1)} %param.6), kind=kOutput, calls=%fused_computation.7 | convolution fusion | flops 2147483648 | bytes 11534336 | tf_op jit(solution)/shard_map/dot_general | solution.py:205
  38.4 0.0 copy-start
  38.4 1.3 %copy.8 = f32[1024,256]{1,0:T(8,128)} copy(f32[1024,256]{0,1:T(8,128)S(1)} %convolution_bitcast_fusion.2) | data formatting | bytes 2097152 | tf_op jit(solution)/shard_map/dot_general | solution.py:205
  39.7 21.7 %shard_map.69 = bf16[8,2,64,256]{3,2,1,0:T(8,128)(2,1)} custom-call(f32[8,2,64,256]{3,2,1,0:T(8,128)} %bitcast.20), custom_call_target="tpu_custom_call" | custom-call | tf_op jit(solution)/shard_map/pallas_call | solution.py:155
  61.5 0.0 copy-done
  61.5 5.9 %multiply_reduce_fusion = (f32[256]{0:T(256)S(1)}, bf16[4096,256]{1,0:T(8,128)(2,1)S(1)}) fusion(bf16[4096,1024]{1,0:T(8,128)(2,1)} %param.6, bf16[1024,256]{1,0:T(8,128)(2,1)} %bitcast.21, bf16[4096,256]{1,0:T(8,128)(2,1)S(1)} %copy-done), kind=kOutput, calls=%fused_computation.3 | convolution fusion | flops 2153774848 | bytes 13108224 | tf_op jit(solution)/shard_map/dot_general | solution.py:209
  67.4 0.0 copy-start.1
  67.4 2.5 %collective-permute-start.2 = (bf16[512,256]{1,0:T(8,128)(2,1)S(1)}, bf16[512,256]{1,0:T(8,128)(2,1)S(1)}, u32[]{:S(2)}, u32[]{:S(2)}) collective-permute-start(bf16[512,256]{1,0:T(8,128)(2,1)S(1)} %get-tuple-element.2), channel_id=1, source_target_pairs={{0,8},{8,16},{16,24},{24,32},{32,40},{40,48},{48,56},{56,64},{64,7... | collective-permute-start | bytes 786440 | tf_op jit(solution)/shard_map/ppermute | solution.py:20
  70.0 1.9 %collective-permute-start.3 = (bf16[512,256]{1,0:T(8,128)(2,1)S(1)}, bf16[512,256]{1,0:T(8,128)(2,1)S(1)}, u32[]{:S(2)}, u32[]{:S(2)}) collective-permute-start(bf16[512,256]{1,0:T(8,128)(2,1)S(1)} %get-tuple-element.3), channel_id=1, source_target_pairs={{8,0},{16,8},{24,16},{32,24},{40,32},{48,40},{56,48},{64,56},{72,6... | collective-permute-start | bytes 786440 | tf_op jit(solution)/shard_map/ppermute | solution.py:23
  71.9 1.4 %collective-permute-done.2 = bf16[512,256]{1,0:T(8,128)(2,1)S(1)} collective-permute-done((bf16[512,256]{1,0:T(8,128)(2,1)S(1)}, bf16[512,256]{1,0:T(8,128)(2,1)S(1)}, u32[]{:S(2)}, u32[]{:S(2)}) %collective-permute-start.2) | collective-permute-done | bytes 262176 | tf_op jit(solution)/shard_map/ppermute | solution.py:20
  73.2 4.4 %collective-permute-done.3 = bf16[512,256]{1,0:T(8,128)(2,1)S(1)} collective-permute-done((bf16[512,256]{1,0:T(8,128)(2,1)S(1)}, bf16[512,256]{1,0:T(8,128)(2,1)S(1)}, u32[]{:S(2)}, u32[]{:S(2)}) %collective-permute-start.3) | collective-permute-done | bytes 262176 | tf_op jit(solution)/shard_map/ppermute | solution.py:23
  77.6 0.0 copy-done.1
  77.6 1.7 %pad_maximum_fusion.1.field_ref = bf16[5120,256]{1,0:T(8,128)(2,1)} fusion(bf16[512,256]{1,0:T(8,128)(2,1)S(1)} %collective-permute-done.3, bf16[4096,256]{1,0:T(8,128)(2,1)S(1)} %get-tuple-element.10, bf16[512,256]{1,0:T(8,128)(2,1)S(1)} %collective-permute-done.2), kind=kLoop, calls=%fused_computation.5 | loop fusion | flops 7864320 | bytes 5242880 | tf_op jit(solution)/shard_map/concatenate | solution.py:24
  79.3 14.4 %shard_map.70 = bf16[4096,256]{1,0:T(8,128)(2,1)} custom-call(s32[16,4]{1,0:T(8,128)} %copy.7.off_ref, bf16[16,4,256,256]{3,2,1,0:T(8,128)(2,1)} %blk_ref.3, bf16[5120,256]{1,0:T(8,128)(2,1)} %pad_maximum_fusion.1.field_ref), custom_call_target="tpu_custom_call" | custom-call | flops 2147483648 | bytes 13107200 | tf_op jit(solution)/shard_map/pallas_call | solution.py:43
  93.7 6.4 %convolution_bitcast_fusion.1 = f32[1024,256]{0,1:T(8,128)S(1)} fusion(bf16[4096,256]{1,0:T(8,128)(2,1)} %shard_map.70, bf16[4096,1024]{1,0:T(8,128)(2,1)} %param.6), kind=kOutput, calls=%fused_computation.6 | convolution fusion | flops 2147483648 | bytes 11534336 | tf_op jit(solution)/shard_map/dot_general | solution.py:214
  100.1 0.3 copy.11
  100.5 1.1 pad_maximum_fusion.2.x_ref
  101.6 12.6 %shard_map.71 = bf16[64,256]{1,0:T(8,128)(2,1)} custom-call(f32[8,2,72,256]{3,2,1,0:T(8,128)} %pad_maximum_fusion.2.x_ref), custom_call_target="tpu_custom_call" | custom-call | tf_op jit(solution)/shard_map/pallas_call | solution.py:189
  114.3 1.4 %copy.14 = bf16[64,256]{1,0:T(8,128)(2,1)} copy(bf16[64,256]{1,0:T(8,128)(2,1)} %shard_map.71) | data formatting | bytes 65536
  (2 shorter events, 0.0 us)
Async XLA Ops:
  1.7 8.2 %collective-permute-start = (bf16[512,256]{1,0:T(8,128)(2,1)S(1)}, bf16[512,256]{1,0:T(8,128)(2,1)S(1)}, u32[]{:S(2)}, u32[]{:S(2)}) collective-permute-start(bf16[512,256]{1,0:T(8,128)(2,1)S(1)} %get-tuple-element.4), channel_id=1, source_target_pairs={{0,8},{8,16},{16,24},{24,32},{32,40},{40,48},{48,56},{56,64},{64,7... | collective-permute-start | bytes 786440 | tf_op jit(solution)/shard_map/ppermute | solution.py:20
  6.6 7.7 %collective-permute-start.1 = (bf16[512,256]{1,0:T(8,128)(2,1)S(1)}, bf16[512,256]{1,0:T(8,128)(2,1)S(1)}, u32[]{:S(2)}, u32[]{:S(2)}) collective-permute-start(bf16[512,256]{1,0:T(8,128)(2,1)S(1)} %get-tuple-element.5), channel_id=1, source_target_pairs={{8,0},{16,8},{24,16},{32,24},{40,32},{48,40},{56,48},{64,56},{72,6... | collective-permute-start | bytes 786440 | tf_op jit(solution)/shard_map/ppermute | solution.py:23
  38.4 23.1 %copy-start = (bf16[4096,256]{1,0:T(8,128)(2,1)S(1)}, bf16[4096,256]{1,0:T(8,128)(2,1)}, u32[]{:S(2)}) copy-start(bf16[4096,256]{1,0:T(8,128)(2,1)} %param.5) | copy-start | bytes 6291460
  67.4 10.3 %copy-start.1 = (bf16[4096,256]{1,0:T(8,128)(2,1)}, bf16[4096,256]{1,0:T(8,128)(2,1)S(1)}, u32[]{:S(2)}) copy-start(bf16[4096,256]{1,0:T(8,128)(2,1)S(1)} %get-tuple-element.10) | copy-start | bytes 6291460
  67.4 5.8 %collective-permute-start.2 = (bf16[512,256]{1,0:T(8,128)(2,1)S(1)}, bf16[512,256]{1,0:T(8,128)(2,1)S(1)}, u32[]{:S(2)}, u32[]{:S(2)}) collective-permute-start(bf16[512,256]{1,0:T(8,128)(2,1)S(1)} %get-tuple-element.2), channel_id=1, source_target_pairs={{0,8},{8,16},{16,24},{24,32},{32,40},{40,48},{48,56},{56,64},{64,7... | collective-permute-start | bytes 786440 | tf_op jit(solution)/shard_map/ppermute | solution.py:20
  70.0 7.7 %collective-permute-start.3 = (bf16[512,256]{1,0:T(8,128)(2,1)S(1)}, bf16[512,256]{1,0:T(8,128)(2,1)S(1)}, u32[]{:S(2)}, u32[]{:S(2)}) collective-permute-start(bf16[512,256]{1,0:T(8,128)(2,1)S(1)} %get-tuple-element.3), channel_id=1, source_target_pairs={{8,0},{16,8},{24,16},{32,24},{40,32},{48,40},{56,48},{64,56},{72,6... | collective-permute-start | bytes 786440 | tf_op jit(solution)/shard_map/ppermute | solution.py:23

commit v4 on v3

--- a/solution.py
+++ b/solution.py
@@ -25,38 +25,42 @@
     return block
 
 
-def band_kernel(off_ref, blk_ref, field_ref, out_ref):
-    b = pl.program_id(0)
-    acc = None
-    for k in range(KB):
-        start = pl.multiple_of((b + 2 + off_ref[b, k]) * BK, BK)
-        term = jnp.dot(
-            blk_ref[0, k], field_ref[pl.ds(start, BK), :], preferred_element_type=jnp.float32
-        )
-        acc = term if acc is None else acc + term
-    out_ref[...] = acc.astype(out_ref.dtype)
+def band_kernel(rows_per_step, off_ref, blk_ref, field_ref, out_ref):
+    g = pl.program_id(0)
+    for r in range(rows_per_step):
+        b = g * rows_per_step + r
+        acc = None
+        for k in range(KB):
+            start = pl.multiple_of((b + 2 + off_ref[b, k]) * BK, BK)
+            term = jnp.dot(
+                blk_ref[r, k], field_ref[pl.ds(start, BK), :], preferred_element_type=jnp.float32
+            )
+            acc = term if acc is None else acc + term
+        out_ref[pl.ds(r * BK, BK), :] = acc.astype(out_ref.dtype)
 
 
 def band_local(blocks, offsets, padded):
     nblk = blocks.shape[0]
     rows, width = padded.shape
+    per = 8 if nblk % 8 == 0 else 1
     return pl.pallas_call(
-        band_kernel,
+        functools.partial(band_kernel, per),
         out_shape=jax.ShapeDtypeStruct((nblk * BK, width), jnp.bfloat16),
         grid_spec=pltpu.PrefetchScalarGridSpec(
             num_scalar_prefetch=1,
-            grid=(nblk,),
+            grid=(nblk // per,),
             in_specs=[
-                pl.BlockSpec((1, KB, BK, BK), lambda b, off: (b, 0, 0, 0)),
-                pl.BlockSpec((rows, width), lambda b, off: (0, 0)),
+                pl.BlockSpec((per, KB, BK, BK), lambda g, off: (g, 0, 0, 0)),
+                pl.BlockSpec((rows, width), lambda g, off: (0, 0)),
             ],
-            out_specs=pl.BlockSpec((BK, width), lambda b, off: (b, 0)),
+            out_specs=pl.BlockSpec((per * BK, width), lambda g, off: (g, 0)),
         ),
         cost_estimate=pl.CostEstimate(
             flops=2 * nblk * KB * BK * BK * width,
             bytes_accessed=blocks.size * 2 + padded.size * 2 + nblk * BK * width * 2,
             transcendentals=0,
         ),
+        compiler_params=pltpu.CompilerParams(vmem_limit_bytes=24 * 1024 * 1024),
     )(offsets, blocks, padded)
 
 

time: 118 us -> 94.2 us (0.80)
  Pallas kernels: 63.2 us -> 40.8 us
  local copies, waits for them, and re-layouts: 5.5 us -> 11.8 us
  matrix products: 18.6 us -> 14 us
  other arithmetic: 6.11 us -> 3.06 us
    pallas_call x2, Pallas kernels: 28.8 us -> 6.43 us  [band_local(): pl.pallas_call(functools.partial(band_kernel, per), out_shape=jax.ShapeDt...]
    unnamed x6 -> x12, local copies, waits for them, and re-layouts: 2.75 us -> 9.06 us
    dot_general x1, matrix products: 6.37 us -> 2.35 us  [on_device(): lax.dot_general(target_orbitals, margin_cont, (((0,), (0,)), ((), ())), p...]
    concatenate x2, other arithmetic: 4.98 us -> 1.93 us  [padded_2(): block = jnp.concatenate([low, block, high], axis=dim)]
  transfers between devices with their start and end apart: 4 -> 4, of which waited for: 3 -> 4; matrix products, arithmetic and copies ran while one was open for 1% -> 1% of each run, Pallas kernels for 0% -> 0%
where the time goes in v4:
time: 94.2 us; the launch traced here: 92.6 us
  Pallas kernels  40.8 us (43%)
  matrix products  14 us (15%)
  local copies, waits for them, and re-layouts  11.8 us (13%)
  starting transfers between devices  11.3 us (12%)
  waiting for transfers between devices  10.8 us (11%)
  other arithmetic  3.06 us (3%)
    pallas_call x1, Pallas kernels, allreduce_to_bf16(): pl.pallas_call(functools.partial(allreduce_kernel, nchip), out_shape=jax....  21.8 us
    pallas_call x1, Pallas kernels, dipole_scatter(): pl.pallas_call(functools.partial(dipole_kernel, nchip, chunk, count), out...  12.7 us
    unnamed x12, local copies, waits for them, and re-layouts  9.06 us
    ppermute x2, waiting for transfers between devices, padded_2(): lax.ppermute(lax.slice_in_dim(block, 0, width, axis=dim), axis, backward)  8.79 us
    ppermute x2, starting transfers between devices, padded_2(): lax.ppermute(lax.slice_in_dim(block, block.shape[dim] - width, None, axis...  7.46 us
    pallas_call x2, Pallas kernels, band_local(): pl.pallas_call(functools.partial(band_kernel, per), out_shape=jax.ShapeDt...  6.43 us
    dot_general x1, matrix products, on_device(): jnp.dot(target_orbitals, projection_b, preferred_element_type=jnp.float32)  5.96 us
    dot_general x1, matrix products, on_device(): lax.dot_general(target_orbitals, dipole_cont, (((0,), (0,)), ((), ())), p...  5.74 us
  transfers between devices with their start and end apart: 4, of which 4 were waited for; matrix products, arithmetic and copies ran while one was open for 1% of the time, Pallas kernels for 0%

profile of v4, /device:TPU:1, one launch (start us, length us, event | category | flops | bytes accessed | tf_op | source)
XLA Modules:
  0.0 92.6 jit_solution(17501511119614940636)
XLA Ops:
  0.6 1.1 %fusion.3 = (bf16[512,256]{1,0:T(8,128)(2,1)S(1)}, bf16[512,256]{1,0:T(8,128)(2,1)S(1)}) fusion(bf16[4096,256]{1,0:T(8,128)(2,1)} %param.5), kind=kLoop, calls=%fused_computation.10 | loop fusion | bytes 1048576 | tf_op jit(solution)/shard_map/slice | solution.py:21
  1.7 4.9 %collective-permute-start = (bf16[512,256]{1,0:T(8,128)(2,1)S(1)}, bf16[512,256]{1,0:T(8,128)(2,1)S(1)}, u32[]{:S(2)}, u32[]{:S(2)}) collective-permute-start(bf16[512,256]{1,0:T(8,128)(2,1)S(1)} %get-tuple-element.4), channel_id=1, source_target_pairs={{0,8},{8,16},{16,24},{24,32},{32,40},{40,48},{48,56},{56,64},{64,7... | collective-permute-start | bytes 786440 | tf_op jit(solution)/shard_map/ppermute | solution.py:20
  6.6 1.9 %collective-permute-start.1 = (bf16[512,256]{1,0:T(8,128)(2,1)S(1)}, bf16[512,256]{1,0:T(8,128)(2,1)S(1)}, u32[]{:S(2)}, u32[]{:S(2)}) collective-permute-start(bf16[512,256]{1,0:T(8,128)(2,1)S(1)} %get-tuple-element.5), channel_id=1, source_target_pairs={{8,0},{16,8},{24,16},{32,24},{40,32},{48,40},{56,48},{64,56},{72,6... | collective-permute-start | bytes 786440 | tf_op jit(solution)/shard_map/ppermute | solution.py:23
  8.6 0.8 copy.7.off_ref
  9.3 0.6 collective-permute-done
  9.9 4.4 %collective-permute-done.1 = bf16[512,256]{1,0:T(8,128)(2,1)S(1)} collective-permute-done((bf16[512,256]{1,0:T(8,128)(2,1)S(1)}, bf16[512,256]{1,0:T(8,128)(2,1)S(1)}, u32[]{:S(2)}, u32[]{:S(2)}) %collective-permute-start.1) | collective-permute-done | bytes 262176 | tf_op jit(solution)/shard_map/ppermute | solution.py:23
  14.3 1.8 %pad_maximum_fusion.field_ref = bf16[5120,256]{1,0:T(8,128)(2,1)S(1)} fusion(bf16[512,256]{1,0:T(8,128)(2,1)S(1)} %collective-permute-done.1, bf16[4096,256]{1,0:T(8,128)(2,1)} %param.5, bf16[512,256]{1,0:T(8,128)(2,1)S(1)} %collective-permute-done), kind=kLoop, calls=%fused_computation.4 | loop fusion | flops 7864320 | bytes 5242880 | tf_op jit(solution)/shard_map/concatenate | solution.py:24
  16.1 0.0 copy-start
  16.1 3.4 %copy-done = bf16[16,4,256,256]{3,2,1,0:T(8,128)(2,1)S(1)} copy-done((bf16[16,4,256,256]{3,2,1,0:T(8,128)(2,1)S(1)}, bf16[16,4,256,256]{3,2,1,0:T(8,128)(2,1)}, u32[]{:S(2)}) %copy-start) | copy-done | bytes 8388632
  19.5 0.0 copy-start.2
  19.5 3.2 %shard_map.68 = bf16[4096,256]{1,0:T(8,128)(2,1)S(1)} custom-call(s32[16,4]{1,0:T(8,128)S(1)} %copy.7.off_ref, bf16[16,4,256,256]{3,2,1,0:T(8,128)(2,1)S(1)} %copy-done, bf16[5120,256]{1,0:T(8,128)(2,1)S(1)} %pad_maximum_fusion.field_ref), custom_call_target="tpu_custom_call" | custom-call | flops 2147483648 | bytes 13107200 | tf_op jit(solution)/shard_map/pallas_call | solution.py:46
  22.7 0.2 copy-done.2
  22.9 2.3 %convolution_bitcast_fusion.2 = f32[1024,256]{0,1:T(8,128)S(1)} fusion(bf16[4096,256]{1,0:T(8,128)(2,1)S(1)} %shard_map.68, bf16[4096,1024]{1,0:T(8,128)(2,1)S(1)} %copy-done.2), kind=kOutput, calls=%fused_computation.7 | convolution fusion | flops 2147483648 | bytes 11534336 | tf_op jit(solution)/shard_map/dot_general | solution.py:209
  25.2 0.0 copy-start.3
  25.2 1.3 %copy.8 = f32[1024,256]{1,0:T(8,128)} copy(f32[1024,256]{0,1:T(8,128)S(1)} %convolution_bitcast_fusion.2) | data formatting | bytes 2097152 | tf_op jit(solution)/shard_map/dot_general | solution.py:209
  26.5 21.8 %shard_map.69 = bf16[8,2,64,256]{3,2,1,0:T(8,128)(2,1)} custom-call(f32[8,2,64,256]{3,2,1,0:T(8,128)} %bitcast.20), custom_call_target="tpu_custom_call" | custom-call | tf_op jit(solution)/shard_map/pallas_call | solution.py:159
  48.3 0.0 copy-done.3
  48.3 6.0 %multiply_reduce_fusion = (f32[256]{0:T(256)S(1)}, bf16[4096,256]{1,0:T(8,128)(2,1)S(1)}) fusion(bf16[4096,1024]{1,0:T(8,128)(2,1)} %param.6, bf16[1024,256]{1,0:T(8,128)(2,1)} %bitcast.21, bf16[4096,256]{1,0:T(8,128)(2,1)S(1)} %copy-done.3), kind=kOutput, calls=%fused_computation.3 | convolution fusion | flops 2153774848 | bytes 13108224 | tf_op jit(solution)/shard_map/dot_general | solution.py:213
  54.3 0.0 copy-start.4
  54.3 2.5 %collective-permute-start.2 = (bf16[512,256]{1,0:T(8,128)(2,1)S(1)}, bf16[512,256]{1,0:T(8,128)(2,1)S(1)}, u32[]{:S(2)}, u32[]{:S(2)}) collective-permute-start(bf16[512,256]{1,0:T(8,128)(2,1)S(1)} %get-tuple-element.2), channel_id=1, source_target_pairs={{0,8},{8,16},{16,24},{24,32},{32,40},{40,48},{48,56},{56,64},{64,7... | collective-permute-start | bytes 786440 | tf_op jit(solution)/shard_map/ppermute | solution.py:20
  56.9 1.9 %collective-permute-start.3 = (bf16[512,256]{1,0:T(8,128)(2,1)S(1)}, bf16[512,256]{1,0:T(8,128)(2,1)S(1)}, u32[]{:S(2)}, u32[]{:S(2)}) collective-permute-start(bf16[512,256]{1,0:T(8,128)(2,1)S(1)} %get-tuple-element.3), channel_id=1, source_target_pairs={{8,0},{16,8},{24,16},{32,24},{40,32},{48,40},{56,48},{64,56},{72,6... | collective-permute-start | bytes 786440 | tf_op jit(solution)/shard_map/ppermute | solution.py:23
  58.8 1.4 %collective-permute-done.2 = bf16[512,256]{1,0:T(8,128)(2,1)S(1)} collective-permute-done((bf16[512,256]{1,0:T(8,128)(2,1)S(1)}, bf16[512,256]{1,0:T(8,128)(2,1)S(1)}, u32[]{:S(2)}, u32[]{:S(2)}) %collective-permute-start.2) | collective-permute-done | bytes 262176 | tf_op jit(solution)/shard_map/ppermute | solution.py:20
  60.2 4.4 %collective-permute-done.3 = bf16[512,256]{1,0:T(8,128)(2,1)S(1)} collective-permute-done((bf16[512,256]{1,0:T(8,128)(2,1)S(1)}, bf16[512,256]{1,0:T(8,128)(2,1)S(1)}, u32[]{:S(2)}, u32[]{:S(2)}) %collective-permute-start.3) | collective-permute-done | bytes 262176 | tf_op jit(solution)/shard_map/ppermute | solution.py:23
  64.5 0.0 copy-done.4
  64.6 0.2 pad_maximum_fusion.1.field_ref
  64.7 0.0 copy-start.1
  64.7 3.4 %copy-done.1 = bf16[16,4,256,256]{3,2,1,0:T(8,128)(2,1)S(1)} copy-done((bf16[16,4,256,256]{3,2,1,0:T(8,128)(2,1)S(1)}, bf16[16,4,256,256]{3,2,1,0:T(8,128)(2,1)}, u32[]{:S(2)}) %copy-start.1) | copy-done | bytes 8388632
  68.1 3.2 %shard_map.70 = bf16[4096,256]{1,0:T(8,128)(2,1)S(1)} custom-call(s32[16,4]{1,0:T(8,128)S(1)} %copy.7.off_ref, bf16[16,4,256,256]{3,2,1,0:T(8,128)(2,1)S(1)} %copy-done.1, bf16[5120,256]{1,0:T(8,128)(2,1)S(1)} %pad_maximum_fusion.1.field_ref), custom_call_target="tpu_custom_call" | custom-call | flops 2147483648 | bytes 13107200 | tf_op jit(solution)/shard_map/pallas_call | solution.py:46
  71.3 5.7 %convolution_bitcast_fusion.1 = f32[1024,256]{0,1:T(8,128)S(1)} fusion(bf16[4096,256]{1,0:T(8,128)(2,1)S(1)} %shard_map.70, bf16[4096,1024]{1,0:T(8,128)(2,1)} %param.6), kind=kOutput, calls=%fused_computation.6 | convolution fusion | flops 2147483648 | bytes 11534336 | tf_op jit(solution)/shard_map/dot_general | solution.py:218
  77.1 0.3 copy.11
  77.4 1.1 %pad_maximum_fusion.2.x_ref = f32[8,2,72,256]{3,2,1,0:T(8,128)} fusion(f32[8,2,8,256]{3,2,1,0:T(8,128)S(1)} %broadcast_in_dim.2, f32[8,2,64,256]{3,2,1,0:T(8,128)S(1)} %bitcast.19), kind=kLoop, calls=%fused_computation.8 | loop fusion | flops 294912 | bytes 2359296 | tf_op jit(solution)/shard_map/concatenate | solution.py:186
  78.6 12.7 %shard_map.71 = bf16[64,256]{1,0:T(8,128)(2,1)} custom-call(f32[8,2,72,256]{3,2,1,0:T(8,128)} %pad_maximum_fusion.2.x_ref), custom_call_target="tpu_custom_call" | custom-call | tf_op jit(solution)/shard_map/pallas_call | solution.py:193
  91.2 1.4 %copy.14 = bf16[64,256]{1,0:T(8,128)(2,1)} copy(bf16[64,256]{1,0:T(8,128)(2,1)} %shard_map.71) | data formatting | bytes 65536
  (2 shorter events, 0.0 us)
Async XLA Ops:
  1.7 8.2 %collective-permute-start = (bf16[512,256]{1,0:T(8,128)(2,1)S(1)}, bf16[512,256]{1,0:T(8,128)(2,1)S(1)}, u32[]{:S(2)}, u32[]{:S(2)}) collective-permute-start(bf16[512,256]{1,0:T(8,128)(2,1)S(1)} %get-tuple-element.4), channel_id=1, source_target_pairs={{0,8},{8,16},{16,24},{24,32},{32,40},{40,48},{48,56},{56,64},{64,7... | collective-permute-start | bytes 786440 | tf_op jit(solution)/shard_map/ppermute | solution.py:20
  6.6 7.7 %collective-permute-start.1 = (bf16[512,256]{1,0:T(8,128)(2,1)S(1)}, bf16[512,256]{1,0:T(8,128)(2,1)S(1)}, u32[]{:S(2)}, u32[]{:S(2)}) collective-permute-start(bf16[512,256]{1,0:T(8,128)(2,1)S(1)} %get-tuple-element.5), channel_id=1, source_target_pairs={{8,0},{16,8},{24,16},{32,24},{40,32},{48,40},{56,48},{64,56},{72,6... | collective-permute-start | bytes 786440 | tf_op jit(solution)/shard_map/ppermute | solution.py:23
  16.1 3.4 %copy-start = (bf16[16,4,256,256]{3,2,1,0:T(8,128)(2,1)S(1)}, bf16[16,4,256,256]{3,2,1,0:T(8,128)(2,1)}, u32[]{:S(2)}) copy-start(bf16[16,4,256,256]{3,2,1,0:T(8,128)(2,1)} %blk_ref.2) | copy-start | bytes 25165828
  19.5 3.4 %copy-start.2 = (bf16[4096,1024]{1,0:T(8,128)(2,1)S(1)}, bf16[4096,1024]{1,0:T(8,128)(2,1)}, u32[]{:S(2)}) copy-start(bf16[4096,1024]{1,0:T(8,128)(2,1)} %param.6) | copy-start | bytes 25165828
  25.2 23.1 %copy-start.3 = (bf16[4096,256]{1,0:T(8,128)(2,1)S(1)}, bf16[4096,256]{1,0:T(8,128)(2,1)}, u32[]{:S(2)}) copy-start(bf16[4096,256]{1,0:T(8,128)(2,1)} %param.5) | copy-start | bytes 6291460
  54.3 10.3 %copy-start.4 = (bf16[4096,256]{1,0:T(8,128)(2,1)}, bf16[4096,256]{1,0:T(8,128)(2,1)S(1)}, u32[]{:S(2)}) copy-start(bf16[4096,256]{1,0:T(8,128)(2,1)S(1)} %get-tuple-element.10) | copy-start | bytes 6291460
  54.3 5.8 %collective-permute-start.2 = (bf16[512,256]{1,0:T(8,128)(2,1)S(1)}, bf16[512,256]{1,0:T(8,128)(2,1)S(1)}, u32[]{:S(2)}, u32[]{:S(2)}) collective-permute-start(bf16[512,256]{1,0:T(8,128)(2,1)S(1)} %get-tuple-element.2), channel_id=1, source_target_pairs={{0,8},{8,16},{16,24},{24,32},{32,40},{40,48},{48,56},{56,64},{64,7... | collective-permute-start | bytes 786440 | tf_op jit(solution)/shard_map/ppermute | solution.py:20
  56.9 7.7 %collective-permute-start.3 = (bf16[512,256]{1,0:T(8,128)(2,1)S(1)}, bf16[512,256]{1,0:T(8,128)(2,1)S(1)}, u32[]{:S(2)}, u32[]{:S(2)}) collective-permute-start(bf16[512,256]{1,0:T(8,128)(2,1)S(1)} %get-tuple-element.3), channel_id=1, source_target_pairs={{8,0},{16,8},{24,16},{32,24},{40,32},{48,40},{56,48},{64,56},{72,6... | collective-permute-start | bytes 786440 | tf_op jit(solution)/shard_map/ppermute | solution.py:23
  64.7 3.4 %copy-start.1 = (bf16[16,4,256,256]{3,2,1,0:T(8,128)(2,1)S(1)}, bf16[16,4,256,256]{3,2,1,0:T(8,128)(2,1)}, u32[]{:S(2)}) copy-start(bf16[16,4,256,256]{3,2,1,0:T(8,128)(2,1)} %blk_ref.3) | copy-start | bytes 25165828

commit v5 on v4

--- a/solution.py
+++ b/solution.py
@@ -166,7 +166,10 @@
             pltpu.VMEM((nchip, chunk, cols), jnp.bfloat16),
             pltpu.VMEM((nchip, chunk, cols), jnp.bfloat16),
         ] + [pltpu.SemaphoreType.DMA((nchip,))] * 6 + [pltpu.SemaphoreType.DMA((1,))] * 2,
-        compiler_params=pltpu.CompilerParams(collective_id=0, has_side_effects=True),
+        compiler_params=pltpu.CompilerParams(
+            collective_id=0, has_side_effects=True, vmem_limit_bytes=12 * 1024 * 1024
+        ),
+        cost_estimate=pl.CostEstimate(flops=0, bytes_accessed=64 * x.size, transcendentals=0),
     )(x)
     return out.reshape(rows, cols)
 
@@ -197,7 +200,10 @@
         out_specs=pl.BlockSpec(memory_space=pltpu.VMEM),
         scratch_shapes=_two_level_scratch(nchip, chunk + 8, cols)
         + [pltpu.SemaphoreType.DMA((nchip,))] * 4,
-        compiler_params=pltpu.CompilerParams(collective_id=1, has_side_effects=True),
+        compiler_params=pltpu.CompilerParams(
+            collective_id=1, has_side_effects=True, vmem_limit_bytes=12 * 1024 * 1024
+        ),
+        cost_estimate=pl.CostEstimate(flops=0, bytes_accessed=32 * x.size, transcendentals=0),
     )(x)
 
 

time: 94.2 us -> 81.7 us (0.87)
  the two profiles are of different devices: /device:TPU:1 before, /device:TPU:0 now
where the time goes in v5:
time: 81.7 us; the launch traced here: 81.3 us
  Pallas kernels  48.3 us (59%)
  matrix products  11.3 us (14%)
  local copies, waits for them, and re-layouts  6.8 us (8%)
  starting transfers between devices  6.22 us (8%)
  waiting for transfers between devices  5.82 us (7%)
  other arithmetic  2.03 us (2%)
  between operations  0.84 us (1%)
    pallas_call x1, Pallas kernels, allreduce_to_bf16(): pl.pallas_call(functools.partial(allreduce_kernel, nchip), out_shape=jax....  24.2 us
    pallas_call x1, Pallas kernels, dipole_scatter(): pl.pallas_call(functools.partial(dipole_kernel, nchip, chunk, count), out...  17.7 us
    dot_general x1, matrix products, on_device(): jnp.dot(target_orbitals, projection_b, preferred_element_type=jnp.float32)  6.59 us
    pallas_call x2, Pallas kernels, band_local(): pl.pallas_call(functools.partial(band_kernel, per), out_shape=jax.ShapeDt...  6.43 us
    ppermute x2, waiting for transfers between devices, padded_2(): lax.ppermute(lax.slice_in_dim(block, 0, width, axis=dim), axis, backward)  5.81 us
    unnamed x16, local copies, waits for them, and re-layouts  5.02 us
    ppermute x2, starting transfers between devices, padded_2(): lax.ppermute(lax.slice_in_dim(block, block.shape[dim] - width, None, axis...  3.63 us
    ppermute x2, starting transfers between devices, padded_2(): lax.ppermute(lax.slice_in_dim(block, 0, width, axis=dim), axis, backward)  2.58 us
  transfers between devices with their start and end apart: 4, of which 2 were waited for; matrix products, arithmetic and copies ran while one was open for 1% of the time, Pallas kernels for 0%

profile of v5, /device:TPU:0, one launch (start us, length us, event | category | flops | bytes accessed | tf_op | source)
XLA Modules:
  0.0 81.3 jit_solution(3188517119933820221)
XLA Ops:
  0.6 1.1 %fusion.3 = (bf16[512,256]{1,0:T(8,128)(2,1)S(1)}, bf16[512,256]{1,0:T(8,128)(2,1)S(1)}) fusion(bf16[4096,256]{1,0:T(8,128)(2,1)} %param.5), kind=kLoop, calls=%fused_computation.10 | loop fusion | bytes 1048576 | tf_op jit(solution)/shard_map/slice | solution.py:21
  1.7 1.3 %collective-permute-start = (bf16[512,256]{1,0:T(8,128)(2,1)S(1)}, bf16[512,256]{1,0:T(8,128)(2,1)S(1)}, u32[]{:S(2)}, u32[]{:S(2)}) collective-permute-start(bf16[512,256]{1,0:T(8,128)(2,1)S(1)} %get-tuple-element.4), channel_id=1, source_target_pairs={{0,8},{8,16},{16,24},{24,32},{32,40},{40,48},{48,56},{56,64},{64,7... | collective-permute-start | bytes 786440 | tf_op jit(solution)/shard_map/ppermute | solution.py:20
  3.0 1.3 %collective-permute-start.1 = (bf16[512,256]{1,0:T(8,128)(2,1)S(1)}, bf16[512,256]{1,0:T(8,128)(2,1)S(1)}, u32[]{:S(2)}, u32[]{:S(2)}) collective-permute-start(bf16[512,256]{1,0:T(8,128)(2,1)S(1)} %get-tuple-element.5), channel_id=1, source_target_pairs={{8,0},{16,8},{24,16},{32,24},{40,32},{48,40},{56,48},{64,56},{72,6... | collective-permute-start | bytes 786440 | tf_op jit(solution)/shard_map/ppermute | solution.py:23
  4.3 0.8 copy.7.off_ref
  5.1 0.0 collective-permute-done
  5.1 3.6 %collective-permute-done.1 = bf16[512,256]{1,0:T(8,128)(2,1)S(1)} collective-permute-done((bf16[512,256]{1,0:T(8,128)(2,1)S(1)}, bf16[512,256]{1,0:T(8,128)(2,1)S(1)}, u32[]{:S(2)}, u32[]{:S(2)}) %collective-permute-start.1) | collective-permute-done | bytes 262176 | tf_op jit(solution)/shard_map/ppermute | solution.py:23
  8.7 1.8 %pad_maximum_fusion.field_ref = bf16[5120,256]{1,0:T(8,128)(2,1)S(1)} fusion(bf16[512,256]{1,0:T(8,128)(2,1)S(1)} %collective-permute-done.1, bf16[4096,256]{1,0:T(8,128)(2,1)} %param.5, bf16[512,256]{1,0:T(8,128)(2,1)S(1)} %collective-permute-done), kind=kLoop, calls=%fused_computation.4 | loop fusion | flops 7864320 | bytes 5242880 | tf_op jit(solution)/shard_map/concatenate | solution.py:24
  10.4 0.0 copy-start
  10.4 3.4 %copy-done = bf16[16,4,256,256]{3,2,1,0:T(8,128)(2,1)S(1)} copy-done((bf16[16,4,256,256]{3,2,1,0:T(8,128)(2,1)S(1)}, bf16[16,4,256,256]{3,2,1,0:T(8,128)(2,1)}, u32[]{:S(2)}) %copy-start) | copy-done | bytes 8388632
  13.8 0.0 copy-start.1
  13.8 3.2 %shard_map.68 = bf16[4096,256]{1,0:T(8,128)(2,1)S(1)} custom-call(s32[16,4]{1,0:T(8,128)S(1)} %copy.7.off_ref, bf16[16,4,256,256]{3,2,1,0:T(8,128)(2,1)S(1)} %copy-done, bf16[5120,256]{1,0:T(8,128)(2,1)S(1)} %pad_maximum_fusion.field_ref), custom_call_target="tpu_custom_call" | custom-call | flops 2147483648 | bytes 13107200 | tf_op jit(solution)/shard_map/pallas_call | solution.py:46
  17.0 0.2 copy-done.1
  17.2 2.4 %convolution_bitcast_fusion.2 = f32[1024,256]{0,1:T(8,128)S(1)} fusion(bf16[4096,256]{1,0:T(8,128)(2,1)S(1)} %shard_map.68, bf16[4096,1024]{1,0:T(8,128)(2,1)S(1)} %copy-done.1), kind=kOutput, calls=%fused_computation.7 | convolution fusion | flops 2147483648 | bytes 11534336 | tf_op jit(solution)/shard_map/dot_general | solution.py:215
  19.6 0.3 copy.8
  19.9 0.0 slice-start
  19.9 24.2 %shard_map.69 = bf16[8,2,64,256]{3,2,1,0:T(8,128)(2,1)S(1)} custom-call(f32[8,2,64,256]{3,2,1,0:T(8,128)S(1)} %bitcast.21), custom_call_target="tpu_custom_call" | custom-call | bytes 16777216 | tf_op jit(solution)/shard_map/pallas_call | solution.py:159
  44.1 0.0 slice-start.1
  44.1 6.6 %multiply_reduce_fusion = (f32[256]{0:T(256)S(1)}, bf16[4096,256]{1,0:T(8,128)(2,1)S(1)}) fusion(bf16[4096,1024]{1,0:T(8,128)(2,1)} %param.6, bf16[1024,256]{1,0:T(8,128)(2,1)S(1)} %bitcast.22, bf16[4096,256]{1,0:T(8,128)(2,1)} %param.5), kind=kOutput, calls=%fused_computation.3 | convolution fusion | flops 2153774848 | bytes 13108224 | tf_op jit(solution)/shard_map/dot_general | solution.py:219
  50.7 0.0 copy-start.2
  50.8 2.3 %collective-permute-start.2 = (bf16[512,256]{1,0:T(8,128)(2,1)S(1)}, bf16[512,256]{1,0:T(8,128)(2,1)S(1)}, u32[]{:S(2)}, u32[]{:S(2)}) collective-permute-start(bf16[512,256]{1,0:T(8,128)(2,1)S(1)} %get-tuple-element.2), channel_id=1, source_target_pairs={{0,8},{8,16},{16,24},{24,32},{32,40},{40,48},{48,56},{56,64},{64,7... | collective-permute-start | bytes 786440 | tf_op jit(solution)/shard_map/ppermute | solution.py:20
  53.1 1.3 %collective-permute-start.3 = (bf16[512,256]{1,0:T(8,128)(2,1)S(1)}, bf16[512,256]{1,0:T(8,128)(2,1)S(1)}, u32[]{:S(2)}, u32[]{:S(2)}) collective-permute-start(bf16[512,256]{1,0:T(8,128)(2,1)S(1)} %get-tuple-element.3), channel_id=1, source_target_pairs={{8,0},{16,8},{24,16},{32,24},{40,32},{48,40},{56,48},{64,56},{72,6... | collective-permute-start | bytes 786440 | tf_op jit(solution)/shard_map/ppermute | solution.py:23
  54.4 0.0 collective-permute-done.2
  54.4 2.2 %collective-permute-done.3 = bf16[512,256]{1,0:T(8,128)(2,1)S(1)} collective-permute-done((bf16[512,256]{1,0:T(8,128)(2,1)S(1)}, bf16[512,256]{1,0:T(8,128)(2,1)S(1)}, u32[]{:S(2)}, u32[]{:S(2)}) %collective-permute-start.3) | collective-permute-done | bytes 262176 | tf_op jit(solution)/shard_map/ppermute | solution.py:23
  56.6 0.0 copy-done.2
  56.6 0.0 slice-start.2
  56.7 0.2 pad_maximum_fusion.1.field_ref
  56.8 0.0 slice-done
  56.8 0.0 slice-done.1
  56.9 0.0 slice-start.3
  56.9 3.2 %shard_map.70 = bf16[4096,256]{1,0:T(8,128)(2,1)S(1)} custom-call(s32[16,4]{1,0:T(8,128)S(1)} %copy.7.off_ref, bf16[16,4,256,256]{3,2,1,0:T(8,128)(2,1)S(1)} %bitcast.20, bf16[5120,256]{1,0:T(8,128)(2,1)S(1)} %pad_maximum_fusion.1.field_ref), custom_call_target="tpu_custom_call" | custom-call | flops 2147483648 | bytes 13107200 | tf_op jit(solution)/shard_map/pallas_call | solution.py:46
  60.1 0.0 slice-done.2
  60.1 0.1 slice-done.3
  60.2 2.4 %convolution_bitcast_fusion.1 = f32[1024,256]{0,1:T(8,128)S(1)} fusion(bf16[4096,256]{1,0:T(8,128)(2,1)S(1)} %shard_map.70, bf16[4096,1024]{1,0:T(8,128)(2,1)S(1)} %bitcast.24), kind=kOutput, calls=%fused_computation.6 | convolution fusion | flops 2147483648 | bytes 11534336 | tf_op jit(solution)/shard_map/dot_general | solution.py:224
  62.5 0.3 copy.11
  62.9 0.1 pad_maximum_fusion.2.x_ref
  63.0 17.7 %shard_map.71 = bf16[64,256]{1,0:T(8,128)(2,1)S(1)} custom-call(f32[8,2,72,256]{3,2,1,0:T(8,128)S(1)} %pad_maximum_fusion.2.x_ref), custom_call_target="tpu_custom_call" | custom-call | bytes 9437184 | tf_op jit(solution)/shard_map/pallas_call | solution.py:196
  80.7 0.6 copy.14
  (4 shorter events, 0.0 us)
Async XLA Ops:
  1.7 3.4 %collective-permute-start = (bf16[512,256]{1,0:T(8,128)(2,1)S(1)}, bf16[512,256]{1,0:T(8,128)(2,1)S(1)}, u32[]{:S(2)}, u32[]{:S(2)}) collective-permute-start(bf16[512,256]{1,0:T(8,128)(2,1)S(1)} %get-tuple-element.4), channel_id=1, source_target_pairs={{0,8},{8,16},{16,24},{24,32},{32,40},{40,48},{48,56},{56,64},{64,7... | collective-permute-start | bytes 786440 | tf_op jit(solution)/shard_map/ppermute | solution.py:20
  3.0 5.7 %collective-permute-start.1 = (bf16[512,256]{1,0:T(8,128)(2,1)S(1)}, bf16[512,256]{1,0:T(8,128)(2,1)S(1)}, u32[]{:S(2)}, u32[]{:S(2)}) collective-permute-start(bf16[512,256]{1,0:T(8,128)(2,1)S(1)} %get-tuple-element.5), channel_id=1, source_target_pairs={{8,0},{16,8},{24,16},{32,24},{40,32},{48,40},{56,48},{64,56},{72,6... | collective-permute-start | bytes 786440 | tf_op jit(solution)/shard_map/ppermute | solution.py:23
  10.4 3.4 %copy-start = (bf16[16,4,256,256]{3,2,1,0:T(8,128)(2,1)S(1)}, bf16[16,4,256,256]{3,2,1,0:T(8,128)(2,1)}, u32[]{:S(2)}) copy-start(bf16[16,4,256,256]{3,2,1,0:T(8,128)(2,1)} %blk_ref.2) | copy-start | bytes 25165828
  13.8 3.4 %copy-start.1 = (bf16[4096,1024]{1,0:T(8,128)(2,1)S(1)}, bf16[4096,1024]{1,0:T(8,128)(2,1)}, u32[]{:S(2)}) copy-start(bf16[4096,1024]{1,0:T(8,128)(2,1)} %param.6) | copy-start | bytes 25165828
  19.9 36.9 %slice-start = ((s8[8388608]{0:T(1024)(128)(4,1)}), s8[4194304]{0:T(1024)(128)(4,1)S(1)}, s32[]{:S(2)}) async-start(s8[8388608]{0:T(1024)(128)(4,1)} %bitcast.19), calls=%async_computation | async-start | bytes 8388608
  44.1 12.7 %slice-start.1 = ((s8[8388608]{0:T(1024)(128)(4,1)}), s8[4194304]{0:T(1024)(128)(4,1)S(1)}, s32[]{:S(2)}) async-start(s8[8388608]{0:T(1024)(128)(4,1)} %bitcast.19), calls=%async_computation.1 | async-start | bytes 8388608
  50.7 5.9 %copy-start.2 = (bf16[4096,256]{1,0:T(8,128)(2,1)}, bf16[4096,256]{1,0:T(8,128)(2,1)S(1)}, u32[]{:S(2)}) copy-start(bf16[4096,256]{1,0:T(8,128)(2,1)S(1)} %get-tuple-element.10) | copy-start | bytes 6291460
  50.8 3.6 %collective-permute-start.2 = (bf16[512,256]{1,0:T(8,128)(2,1)S(1)}, bf16[512,256]{1,0:T(8,128)(2,1)S(1)}, u32[]{:S(2)}, u32[]{:S(2)}) collective-permute-start(bf16[512,256]{1,0:T(8,128)(2,1)S(1)} %get-tuple-element.2), channel_id=1, source_target_pairs={{0,8},{8,16},{16,24},{24,32},{32,40},{40,48},{48,56},{56,64},{64,7... | collective-permute-start | bytes 786440 | tf_op jit(solution)/shard_map/ppermute | solution.py:20
  53.1 3.5 %collective-permute-start.3 = (bf16[512,256]{1,0:T(8,128)(2,1)S(1)}, bf16[512,256]{1,0:T(8,128)(2,1)S(1)}, u32[]{:S(2)}, u32[]{:S(2)}) collective-permute-start(bf16[512,256]{1,0:T(8,128)(2,1)S(1)} %get-tuple-element.3), channel_id=1, source_target_pairs={{8,0},{16,8},{24,16},{32,24},{40,32},{48,40},{56,48},{64,56},{72,6... | collective-permute-start | bytes 786440 | tf_op jit(solution)/shard_map/ppermute | solution.py:23
  56.6 3.4 %slice-start.2 = ((s8[8388608]{0:T(1024)(128)(4,1)}), s8[4194304]{0:T(1024)(128)(4,1)S(1)}, s32[]{:S(2)}) async-start(s8[8388608]{0:T(1024)(128)(4,1)} %bitcast.23), calls=%async_computation.2 | async-start | bytes 8388608
  56.9 3.3 %slice-start.3 = ((s8[8388608]{0:T(1024)(128)(4,1)}), s8[4194304]{0:T(1024)(128)(4,1)S(1)}, s32[]{:S(2)}) async-start(s8[8388608]{0:T(1024)(128)(4,1)} %bitcast.23), calls=%async_computation.3 | async-start | bytes 8388608

commit v6 on v5

--- a/solution.py
+++ b/solution.py
@@ -25,43 +25,124 @@
     return block
 
 
-def band_kernel(rows_per_step, off_ref, blk_ref, field_ref, out_ref):
-    g = pl.program_id(0)
-    for r in range(rows_per_step):
-        b = g * rows_per_step + r
+def band_kernel(n, off_ref, blk_hbm, field_ref, out_ref, blk, low, high, blk_sem, send_sem, recv_sem):
+    nblk = blk.shape[0]
+    me = lax.axis_index("basis")
+    orb = lax.axis_index("orb")
+    has_low = me > 0
+    has_high = me < n - 1
+    loads = []
+    for b in range(nblk):
+        cp = pltpu.make_async_copy(blk_hbm.at[b], blk.at[b], blk_sem.at[b])
+        cp.start()
+        loads.append(cp)
+    barrier = pltpu.get_barrier_semaphore()
+
+    @pl.when(has_low)
+    def _():
+        pl.semaphore_signal(barrier, inc=1, device_id=(me - 1, orb), device_id_type=MESH)
+
+    @pl.when(has_high)
+    def _():
+        pl.semaphore_signal(barrier, inc=1, device_id=(me + 1, orb), device_id_type=MESH)
+
+    pl.semaphore_wait(barrier, has_low.astype(jnp.int32) + has_high.astype(jnp.int32))
+    to_low = pltpu.make_async_remote_copy(
+        src_ref=field_ref.at[pl.ds(0, 2)], dst_ref=high.at[pl.ds(4, 2)],
+        send_sem=send_sem.at[0], recv_sem=recv_sem.at[0],
+        device_id=(jnp.maximum(me - 1, 0), orb), device_id_type=MESH,
+    )
+    to_high = pltpu.make_async_remote_copy(
+        src_ref=field_ref.at[pl.ds(nblk - 2, 2)], dst_ref=low.at[pl.ds(0, 2)],
+        send_sem=send_sem.at[1], recv_sem=recv_sem.at[1],
+        device_id=(jnp.minimum(me + 1, n - 1), orb), device_id_type=MESH,
+    )
+
+    @pl.when(has_low)
+    def _():
+        to_low.start()
+
+    @pl.when(has_high)
+    def _():
+        to_high.start()
+
+    for i in range(4):
+        low[2 + i] = field_ref[i]
+        high[i] = field_ref[nblk - 4 + i]
+
+    def row(b, src, base):
+        loads[b].wait()
         acc = None
         for k in range(KB):
-            start = pl.multiple_of((b + 2 + off_ref[b, k]) * BK, BK)
-            term = jnp.dot(
-                blk_ref[r, k], field_ref[pl.ds(start, BK), :], preferred_element_type=jnp.float32
-            )
+            term = jnp.dot(blk[b, k], src[b + base + off_ref[b, k]], preferred_element_type=jnp.float32)
             acc = term if acc is None else acc + term
-        out_ref[pl.ds(r * BK, BK), :] = acc.astype(out_ref.dtype)
-
-
-def band_local(blocks, offsets, padded):
+        out_ref[b] = acc.astype(out_ref.dtype)
+
+    for b in range(2, nblk - 2):
+        row(b, field_ref, 0)
+
+    @pl.when(has_high)
+    def _():
+        to_low.wait_recv()
+
+    @pl.when(jnp.logical_not(has_high))
+    def _():
+        high[4] = jnp.zeros(field_ref.shape[1:], field_ref.dtype)
+        high[5] = jnp.zeros(field_ref.shape[1:], field_ref.dtype)
+
+    @pl.when(has_low)
+    def _():
+        to_high.wait_recv()
+
+    @pl.when(jnp.logical_not(has_low))
+    def _():
+        low[0] = jnp.zeros(field_ref.shape[1:], field_ref.dtype)
+        low[1] = jnp.zeros(field_ref.shape[1:], field_ref.dtype)
+
+    row(0, low, 2)
+    row(1, low, 2)
+    row(nblk - 2, high, 4 - nblk)
+    row(nblk - 1, high, 4 - nblk)
+
+    @pl.when(has_low)
+    def _():
+        to_low.wait_send()
+
+    @pl.when(has_high)
+    def _():
+        to_high.wait_send()
+
+
+def band_local(blocks, offsets, field, collective_id):
     nblk = blocks.shape[0]
-    rows, width = padded.shape
-    per = 8 if nblk % 8 == 0 else 1
+    rows, width = field.shape
+    n = lax.axis_size("basis")
     return pl.pallas_call(
-        functools.partial(band_kernel, per),
-        out_shape=jax.ShapeDtypeStruct((nblk * BK, width), jnp.bfloat16),
-        grid_spec=pltpu.PrefetchScalarGridSpec(
-            num_scalar_prefetch=1,
-            grid=(nblk // per,),
-            in_specs=[
-                pl.BlockSpec((per, KB, BK, BK), lambda g, off: (g, 0, 0, 0)),
-                pl.BlockSpec((rows, width), lambda g, off: (0, 0)),
-            ],
-            out_specs=pl.BlockSpec((per * BK, width), lambda g, off: (g, 0)),
-        ),
+        functools.partial(band_kernel, n),
+        out_shape=jax.ShapeDtypeStruct((nblk, BK, width), jnp.bfloat16),
+        in_specs=[
+            pl.BlockSpec(memory_space=pltpu.SMEM),
+            pl.BlockSpec(memory_space=pl.ANY),
+            pl.BlockSpec(memory_space=pltpu.VMEM),
+        ],
+        out_specs=pl.BlockSpec(memory_space=pltpu.VMEM),
+        scratch_shapes=[
+            pltpu.VMEM(blocks.shape, blocks.dtype),
+            pltpu.VMEM((6, BK, width), field.dtype),
+            pltpu.VMEM((6, BK, width), field.dtype),
+            pltpu.SemaphoreType.DMA((nblk,)),
+            pltpu.SemaphoreType.DMA((2,)),
+            pltpu.SemaphoreType.DMA((2,)),
+        ],
         cost_estimate=pl.CostEstimate(
             flops=2 * nblk * KB * BK * BK * width,
-            bytes_accessed=blocks.size * 2 + padded.size * 2 + nblk * BK * width * 2,
+            bytes_accessed=blocks.size * 2 + 2 * field.size * 2,
             transcendentals=0,
         ),
-        compiler_params=pltpu.CompilerParams(vmem_limit_bytes=24 * 1024 * 1024),
-    )(offsets, blocks, padded)
+        compiler_params=pltpu.CompilerParams(
+            collective_id=collective_id, has_side_effects=True, vmem_limit_bytes=24 * 1024 * 1024
+        ),
+    )(offsets, blocks, field.reshape(nblk, BK, width)).reshape(rows, width)
 
 
 def _place():
@@ -210,8 +291,7 @@
 def on_device(cont_orbitals, target_orbitals, margin_blocks, dipole_blocks, band_offsets):
     n = lax.axis_size("basis")
     count = band_offsets.shape[0] * BK * n
-    cont_padded = padded_2(cont_orbitals, (("basis", 0),), 2 * BK)
-    margin_cont = band_local(margin_blocks, band_offsets, cont_padded)
+    margin_cont = band_local(margin_blocks, band_offsets, cont_orbitals, 2)
     partial_proj = lax.dot_general(
         target_orbitals, margin_cont, (((0,), (0,)), ((), ())), preferred_element_type=jnp.float32
     )
@@ -219,8 +299,7 @@
     removed = jnp.dot(target_orbitals, projection_b, preferred_element_type=jnp.float32)
     cont_orth = (cont_orbitals.astype(jnp.float32) - removed).astype(jnp.bfloat16)
     squares = jnp.sum(jnp.square(cont_orth.astype(jnp.float32)), axis=0)
-    orth_padded = padded_2(cont_orth, (("basis", 0),), 2 * BK)
-    dipole_cont = band_local(dipole_blocks, band_offsets, orth_padded)
+    dipole_cont = band_local(dipole_blocks, band_offsets, cont_orth, 3)
     partial_dip = lax.dot_general(
         target_orbitals,
         dipole_cont,

time: 81.7 us -> 95.7 us (1.17)
  the two profiles are of different devices: /device:TPU:0 before, /device:TPU:1 now
where the time goes in v6:
time: 95.7 us; the launch traced here: 95.2 us
  Pallas kernels  57.7 us (60%)
  local copies, waits for them, and re-layouts  19.4 us (20%)
  matrix products  17.2 us (18%)
    pallas_call x1, Pallas kernels, allreduce_to_bf16(): pl.pallas_call(functools.partial(allreduce_kernel, nchip), out_shape=jax....  23.2 us
    pallas_call x2, Pallas kernels, band_local(): pl.pallas_call(functools.partial(band_kernel, n), out_shape=jax.ShapeDtyp...  20.3 us
    unnamed x20, local copies, waits for them, and re-layouts  17.4 us
    pallas_call x1, Pallas kernels, dipole_scatter(): pl.pallas_call(functools.partial(dipole_kernel, nchip, chunk, count), out...  14.3 us
    dot_general x1, matrix products, on_device(): jnp.dot(target_orbitals, projection_b, preferred_element_type=jnp.float32)  8.16 us
    dot_general x1, matrix products, on_device(): lax.dot_general(target_orbitals, dipole_cont, (((0,), (0,)), ((), ())), p...  5.74 us
    dot_general x1, matrix products, on_device(): lax.dot_general(target_orbitals, margin_cont, (((0,), (0,)), ((), ())), p...  3.32 us

profile of v6, /device:TPU:1, one launch (start us, length us, event | category | flops | bytes accessed | tf_op | source)
XLA Modules:
  0.0 95.2 jit_solution(14915831559158180540)
XLA Ops:
  0.6 0.8 copy.8.off_ref
  1.4 0.0 copy-start
  1.4 3.4 %copy-done = bf16[16,4,256,256]{3,2,1,0:T(8,128)(2,1)S(1)} copy-done((bf16[16,4,256,256]{3,2,1,0:T(8,128)(2,1)S(1)}, bf16[16,4,256,256]{3,2,1,0:T(8,128)(2,1)}, u32[]{:S(2)}) %copy-start) | copy-done | bytes 8388632
  4.8 0.0 copy-start.2
  4.8 1.6 %copy-done.2 = bf16[4096,256]{1,0:T(8,128)(2,1)S(1)} copy-done((bf16[4096,256]{1,0:T(8,128)(2,1)S(1)}, bf16[4096,256]{1,0:T(8,128)(2,1)}, u32[]{:S(2)}) %copy-start.2) | copy-done | bytes 2097176
  6.4 0.0 copy-start.7
  6.4 11.3 %shard_map.68 = bf16[16,256,256]{2,1,0:T(8,128)(2,1)S(1)} custom-call(s32[16,4]{1,0:T(8,128)S(1)} %copy.8.off_ref, bf16[16,4,256,256]{3,2,1,0:T(8,128)(2,1)S(1)} %copy-done, bf16[16,256,256]{2,1,0:T(8,128)(2,1)S(1)} %bitcast.25), custom_call_target="tpu_custom_call" | custom-call | flops 2147483648 | bytes 12582912 | tf_op jit(solution)/shard_map/pallas_call | solution.py:120
  17.7 0.0 copy-done.7
  17.7 3.3 %convolution_bitcast_fusion.2 = f32[1024,256]{0,1:T(8,128)} fusion(bf16[4096,256]{1,0:T(8,128)(2,1)S(1)} %bitcast.24, bf16[4096,1024]{1,0:T(8,128)(2,1)S(1)} %copy-done.7), kind=kOutput, calls=%fused_computation.5 | convolution fusion | flops 2147483648 | bytes 11534336 | tf_op jit(solution)/shard_map/dot_general | solution.py:295
  21.0 0.0 copy-start.3
  21.0 1.7 %copy.9 = f32[1024,256]{1,0:T(8,128)S(1)} copy(f32[1024,256]{0,1:T(8,128)} %convolution_bitcast_fusion.2) | data formatting | bytes 2097152 | tf_op jit(solution)/shard_map/dot_general | solution.py:295
  22.7 23.2 %shard_map.69 = bf16[8,2,64,256]{3,2,1,0:T(8,128)(2,1)S(1)} custom-call(f32[8,2,64,256]{3,2,1,0:T(8,128)S(1)} %bitcast.27), custom_call_target="tpu_custom_call" | custom-call | bytes 16777216 | tf_op jit(solution)/shard_map/pallas_call | solution.py:240
  45.9 0.0 copy-start.5
  45.9 0.8 copy-done.5
  46.7 0.0 copy-done.3
  46.7 0.0 copy-start.6
  46.7 2.8 %copy.7 = bf16[4096,256]{0,1:T(8,128)(2,1)} copy(bf16[4096,256]{1,0:T(8,128)(2,1)S(1)} %copy-done.3) | data formatting | bytes 4194304 | tf_op args[0]
  49.5 0.0 copy-done.6
  49.5 8.2 %multiply_reduce_fusion = (f32[256]{0:T(256)S(1)}, bf16[4096,256]{0,1:T(8,128)(2,1)}) fusion(bf16[1024,256]{1,0:T(8,128)(2,1)S(1)} %bitcast.28, bf16[4096,1024]{1,0:T(8,128)(2,1)} %param.6, bf16[4096,256]{0,1:T(8,128)(2,1)} %copy.7), kind=kOutput, calls=%fused_computation.3 | convolution fusion | flops 2153774848 | bytes 13108224 | tf_op jit(solution)/shard_map/dot_general | solution.py:299
  57.7 3.3 %copy.13 = bf16[4096,256]{1,0:T(8,128)(2,1)S(1)} copy(bf16[4096,256]{0,1:T(8,128)(2,1)} %get-tuple-element.5) | data formatting | bytes 4194304
  61.0 0.0 copy-start.4
  61.0 0.0 copy-start.1
  61.0 4.1 %copy-done.1 = bf16[16,4,256,256]{3,2,1,0:T(8,128)(2,1)S(1)} copy-done((bf16[16,4,256,256]{3,2,1,0:T(8,128)(2,1)S(1)}, bf16[16,4,256,256]{3,2,1,0:T(8,128)(2,1)}, u32[]{:S(2)}) %copy-start.1) | copy-done | bytes 8388632
  65.1 8.9 %shard_map.70 = bf16[16,256,256]{2,1,0:T(8,128)(2,1)S(1)} custom-call(s32[16,4]{1,0:T(8,128)S(1)} %copy.8.off_ref, bf16[16,4,256,256]{3,2,1,0:T(8,128)(2,1)S(1)} %copy-done.1, bf16[16,256,256]{2,1,0:T(8,128)(2,1)S(1)} %bitcast.26), custom_call_target="tpu_custom_call" | custom-call | flops 2147483648 | bytes 12582912 | tf_op jit(solution)/shard_map/pallas_call | solution.py:120
  74.1 0.0 copy-done.4
  74.1 5.7 %convolution_bitcast_fusion.1 = f32[1024,256]{0,1:T(8,128)S(1)} fusion(bf16[4096,256]{1,0:T(8,128)(2,1)S(1)} %bitcast.23, bf16[4096,1024]{1,0:T(8,128)(2,1)} %param.6), kind=kOutput, calls=%fused_computation.4 | convolution fusion | flops 2147483648 | bytes 11534336 | tf_op jit(solution)/shard_map/dot_general | solution.py:303
  79.8 0.3 copy.12
  80.2 0.1 pad_maximum_fusion.x_ref
  80.3 14.3 %shard_map.71 = bf16[64,256]{1,0:T(8,128)(2,1)S(1)} custom-call(f32[8,2,72,256]{3,2,1,0:T(8,128)S(1)} %pad_maximum_fusion.x_ref), custom_call_target="tpu_custom_call" | custom-call | bytes 9437184 | tf_op jit(solution)/shard_map/pallas_call | solution.py:277
  94.6 0.6 copy.15
  (1 shorter events, 0.0 us)
Async XLA Ops:
  1.4 3.4 %copy-start = (bf16[16,4,256,256]{3,2,1,0:T(8,128)(2,1)S(1)}, bf16[16,4,256,256]{3,2,1,0:T(8,128)(2,1)}, u32[]{:S(2)}) copy-start(bf16[16,4,256,256]{3,2,1,0:T(8,128)(2,1)} %blk_hbm.2) | copy-start | bytes 25165828
  4.8 1.6 %copy-start.2 = (bf16[4096,256]{1,0:T(8,128)(2,1)S(1)}, bf16[4096,256]{1,0:T(8,128)(2,1)}, u32[]{:S(2)}) copy-start(bf16[4096,256]{1,0:T(8,128)(2,1)} %param.5) | copy-start | bytes 6291460
  6.4 11.3 %copy-start.7 = (bf16[4096,1024]{1,0:T(8,128)(2,1)S(1)}, bf16[4096,1024]{1,0:T(8,128)(2,1)}, u32[]{:S(2)}) copy-start(bf16[4096,1024]{1,0:T(8,128)(2,1)} %param.6) | copy-start | bytes 25165828
  21.0 25.7 %copy-start.3 = (bf16[4096,256]{1,0:T(8,128)(2,1)S(1)}, bf16[4096,256]{1,0:T(8,128)(2,1)}, u32[]{:S(2)}) copy-start(bf16[4096,256]{1,0:T(8,128)(2,1)} %param.5) | copy-start | bytes 6291460
  45.9 0.8 copy-start.5
  46.7 2.9 %copy-start.6 = (bf16[8,2,64,256]{3,2,1,0:T(8,128)(2,1)S(1)}, bf16[8,2,64,256]{3,2,1,0:T(8,128)(2,1)}, u32[]{:S(2)}) copy-start(bf16[8,2,64,256]{3,2,1,0:T(8,128)(2,1)} %copy-done.5) | copy-start | bytes 1572868
  61.0 13.1 %copy-start.4 = (bf16[4096,256]{1,0:T(8,128)(2,1)}, bf16[4096,256]{1,0:T(8,128)(2,1)S(1)}, u32[]{:S(2)}) copy-start(bf16[4096,256]{1,0:T(8,128)(2,1)S(1)} %copy.13) | copy-start | bytes 6291460
  61.0 4.1 %copy-start.1 = (bf16[16,4,256,256]{3,2,1,0:T(8,128)(2,1)S(1)}, bf16[16,4,256,256]{3,2,1,0:T(8,128)(2,1)}, u32[]{:S(2)}) copy-start(bf16[16,4,256,256]{3,2,1,0:T(8,128)(2,1)} %blk_hbm.3) | copy-start | bytes 25165828

commit v7 on v5

--- a/solution.py
+++ b/solution.py
@@ -97,20 +97,21 @@
         cp = _remote(x_ref.at[i, 1 - core], pair_recv.at[i], p_send.at[i], p_recv.at[i], partner, orb)
         cp.start()
         pair.append(cp)
+    f32 = jnp.float32
     for i in range(nchip):
         pair[i].wait_recv()
-        part[i] = x_ref[i, core] + pair_recv[i]
+        part[i] = (x_ref[i, core].astype(f32) + pair_recv[i].astype(f32)).astype(part.dtype)
     sends = []
     for j in range(1, nchip):
         dst = lax.rem(chip + j, nchip)
         cp = _remote(part.at[dst], chip_recv.at[chip], c_send.at[j], c_recv.at[chip], 2 * dst + core, orb)
         cp.start()
         sends.append(cp)
-    total = part[chip]
+    total = x_ref[chip, core].astype(f32) + pair_recv[chip].astype(f32)
     for j in range(1, nchip):
         src = lax.rem(chip + nchip - j, nchip)
         _remote(part.at[src], chip_recv.at[src], c_send.at[j], c_recv.at[src], 2 * src + core, orb).wait_recv()
-        total = total + chip_recv[src]
+        total = total + chip_recv[src].astype(f32)
     for cp in pair + sends:
         cp.wait_send()
     return total
@@ -144,18 +145,14 @@
 
 
 def _two_level_scratch(nchip, rows, cols):
-    return [
-        pltpu.VMEM((nchip, rows, cols), jnp.float32),
-        pltpu.VMEM((nchip, rows, cols), jnp.float32),
-        pltpu.VMEM((nchip, rows, cols), jnp.float32),
-    ]
+    return [pltpu.VMEM((nchip, rows, cols), jnp.bfloat16)] * 3
 
 
 def allreduce_to_bf16(partial, n):
     rows, cols = partial.shape
     nchip = n // 2
     chunk = rows // n
-    x = partial.reshape(nchip, 2, chunk, cols)
+    x = partial.astype(jnp.bfloat16).reshape(nchip, 2, chunk, cols)
     out = pl.pallas_call(
         functools.partial(allreduce_kernel, nchip),
         out_shape=jax.ShapeDtypeStruct((nchip, 2, chunk, cols), jnp.bfloat16),
@@ -177,7 +174,7 @@
 def dipole_kernel(nchip, chunk, count, x_ref, out_ref, pair_recv, part, chip_recv,
                   p_send, p_recv, c_send, c_recv):
     total = _two_level_sum(nchip, x_ref, pair_recv, part, chip_recv, p_send, p_recv, c_send, c_recv)
-    squares = total[chunk:chunk + 1, :]
+    squares = total[chunk:chunk + 1, :] + total[chunk + 1:chunk + 2, :]
     col_norm = 1.0 / jnp.sqrt(squares / count + 1e-06)
     out_ref[...] = (total[:chunk, :] * col_norm).astype(out_ref.dtype)
 
@@ -186,10 +183,13 @@
     rows, cols = partial.shape
     nchip = n // 2
     chunk = rows // n
+    high = squares.astype(jnp.bfloat16)
+    low = (squares - high.astype(jnp.float32)).astype(jnp.bfloat16)
+    tail = jnp.concatenate([high[None, :], low[None, :], jnp.zeros((6, cols), jnp.bfloat16)], axis=0)
     x = jnp.concatenate(
         [
-            partial.reshape(nchip, 2, chunk, cols),
-            jnp.broadcast_to(squares[None, None, None, :], (nchip, 2, 8, cols)),
+            partial.astype(jnp.bfloat16).reshape(nchip, 2, chunk, cols),
+            jnp.broadcast_to(tail[None, None], (nchip, 2, 8, cols)),
         ],
         axis=2,
     )

time: 81.7 us -> 74.2 us (0.908)
  the two profiles are of different devices: /device:TPU:0 before, /device:TPU:1 now
where the time goes in v7:
time: 74.2 us; the launch traced here: 73 us
  Pallas kernels  30.8 us (42%)
  starting transfers between devices  11.3 us (15%)
  matrix products  10.8 us (15%)
  waiting for transfers between devices  10.6 us (14%)
  local copies, waits for them, and re-layouts  6.61 us (9%)
  other arithmetic  2.05 us (3%)
  between operations  0.85 us (1%)
    pallas_call x1, Pallas kernels, allreduce_to_bf16(): pl.pallas_call(functools.partial(allreduce_kernel, nchip), out_shape=jax....  17.2 us
    ppermute x2, waiting for transfers between devices, padded_2(): lax.ppermute(lax.slice_in_dim(block, 0, width, axis=dim), axis, backward)  8.79 us
    ppermute x2, starting transfers between devices, padded_2(): lax.ppermute(lax.slice_in_dim(block, block.shape[dim] - width, None, axis...  7.46 us
    pallas_call x1, Pallas kernels, dipole_scatter(): pl.pallas_call(functools.partial(dipole_kernel, nchip, chunk, count), out...  7.14 us
    pallas_call x2, Pallas kernels, band_local(): pl.pallas_call(functools.partial(band_kernel, per), out_shape=jax.ShapeDt...  6.43 us
    dot_general x1, matrix products, on_device(): jnp.dot(target_orbitals, projection_b, preferred_element_type=jnp.float32)  6.06 us
    unnamed x18, local copies, waits for them, and re-layouts  5.01 us
    ppermute x2, starting transfers between devices, padded_2(): lax.ppermute(lax.slice_in_dim(block, 0, width, axis=dim), axis, backward)  3.84 us
  transfers between devices with their start and end apart: 4, of which 4 were waited for; matrix products, arithmetic and copies ran while one was open for 1% of the time, Pallas kernels for 0%

profile of v7, /device:TPU:1, one launch (start us, length us, event | category | flops | bytes accessed | tf_op | source)
XLA Modules:
  0.0 73.0 jit_solution(11912135273762594297)
XLA Ops:
  0.6 1.1 %fusion.5 = (bf16[512,256]{1,0:T(8,128)(2,1)S(1)}, bf16[512,256]{1,0:T(8,128)(2,1)S(1)}) fusion(bf16[4096,256]{1,0:T(8,128)(2,1)} %param.5), kind=kLoop, calls=%fused_computation.14 | loop fusion | bytes 1048576 | tf_op jit(solution)/shard_map/slice | solution.py:21
  1.7 4.9 %collective-permute-start = (bf16[512,256]{1,0:T(8,128)(2,1)S(1)}, bf16[512,256]{1,0:T(8,128)(2,1)S(1)}, u32[]{:S(2)}, u32[]{:S(2)}) collective-permute-start(bf16[512,256]{1,0:T(8,128)(2,1)S(1)} %get-tuple-element.4), channel_id=1, source_target_pairs={{0,8},{8,16},{16,24},{24,32},{32,40},{40,48},{48,56},{56,64},{64,7... | collective-permute-start | bytes 786440 | tf_op jit(solution)/shard_map/ppermute | solution.py:20
  6.6 1.9 %collective-permute-start.1 = (bf16[512,256]{1,0:T(8,128)(2,1)S(1)}, bf16[512,256]{1,0:T(8,128)(2,1)S(1)}, u32[]{:S(2)}, u32[]{:S(2)}) collective-permute-start(bf16[512,256]{1,0:T(8,128)(2,1)S(1)} %get-tuple-element.5), channel_id=1, source_target_pairs={{8,0},{16,8},{24,16},{32,24},{40,32},{48,40},{56,48},{64,56},{72,6... | collective-permute-start | bytes 786440 | tf_op jit(solution)/shard_map/ppermute | solution.py:23
  8.6 0.8 %copy.7.off_ref = s32[16,4]{1,0:T(8,128)S(1)} copy(s32[16,4]{0,1:T(4,128)} %param.9) | data formatting | bytes 512 | tf_op args[4]
  9.3 0.1 pad.4.clone
  9.4 0.5 collective-permute-done
  9.9 4.4 %collective-permute-done.1 = bf16[512,256]{1,0:T(8,128)(2,1)S(1)} collective-permute-done((bf16[512,256]{1,0:T(8,128)(2,1)S(1)}, bf16[512,256]{1,0:T(8,128)(2,1)S(1)}, u32[]{:S(2)}, u32[]{:S(2)}) %collective-permute-start.1) | collective-permute-done | bytes 262176 | tf_op jit(solution)/shard_map/ppermute | solution.py:23
  14.3 1.8 %pad_maximum_fusion.field_ref = bf16[5120,256]{1,0:T(8,128)(2,1)S(1)} fusion(bf16[512,256]{1,0:T(8,128)(2,1)S(1)} %collective-permute-done.1, bf16[4096,256]{1,0:T(8,128)(2,1)} %param.5, bf16[512,256]{1,0:T(8,128)(2,1)S(1)} %collective-permute-done), kind=kLoop, calls=%fused_computation.4 | loop fusion | flops 7864320 | bytes 5242880 | tf_op jit(solution)/shard_map/concatenate | solution.py:24
  16.1 0.0 copy-start
  16.1 3.4 %copy-done = bf16[16,4,256,256]{3,2,1,0:T(8,128)(2,1)S(1)} copy-done((bf16[16,4,256,256]{3,2,1,0:T(8,128)(2,1)S(1)}, bf16[16,4,256,256]{3,2,1,0:T(8,128)(2,1)}, u32[]{:S(2)}) %copy-start) | copy-done | bytes 8388632
  19.5 0.0 copy-start.1
  19.5 3.2 %shard_map.68 = bf16[4096,256]{1,0:T(8,128)(2,1)S(1)} custom-call(s32[16,4]{1,0:T(8,128)S(1)} %copy.7.off_ref, bf16[16,4,256,256]{3,2,1,0:T(8,128)(2,1)S(1)} %copy-done, bf16[5120,256]{1,0:T(8,128)(2,1)S(1)} %pad_maximum_fusion.field_ref), custom_call_target="tpu_custom_call" | custom-call | flops 2147483648 | bytes 13107200 | tf_op jit(solution)/shard_map/pallas_call | solution.py:46
  22.7 0.2 copy-done.1
  22.9 0.0 copy-start.2
  22.9 2.4 %fusion.2 = bf16[1024,256]{0,1:T(8,128)(2,1)S(1)} fusion(bf16[4096,256]{1,0:T(8,128)(2,1)S(1)} %shard_map.68, bf16[4096,1024]{1,0:T(8,128)(2,1)S(1)} %copy-done.1), kind=kOutput, calls=%fused_computation.8 | convolution fusion | flops 2147745792 | bytes 11010048 | tf_op jit(solution)/shard_map/dot_general | solution.py:215
  25.3 0.2 copy.8
  25.5 0.0 slice-start
  25.5 17.2 %shard_map.69 = bf16[8,2,64,256]{3,2,1,0:T(8,128)(2,1)S(1)} custom-call(bf16[8,2,64,256]{3,2,1,0:T(8,128)(2,1)S(1)} %bitcast.22), custom_call_target="tpu_custom_call" | custom-call | bytes 16777216 | tf_op jit(solution)/shard_map/pallas_call | solution.py:156
  42.7 0.0 copy-done.2
  42.7 0.0 slice-start.1
  42.7 6.1 %multiply_reduce_fusion = (f32[256]{0:T(256)S(1)}, bf16[4096,256]{1,0:T(8,128)(2,1)S(1)}) fusion(bf16[4096,1024]{1,0:T(8,128)(2,1)} %param.6, bf16[1024,256]{1,0:T(8,128)(2,1)S(1)} %bitcast.23, bf16[4096,256]{1,0:T(8,128)(2,1)S(1)} %copy-done.2), kind=kOutput, calls=%fused_computation.3 | convolution fusion | flops 2153774848 | bytes 13108224 | tf_op jit(solution)/shard_map/dot_general | solution.py:219
  48.8 0.0 copy-start.3
  48.9 2.5 %collective-permute-start.2 = (bf16[512,256]{1,0:T(8,128)(2,1)S(1)}, bf16[512,256]{1,0:T(8,128)(2,1)S(1)}, u32[]{:S(2)}, u32[]{:S(2)}) collective-permute-start(bf16[512,256]{1,0:T(8,128)(2,1)S(1)} %get-tuple-element.2), channel_id=1, source_target_pairs={{0,8},{8,16},{16,24},{24,32},{32,40},{40,48},{48,56},{56,64},{64,7... | collective-permute-start | bytes 786440 | tf_op jit(solution)/shard_map/ppermute | solution.py:20
  51.4 1.9 %collective-permute-start.3 = (bf16[512,256]{1,0:T(8,128)(2,1)S(1)}, bf16[512,256]{1,0:T(8,128)(2,1)S(1)}, u32[]{:S(2)}, u32[]{:S(2)}) collective-permute-start(bf16[512,256]{1,0:T(8,128)(2,1)S(1)} %get-tuple-element.3), channel_id=1, source_target_pairs={{8,0},{16,8},{24,16},{32,24},{40,32},{48,40},{56,48},{64,56},{72,6... | collective-permute-start | bytes 786440 | tf_op jit(solution)/shard_map/ppermute | solution.py:23
  53.3 0.1 maximum_maximum_fusion
  53.4 1.3 %collective-permute-done.2 = bf16[512,256]{1,0:T(8,128)(2,1)S(1)} collective-permute-done((bf16[512,256]{1,0:T(8,128)(2,1)S(1)}, bf16[512,256]{1,0:T(8,128)(2,1)S(1)}, u32[]{:S(2)}, u32[]{:S(2)}) %collective-permute-start.2) | collective-permute-done | bytes 262176 | tf_op jit(solution)/shard_map/ppermute | solution.py:20
  54.7 4.4 %collective-permute-done.3 = bf16[512,256]{1,0:T(8,128)(2,1)S(1)} collective-permute-done((bf16[512,256]{1,0:T(8,128)(2,1)S(1)}, bf16[512,256]{1,0:T(8,128)(2,1)S(1)}, u32[]{:S(2)}, u32[]{:S(2)}) %collective-permute-start.3) | collective-permute-done | bytes 262176 | tf_op jit(solution)/shard_map/ppermute | solution.py:23
  59.1 0.0 copy-done.3
  59.1 0.0 slice-start.2
  59.1 0.2 pad_maximum_fusion.1.field_ref
  59.3 0.0 slice-done
  59.3 0.0 slice-done.1
  59.3 0.0 slice-start.3
  59.3 3.2 %shard_map.70 = bf16[4096,256]{1,0:T(8,128)(2,1)S(1)} custom-call(s32[16,4]{1,0:T(8,128)S(1)} %copy.7.off_ref, bf16[16,4,256,256]{3,2,1,0:T(8,128)(2,1)S(1)} %bitcast.21, bf16[5120,256]{1,0:T(8,128)(2,1)S(1)} %pad_maximum_fusion.1.field_ref), custom_call_target="tpu_custom_call" | custom-call | flops 2147483648 | bytes 13107200 | tf_op jit(solution)/shard_map/pallas_call | solution.py:46
  62.5 0.0 slice-done.2
  62.5 0.1 slice-done.3
  62.6 2.4 %fusion.3 = bf16[1024,256]{0,1:T(8,128)(2,1)S(1)} fusion(bf16[4096,256]{1,0:T(8,128)(2,1)S(1)} %shard_map.70, bf16[4096,1024]{1,0:T(8,128)(2,1)S(1)} %bitcast.25), kind=kOutput, calls=%fused_computation.9 | convolution fusion | flops 2147745792 | bytes 11010048 | tf_op jit(solution)/shard_map/dot_general | solution.py:224
  65.0 0.2 copy.11
  65.3 7.1 %shard_map.71 = bf16[64,256]{1,0:T(8,128)(2,1)S(1)} custom-call(bf16[8,2,72,256]{3,2,1,0:T(8,128)(2,1)S(1)} %pad_maximum_fusion.2.x_ref), custom_call_target="tpu_custom_call" | custom-call | bytes 9437184 | tf_op jit(solution)/shard_map/pallas_call | solution.py:196
  72.4 0.6 copy.14
  (8 shorter events, 0.1 us)
Async XLA Ops:
  1.7 8.2 %collective-permute-start = (bf16[512,256]{1,0:T(8,128)(2,1)S(1)}, bf16[512,256]{1,0:T(8,128)(2,1)S(1)}, u32[]{:S(2)}, u32[]{:S(2)}) collective-permute-start(bf16[512,256]{1,0:T(8,128)(2,1)S(1)} %get-tuple-element.4), channel_id=1, source_target_pairs={{0,8},{8,16},{16,24},{24,32},{32,40},{40,48},{48,56},{56,64},{64,7... | collective-permute-start | bytes 786440 | tf_op jit(solution)/shard_map/ppermute | solution.py:20
  6.6 7.7 %collective-permute-start.1 = (bf16[512,256]{1,0:T(8,128)(2,1)S(1)}, bf16[512,256]{1,0:T(8,128)(2,1)S(1)}, u32[]{:S(2)}, u32[]{:S(2)}) collective-permute-start(bf16[512,256]{1,0:T(8,128)(2,1)S(1)} %get-tuple-element.5), channel_id=1, source_target_pairs={{8,0},{16,8},{24,16},{32,24},{40,32},{48,40},{56,48},{64,56},{72,6... | collective-permute-start | bytes 786440 | tf_op jit(solution)/shard_map/ppermute | solution.py:23
  16.1 3.4 %copy-start = (bf16[16,4,256,256]{3,2,1,0:T(8,128)(2,1)S(1)}, bf16[16,4,256,256]{3,2,1,0:T(8,128)(2,1)}, u32[]{:S(2)}) copy-start(bf16[16,4,256,256]{3,2,1,0:T(8,128)(2,1)} %blk_ref.2) | copy-start | bytes 25165828
  19.5 3.4 %copy-start.1 = (bf16[4096,1024]{1,0:T(8,128)(2,1)S(1)}, bf16[4096,1024]{1,0:T(8,128)(2,1)}, u32[]{:S(2)}) copy-start(bf16[4096,1024]{1,0:T(8,128)(2,1)} %param.6) | copy-start | bytes 25165828
  22.9 19.9 %copy-start.2 = (bf16[4096,256]{1,0:T(8,128)(2,1)S(1)}, bf16[4096,256]{1,0:T(8,128)(2,1)}, u32[]{:S(2)}) copy-start(bf16[4096,256]{1,0:T(8,128)(2,1)} %param.5) | copy-start | bytes 6291460
  25.5 33.8 %slice-start = ((s8[8388608]{0:T(1024)(128)(4,1)}), s8[4194304]{0:T(1024)(128)(4,1)S(1)}, s32[]{:S(2)}) async-start(s8[8388608]{0:T(1024)(128)(4,1)} %bitcast.20), calls=%async_computation | async-start | bytes 8388608
  42.7 16.6 %slice-start.1 = ((s8[8388608]{0:T(1024)(128)(4,1)}), s8[4194304]{0:T(1024)(128)(4,1)S(1)}, s32[]{:S(2)}) async-start(s8[8388608]{0:T(1024)(128)(4,1)} %bitcast.20), calls=%async_computation.1 | async-start | bytes 8388608
  48.8 10.3 %copy-start.3 = (bf16[4096,256]{1,0:T(8,128)(2,1)}, bf16[4096,256]{1,0:T(8,128)(2,1)S(1)}, u32[]{:S(2)}) copy-start(bf16[4096,256]{1,0:T(8,128)(2,1)S(1)} %get-tuple-element.10) | copy-start | bytes 6291460
  48.9 5.8 %collective-permute-start.2 = (bf16[512,256]{1,0:T(8,128)(2,1)S(1)}, bf16[512,256]{1,0:T(8,128)(2,1)S(1)}, u32[]{:S(2)}, u32[]{:S(2)}) collective-permute-start(bf16[512,256]{1,0:T(8,128)(2,1)S(1)} %get-tuple-element.2), channel_id=1, source_target_pairs={{0,8},{8,16},{16,24},{24,32},{32,40},{40,48},{48,56},{56,64},{64,7... | collective-permute-start | bytes 786440 | tf_op jit(solution)/shard_map/ppermute | solution.py:20
  51.4 7.7 %collective-permute-start.3 = (bf16[512,256]{1,0:T(8,128)(2,1)S(1)}, bf16[512,256]{1,0:T(8,128)(2,1)S(1)}, u32[]{:S(2)}, u32[]{:S(2)}) collective-permute-start(bf16[512,256]{1,0:T(8,128)(2,1)S(1)} %get-tuple-element.3), channel_id=1, source_target_pairs={{8,0},{16,8},{24,16},{32,24},{40,32},{48,40},{56,48},{64,56},{72,6... | collective-permute-start | bytes 786440 | tf_op jit(solution)/shard_map/ppermute | solution.py:23
  59.1 3.4 %slice-start.2 = ((s8[8388608]{0:T(1024)(128)(4,1)}), s8[4194304]{0:T(1024)(128)(4,1)S(1)}, s32[]{:S(2)}) async-start(s8[8388608]{0:T(1024)(128)(4,1)} %bitcast.24), calls=%async_computation.2 | async-start | bytes 8388608
  59.3 3.3 %slice-start.3 = ((s8[8388608]{0:T(1024)(128)(4,1)}), s8[4194304]{0:T(1024)(128)(4,1)S(1)}, s32[]{:S(2)}) async-start(s8[8388608]{0:T(1024)(128)(4,1)} %bitcast.24), calls=%async_computation.3 | async-start | bytes 8388608

commit v8 on v5

--- a/solution.py
+++ b/solution.py
@@ -62,6 +62,52 @@
         ),
         compiler_params=pltpu.CompilerParams(vmem_limit_bytes=24 * 1024 * 1024),
     )(offsets, blocks, padded)
+
+
+def orth_kernel(tgt_ref, proj_ref, cont_ref, orth_ref, sq_ref):
+    removed = jnp.dot(tgt_ref[...], proj_ref[...], preferred_element_type=jnp.float32)
+    orth = (cont_ref[...].astype(jnp.float32) - removed).astype(orth_ref.dtype)
+    orth_ref[...] = orth
+    wide = orth.astype(jnp.float32)
+    part = jnp.sum(wide * wide, axis=0, keepdims=True)
+
+    @pl.when(pl.program_id(0) == 0)
+    def _():
+        sq_ref[...] = part
+
+    @pl.when(pl.program_id(0) > 0)
+    def _():
+        sq_ref[...] += part
+
+
+def orthogonalize(target, projection_b, cont):
+    rows, nt = target.shape
+    width = cont.shape[1]
+    tile = 512 if rows % 512 == 0 else rows
+    orth, squares = pl.pallas_call(
+        orth_kernel,
+        out_shape=(
+            jax.ShapeDtypeStruct((rows, width), jnp.bfloat16),
+            jax.ShapeDtypeStruct((1, width), jnp.float32),
+        ),
+        grid=(rows // tile,),
+        in_specs=[
+            pl.BlockSpec((tile, nt), lambda i: (i, 0)),
+            pl.BlockSpec((nt, width), lambda i: (0, 0)),
+            pl.BlockSpec((tile, width), lambda i: (i, 0)),
+        ],
+        out_specs=(
+            pl.BlockSpec((tile, width), lambda i: (i, 0)),
+            pl.BlockSpec((1, width), lambda i: (0, 0)),
+        ),
+        cost_estimate=pl.CostEstimate(
+            flops=2 * rows * nt * width,
+            bytes_accessed=target.size * 2 + projection_b.size * 2 + 2 * cont.size * 2,
+            transcendentals=0,
+        ),
+        compiler_params=pltpu.CompilerParams(vmem_limit_bytes=16 * 1024 * 1024),
+    )(target, projection_b, cont)
+    return orth, squares[0]
 
 
 def _place():
@@ -216,9 +262,7 @@
         target_orbitals, margin_cont, (((0,), (0,)), ((), ())), preferred_element_type=jnp.float32
     )
     projection_b = allreduce_to_bf16(partial_proj, n)
-    removed = jnp.dot(target_orbitals, projection_b, preferred_element_type=jnp.float32)
-    cont_orth = (cont_orbitals.astype(jnp.float32) - removed).astype(jnp.bfloat16)
-    squares = jnp.sum(jnp.square(cont_orth.astype(jnp.float32)), axis=0)
+    cont_orth, squares = orthogonalize(target_orbitals, projection_b, cont_orbitals)
     orth_padded = padded_2(cont_orth, (("basis", 0),), 2 * BK)
     dipole_cont = band_local(dipole_blocks, band_offsets, orth_padded)
     partial_dip = lax.dot_general(

time: 81.7 us -> 92 us (1.13)
  the two profiles are of different devices: /device:TPU:0 before, /device:TPU:1 now
where the time goes in v8:
time: 92 us; the launch traced here: 90.3 us
  Pallas kernels  42.1 us (46%)
  local copies, waits for them, and re-layouts  15.7 us (17%)
  starting transfers between devices  11.3 us (12%)
  waiting for transfers between devices  10.8 us (12%)
  matrix products  5.72 us (6%)
  other arithmetic  3.9 us (4%)
    pallas_call x1, Pallas kernels, allreduce_to_bf16(): pl.pallas_call(functools.partial(allreduce_kernel, nchip), out_shape=jax....  19.8 us
    unnamed x18, local copies, waits for them, and re-layouts  11.5 us
    pallas_call x1, Pallas kernels, dipole_scatter(): pl.pallas_call(functools.partial(dipole_kernel, nchip, chunk, count), out...  10.7 us
    ppermute x2, waiting for transfers between devices, padded_2(): lax.ppermute(lax.slice_in_dim(block, 0, width, axis=dim), axis, backward)  8.79 us
    ppermute x2, starting transfers between devices, padded_2(): lax.ppermute(lax.slice_in_dim(block, block.shape[dim] - width, None, axis...  7.46 us
    pallas_call x2, Pallas kernels, band_local(): pl.pallas_call(functools.partial(band_kernel, per), out_shape=jax.ShapeDt...  6.44 us
    pallas_call x1, Pallas kernels, orthogonalize(): pl.pallas_call(orth_kernel, out_shape=(jax.ShapeDtypeStruct((rows, width)...  5.1 us
    ppermute x2, starting transfers between devices, padded_2(): lax.ppermute(lax.slice_in_dim(block, 0, width, axis=dim), axis, backward)  3.84 us
  transfers between devices with their start and end apart: 4, of which 4 were waited for; matrix products, arithmetic and copies ran while one was open for 1% of the time, Pallas kernels for 0%

profile of v8, /device:TPU:1, one launch (start us, length us, event | category | flops | bytes accessed | tf_op | source)
XLA Modules:
  0.0 90.3 jit_solution(11050939853613003605)
XLA Ops:
  0.6 1.1 %fusion.1 = (bf16[512,256]{1,0:T(8,128)(2,1)S(1)}, bf16[512,256]{1,0:T(8,128)(2,1)S(1)}) fusion(bf16[4096,256]{1,0:T(8,128)(2,1)} %cont_ref.1), kind=kLoop, calls=%fused_computation.6 | loop fusion | bytes 1048576 | tf_op jit(solution)/shard_map/slice | solution.py:21
  1.7 4.9 %collective-permute-start = (bf16[512,256]{1,0:T(8,128)(2,1)S(1)}, bf16[512,256]{1,0:T(8,128)(2,1)S(1)}, u32[]{:S(2)}, u32[]{:S(2)}) collective-permute-start(bf16[512,256]{1,0:T(8,128)(2,1)S(1)} %get-tuple-element.8), channel_id=1, source_target_pairs={{0,8},{8,16},{16,24},{24,32},{32,40},{40,48},{48,56},{56,64},{64,7... | collective-permute-start | bytes 786440 | tf_op jit(solution)/shard_map/ppermute | solution.py:20
  6.6 1.9 %collective-permute-start.1 = (bf16[512,256]{1,0:T(8,128)(2,1)S(1)}, bf16[512,256]{1,0:T(8,128)(2,1)S(1)}, u32[]{:S(2)}, u32[]{:S(2)}) collective-permute-start(bf16[512,256]{1,0:T(8,128)(2,1)S(1)} %get-tuple-element.9), channel_id=1, source_target_pairs={{8,0},{16,8},{24,16},{32,24},{40,32},{48,40},{56,48},{64,56},{72,6... | collective-permute-start | bytes 786440 | tf_op jit(solution)/shard_map/ppermute | solution.py:23
  8.6 0.8 copy.7.off_ref
  9.3 0.6 collective-permute-done
  9.9 4.4 %collective-permute-done.1 = bf16[512,256]{1,0:T(8,128)(2,1)S(1)} collective-permute-done((bf16[512,256]{1,0:T(8,128)(2,1)S(1)}, bf16[512,256]{1,0:T(8,128)(2,1)S(1)}, u32[]{:S(2)}, u32[]{:S(2)}) %collective-permute-start.1) | collective-permute-done | bytes 262176 | tf_op jit(solution)/shard_map/ppermute | solution.py:23
  14.3 0.0 slice-start
  14.3 1.9 %pad_maximum_fusion.field_ref = bf16[5120,256]{1,0:T(8,128)(2,1)S(1)} fusion(bf16[512,256]{1,0:T(8,128)(2,1)S(1)} %collective-permute-done.1, bf16[4096,256]{1,0:T(8,128)(2,1)} %cont_ref.1, bf16[512,256]{1,0:T(8,128)(2,1)S(1)} %collective-permute-done), kind=kLoop, calls=%fused_computation | loop fusion | flops 7864320 | bytes 5242880 | tf_op jit(solution)/shard_map/concatenate | solution.py:24
  16.3 0.0 copy-start.2
  16.3 3.4 %copy-done.2 = bf16[16,4,256,256]{3,2,1,0:T(8,128)(2,1)S(1)} copy-done((bf16[16,4,256,256]{3,2,1,0:T(8,128)(2,1)S(1)}, bf16[16,4,256,256]{3,2,1,0:T(8,128)(2,1)}, u32[]{:S(2)}) %copy-start.2) | copy-done | bytes 8388632
  19.6 0.0 slice-start.1
  19.6 3.2 %shard_map.68 = bf16[4096,256]{1,0:T(8,128)(2,1)S(1)} custom-call(s32[16,4]{1,0:T(8,128)S(1)} %copy.7.off_ref, bf16[16,4,256,256]{3,2,1,0:T(8,128)(2,1)S(1)} %copy-done.2, bf16[5120,256]{1,0:T(8,128)(2,1)S(1)} %pad_maximum_fusion.field_ref), custom_call_target="tpu_custom_call" | custom-call | flops 2147483648 | bytes 13107200 | tf_op jit(solution)/shard_map/pallas_call | solution.py:46
  22.9 0.0 slice-done
  22.9 0.0 slice-done.1
  22.9 3.3 %convolution_bitcast_fusion.1 = f32[1024,256]{0,1:T(8,128)} fusion(bf16[4096,256]{1,0:T(8,128)(2,1)S(1)} %shard_map.68, bf16[4096,1024]{1,0:T(8,128)(2,1)S(1)} %bitcast.13), kind=kOutput, calls=%fused_computation.3 | convolution fusion | flops 2147483648 | bytes 11534336 | tf_op jit(solution)/shard_map/dot_general | solution.py:261
  26.2 0.0 copy-start.1
  26.2 1.7 %copy.8 = f32[1024,256]{1,0:T(8,128)S(1)} copy(f32[1024,256]{0,1:T(8,128)} %convolution_bitcast_fusion.1) | data formatting | bytes 2097152 | tf_op jit(solution)/shard_map/dot_general | solution.py:261
  27.9 19.8 %shard_map.69 = bf16[8,2,64,256]{3,2,1,0:T(8,128)(2,1)S(1)} custom-call(f32[8,2,64,256]{3,2,1,0:T(8,128)S(1)} %bitcast.16), custom_call_target="tpu_custom_call" | custom-call | bytes 16777216 | tf_op jit(solution)/shard_map/pallas_call | solution.py:205
  47.8 0.0 copy-done.1
  47.8 0.0 copy-start
  47.8 3.4 %copy-done = bf16[4096,1024]{1,0:T(8,128)(2,1)S(1)} copy-done((bf16[4096,1024]{1,0:T(8,128)(2,1)S(1)}, bf16[4096,1024]{1,0:T(8,128)(2,1)}, u32[]{:S(2)}) %copy-start) | copy-done | bytes 8388632
  51.2 5.1 %shard_map.70 = (bf16[4096,256]{1,0:T(8,128)(2,1)}, f32[1,256]{1,0:T(1,128)S(1)}) custom-call(bf16[4096,1024]{1,0:T(8,128)(2,1)S(1)} %copy-done, bf16[1024,256]{1,0:T(8,128)(2,1)S(1)} %bitcast.17, bf16[4096,256]{1,0:T(8,128)(2,1)S(1)} %copy-done.1), custom_call_target="tpu_custom_call" | custom-call | flops 2147483648 | bytes 13107200 | tf_op jit(solution)/shard_map/pallas_call | solution.py:87
  56.3 1.1 %fusion = (bf16[512,256]{1,0:T(8,128)(2,1)S(1)}, bf16[512,256]{1,0:T(8,128)(2,1)S(1)}) fusion(bf16[4096,256]{1,0:T(8,128)(2,1)} %get-tuple-element.12), kind=kLoop, calls=%fused_computation.5 | loop fusion | bytes 1048576 | tf_op jit(solution)/shard_map/slice | solution.py:21
  57.4 2.5 %collective-permute-start.2 = (bf16[512,256]{1,0:T(8,128)(2,1)S(1)}, bf16[512,256]{1,0:T(8,128)(2,1)S(1)}, u32[]{:S(2)}, u32[]{:S(2)}) collective-permute-start(bf16[512,256]{1,0:T(8,128)(2,1)S(1)} %get-tuple-element.6), channel_id=1, source_target_pairs={{0,8},{8,16},{16,24},{24,32},{32,40},{40,48},{48,56},{56,64},{64,7... | collective-permute-start | bytes 786440 | tf_op jit(solution)/shard_map/ppermute | solution.py:20
  59.9 1.9 %collective-permute-start.3 = (bf16[512,256]{1,0:T(8,128)(2,1)S(1)}, bf16[512,256]{1,0:T(8,128)(2,1)S(1)}, u32[]{:S(2)}, u32[]{:S(2)}) collective-permute-start(bf16[512,256]{1,0:T(8,128)(2,1)S(1)} %get-tuple-element.7), channel_id=1, source_target_pairs={{8,0},{16,8},{24,16},{32,24},{40,32},{48,40},{56,48},{64,56},{72,6... | collective-permute-start | bytes 786440 | tf_op jit(solution)/shard_map/ppermute | solution.py:23
  61.8 1.4 %collective-permute-done.2 = bf16[512,256]{1,0:T(8,128)(2,1)S(1)} collective-permute-done((bf16[512,256]{1,0:T(8,128)(2,1)S(1)}, bf16[512,256]{1,0:T(8,128)(2,1)S(1)}, u32[]{:S(2)}, u32[]{:S(2)}) %collective-permute-start.2) | collective-permute-done | bytes 262176 | tf_op jit(solution)/shard_map/ppermute | solution.py:20
  63.2 4.4 %collective-permute-done.3 = bf16[512,256]{1,0:T(8,128)(2,1)S(1)} collective-permute-done((bf16[512,256]{1,0:T(8,128)(2,1)S(1)}, bf16[512,256]{1,0:T(8,128)(2,1)S(1)}, u32[]{:S(2)}, u32[]{:S(2)}) %collective-permute-start.3) | collective-permute-done | bytes 262176 | tf_op jit(solution)/shard_map/ppermute | solution.py:23
  67.6 0.0 slice-start.2
  67.6 1.9 %pad_maximum_fusion.1.field_ref = bf16[5120,256]{1,0:T(8,128)(2,1)S(1)} fusion(bf16[512,256]{1,0:T(8,128)(2,1)S(1)} %collective-permute-done.3, bf16[4096,256]{1,0:T(8,128)(2,1)} %get-tuple-element.12, bf16[512,256]{1,0:T(8,128)(2,1)S(1)} %collective-permute-done.2), kind=kLoop, calls=%fused_computation.1 | loop fusion | flops 7864320 | bytes 5242880 | tf_op jit(solution)/shard_map/concatenate | solution.py:24
  69.5 0.0 copy-start.3
  69.5 3.4 %copy-done.3 = bf16[16,4,256,256]{3,2,1,0:T(8,128)(2,1)S(1)} copy-done((bf16[16,4,256,256]{3,2,1,0:T(8,128)(2,1)S(1)}, bf16[16,4,256,256]{3,2,1,0:T(8,128)(2,1)}, u32[]{:S(2)}) %copy-start.3) | copy-done | bytes 8388632
  72.9 0.0 slice-start.3
  72.9 3.2 %shard_map.71 = bf16[4096,256]{1,0:T(8,128)(2,1)S(1)} custom-call(s32[16,4]{1,0:T(8,128)S(1)} %copy.7.off_ref, bf16[16,4,256,256]{3,2,1,0:T(8,128)(2,1)S(1)} %copy-done.3, bf16[5120,256]{1,0:T(8,128)(2,1)S(1)} %pad_maximum_fusion.1.field_ref), custom_call_target="tpu_custom_call" | custom-call | flops 2147483648 | bytes 13107200 | tf_op jit(solution)/shard_map/pallas_call | solution.py:46
  76.1 0.0 slice-done.2
  76.1 0.0 slice-done.3
  76.2 2.4 %convolution_bitcast_fusion = f32[1024,256]{0,1:T(8,128)S(1)} fusion(bf16[4096,256]{1,0:T(8,128)(2,1)S(1)} %shard_map.71, bf16[4096,1024]{1,0:T(8,128)(2,1)S(1)} %bitcast.15), kind=kOutput, calls=%fused_computation.2 | convolution fusion | flops 2147483648 | bytes 11534336 | tf_op jit(solution)/shard_map/dot_general | solution.py:268
  78.5 0.3 copy.10
  78.9 0.1 pad_maximum_fusion.2.x_ref
  79.0 10.7 %shard_map.72 = bf16[64,256]{1,0:T(8,128)(2,1)S(1)} custom-call(f32[8,2,72,256]{3,2,1,0:T(8,128)S(1)} %pad_maximum_fusion.2.x_ref), custom_call_target="tpu_custom_call" | custom-call | bytes 9437184 | tf_op jit(solution)/shard_map/pallas_call | solution.py:242
  89.6 0.6 copy.12
  (3 shorter events, 0.0 us)
Async XLA Ops:
  1.7 8.2 %collective-permute-start = (bf16[512,256]{1,0:T(8,128)(2,1)S(1)}, bf16[512,256]{1,0:T(8,128)(2,1)S(1)}, u32[]{:S(2)}, u32[]{:S(2)}) collective-permute-start(bf16[512,256]{1,0:T(8,128)(2,1)S(1)} %get-tuple-element.8), channel_id=1, source_target_pairs={{0,8},{8,16},{16,24},{24,32},{32,40},{40,48},{48,56},{56,64},{64,7... | collective-permute-start | bytes 786440 | tf_op jit(solution)/shard_map/ppermute | solution.py:20
  6.6 7.7 %collective-permute-start.1 = (bf16[512,256]{1,0:T(8,128)(2,1)S(1)}, bf16[512,256]{1,0:T(8,128)(2,1)S(1)}, u32[]{:S(2)}, u32[]{:S(2)}) collective-permute-start(bf16[512,256]{1,0:T(8,128)(2,1)S(1)} %get-tuple-element.9), channel_id=1, source_target_pairs={{8,0},{16,8},{24,16},{32,24},{40,32},{48,40},{56,48},{64,56},{72,6... | collective-permute-start | bytes 786440 | tf_op jit(solution)/shard_map/ppermute | solution.py:23
  14.3 8.5 %slice-start = ((s8[8388608]{0:T(1024)(128)(4,1)}), s8[4194304]{0:T(1024)(128)(4,1)S(1)}, s32[]{:S(2)}) async-start(s8[8388608]{0:T(1024)(128)(4,1)} %bitcast.12), calls=%async_computation | async-start | bytes 8388608
  16.3 3.4 %copy-start.2 = (bf16[16,4,256,256]{3,2,1,0:T(8,128)(2,1)S(1)}, bf16[16,4,256,256]{3,2,1,0:T(8,128)(2,1)}, u32[]{:S(2)}) copy-start(bf16[16,4,256,256]{3,2,1,0:T(8,128)(2,1)} %blk_ref.2) | copy-start | bytes 25165828
  19.6 3.2 %slice-start.1 = ((s8[8388608]{0:T(1024)(128)(4,1)}), s8[4194304]{0:T(1024)(128)(4,1)S(1)}, s32[]{:S(2)}) async-start(s8[8388608]{0:T(1024)(128)(4,1)} %bitcast.12), calls=%async_computation.1 | async-start | bytes 8388608
  26.2 21.6 %copy-start.1 = (bf16[4096,256]{1,0:T(8,128)(2,1)S(1)}, bf16[4096,256]{1,0:T(8,128)(2,1)}, u32[]{:S(2)}) copy-start(bf16[4096,256]{1,0:T(8,128)(2,1)} %cont_ref.1) | copy-start | bytes 6291460
  47.8 3.4 %copy-start = (bf16[4096,1024]{1,0:T(8,128)(2,1)S(1)}, bf16[4096,1024]{1,0:T(8,128)(2,1)}, u32[]{:S(2)}) copy-start(bf16[4096,1024]{1,0:T(8,128)(2,1)} %tgt_ref.1) | copy-start | bytes 25165828
  57.4 5.8 %collective-permute-start.2 = (bf16[512,256]{1,0:T(8,128)(2,1)S(1)}, bf16[512,256]{1,0:T(8,128)(2,1)S(1)}, u32[]{:S(2)}, u32[]{:S(2)}) collective-permute-start(bf16[512,256]{1,0:T(8,128)(2,1)S(1)} %get-tuple-element.6), channel_id=1, source_target_pairs={{0,8},{8,16},{16,24},{24,32},{32,40},{40,48},{48,56},{56,64},{64,7... | collective-permute-start | bytes 786440 | tf_op jit(solution)/shard_map/ppermute | solution.py:20
  59.9 7.7 %collective-permute-start.3 = (bf16[512,256]{1,0:T(8,128)(2,1)S(1)}, bf16[512,256]{1,0:T(8,128)(2,1)S(1)}, u32[]{:S(2)}, u32[]{:S(2)}) collective-permute-start(bf16[512,256]{1,0:T(8,128)(2,1)S(1)} %get-tuple-element.7), channel_id=1, source_target_pairs={{8,0},{16,8},{24,16},{32,24},{40,32},{48,40},{56,48},{64,56},{72,6... | collective-permute-start | bytes 786440 | tf_op jit(solution)/shard_map/ppermute | solution.py:23
  67.6 8.5 %slice-start.2 = ((s8[8388608]{0:T(1024)(128)(4,1)}), s8[4194304]{0:T(1024)(128)(4,1)S(1)}, s32[]{:S(2)}) async-start(s8[8388608]{0:T(1024)(128)(4,1)} %bitcast.14), calls=%async_computation.2 | async-start | bytes 8388608
  69.5 3.4 %copy-start.3 = (bf16[16,4,256,256]{3,2,1,0:T(8,128)(2,1)S(1)}, bf16[16,4,256,256]{3,2,1,0:T(8,128)(2,1)}, u32[]{:S(2)}) copy-start(bf16[16,4,256,256]{3,2,1,0:T(8,128)(2,1)} %blk_ref.3) | copy-start | bytes 25165828
  72.9 3.2 %slice-start.3 = ((s8[8388608]{0:T(1024)(128)(4,1)}), s8[4194304]{0:T(1024)(128)(4,1)S(1)}, s32[]{:S(2)}) async-start(s8[8388608]{0:T(1024)(128)(4,1)} %bitcast.14), calls=%async_computation.3 | async-start | bytes 8388608

commit v9 on v5

--- a/solution.py
+++ b/solution.py
@@ -93,20 +93,21 @@
     orb, core, partner, chip = _place()
     _barrier_group(nchip, orb, core, partner, chip)
     pair = []
-    for i in range(nchip):
-        cp = _remote(x_ref.at[i, 1 - core], pair_recv.at[i], p_send.at[i], p_recv.at[i], partner, orb)
+    for j in list(range(1, nchip)) + [0]:
+        dst = lax.rem(chip + j, nchip)
+        cp = _remote(x_ref.at[dst, 1 - core], pair_recv.at[dst], p_send.at[j], p_recv.at[dst], partner, orb)
         cp.start()
         pair.append(cp)
-    for i in range(nchip):
-        pair[i].wait_recv()
-        part[i] = x_ref[i, core] + pair_recv[i]
     sends = []
     for j in range(1, nchip):
         dst = lax.rem(chip + j, nchip)
+        pair[j - 1].wait_recv()
+        part[dst] = x_ref[dst, core] + pair_recv[dst]
         cp = _remote(part.at[dst], chip_recv.at[chip], c_send.at[j], c_recv.at[chip], 2 * dst + core, orb)
         cp.start()
         sends.append(cp)
-    total = part[chip]
+    pair[-1].wait_recv()
+    total = x_ref[chip, core] + pair_recv[chip]
     for j in range(1, nchip):
         src = lax.rem(chip + nchip - j, nchip)
         _remote(part.at[src], chip_recv.at[src], c_send.at[j], c_recv.at[src], 2 * src + core, orb).wait_recv()
@@ -122,25 +123,29 @@
     orb, core, partner, chip = _place()
     rounded = total.astype(sendbuf.dtype)
     sendbuf[...] = rounded
-    half[chip] = rounded
     sends = []
     for j in range(1, nchip):
         dst = lax.rem(chip + j, nchip)
         cp = _remote(sendbuf, half.at[chip], g_send.at[j], g_recv.at[chip], 2 * dst + core, orb)
         cp.start()
         sends.append(cp)
+    cp = _remote(sendbuf, other.at[chip], h_send.at[0], h_recv.at[chip], partner, orb)
+    cp.start()
+    sends.append(cp)
+    out_ref[chip, core] = rounded
     for j in range(1, nchip):
         src = lax.rem(chip + nchip - j, nchip)
         _remote(sendbuf, half.at[src], g_send.at[j], g_recv.at[src], 2 * src + core, orb).wait_recv()
+        cp = _remote(half.at[src], other.at[src], h_send.at[j], h_recv.at[src], partner, orb)
+        cp.start()
+        sends.append(cp)
+        out_ref[src, core] = half[src]
+    for j in range(nchip):
+        src = lax.rem(chip + nchip - j, nchip)
+        _remote(sendbuf, other.at[src], h_send.at[j], h_recv.at[src], partner, orb).wait_recv()
+        out_ref[src, 1 - core] = other[src]
     for cp in sends:
         cp.wait_send()
-    cp = _remote(half, other, h_send.at[0], h_recv.at[0], partner, orb)
-    cp.start()
-    cp.wait_recv()
-    for i in range(nchip):
-        out_ref[i, core] = half[i]
-        out_ref[i, 1 - core] = other[i]
-    cp.wait_send()
 
 
 def _two_level_scratch(nchip, rows, cols):
@@ -165,7 +170,7 @@
             pltpu.VMEM((chunk, cols), jnp.bfloat16),
             pltpu.VMEM((nchip, chunk, cols), jnp.bfloat16),
             pltpu.VMEM((nchip, chunk, cols), jnp.bfloat16),
-        ] + [pltpu.SemaphoreType.DMA((nchip,))] * 6 + [pltpu.SemaphoreType.DMA((1,))] * 2,
+        ] + [pltpu.SemaphoreType.DMA((nchip,))] * 8,
         compiler_params=pltpu.CompilerParams(
             collective_id=0, has_side_effects=True, vmem_limit_bytes=12 * 1024 * 1024
         ),

time: 81.7 us -> 81.9 us (level)
  the two profiles are of different devices: /device:TPU:0 before, /device:TPU:1 now
where the time goes in v9:
time: 81.9 us; the launch traced here: 81.6 us
  Pallas kernels  38.6 us (47%)
  starting transfers between devices  11.3 us (14%)
  matrix products  11.3 us (14%)
  waiting for transfers between devices  10.8 us (13%)
  local copies, waits for them, and re-layouts  6.78 us (8%)
  other arithmetic  2.03 us (2%)
  between operations  0.83 us (1%)
    pallas_call x1, Pallas kernels, allreduce_to_bf16(): pl.pallas_call(functools.partial(allreduce_kernel, nchip), out_shape=jax....  19.7 us
    pallas_call x1, Pallas kernels, dipole_scatter(): pl.pallas_call(functools.partial(dipole_kernel, nchip, chunk, count), out...  12.4 us
    ppermute x2, waiting for transfers between devices, padded_2(): lax.ppermute(lax.slice_in_dim(block, 0, width, axis=dim), axis, backward)  8.79 us
    ppermute x2, starting transfers between devices, padded_2(): lax.ppermute(lax.slice_in_dim(block, block.shape[dim] - width, None, axis...  7.44 us
    dot_general x1, matrix products, on_device(): jnp.dot(target_orbitals, projection_b, preferred_element_type=jnp.float32)  6.58 us
    pallas_call x2, Pallas kernels, band_local(): pl.pallas_call(functools.partial(band_kernel, per), out_shape=jax.ShapeDt...  6.44 us
    unnamed x16, local copies, waits for them, and re-layouts  5 us
    ppermute x2, starting transfers between devices, padded_2(): lax.ppermute(lax.slice_in_dim(block, 0, width, axis=dim), axis, backward)  3.84 us
  transfers between devices with their start and end apart: 4, of which 4 were waited for; matrix products, arithmetic and copies ran while one was open for 1% of the time, Pallas kernels for 0%

profile of v9, /device:TPU:1, one launch (start us, length us, event | category | flops | bytes accessed | tf_op | source)
XLA Modules:
  0.0 81.6 jit_solution(15511239755027876764)
XLA Ops:
  0.6 1.1 %fusion.3 = (bf16[512,256]{1,0:T(8,128)(2,1)S(1)}, bf16[512,256]{1,0:T(8,128)(2,1)S(1)}) fusion(bf16[4096,256]{1,0:T(8,128)(2,1)} %param.5), kind=kLoop, calls=%fused_computation.10 | loop fusion | bytes 1048576 | tf_op jit(solution)/shard_map/slice | solution.py:21
  1.7 4.9 %collective-permute-start = (bf16[512,256]{1,0:T(8,128)(2,1)S(1)}, bf16[512,256]{1,0:T(8,128)(2,1)S(1)}, u32[]{:S(2)}, u32[]{:S(2)}) collective-permute-start(bf16[512,256]{1,0:T(8,128)(2,1)S(1)} %get-tuple-element.4), channel_id=1, source_target_pairs={{0,8},{8,16},{16,24},{24,32},{32,40},{40,48},{48,56},{56,64},{64,7... | collective-permute-start | bytes 786440 | tf_op jit(solution)/shard_map/ppermute | solution.py:20
  6.6 1.9 %collective-permute-start.1 = (bf16[512,256]{1,0:T(8,128)(2,1)S(1)}, bf16[512,256]{1,0:T(8,128)(2,1)S(1)}, u32[]{:S(2)}, u32[]{:S(2)}) collective-permute-start(bf16[512,256]{1,0:T(8,128)(2,1)S(1)} %get-tuple-element.5), channel_id=1, source_target_pairs={{8,0},{16,8},{24,16},{32,24},{40,32},{48,40},{56,48},{64,56},{72,6... | collective-permute-start | bytes 786440 | tf_op jit(solution)/shard_map/ppermute | solution.py:23
  8.6 0.8 copy.7.off_ref
  9.3 0.6 collective-permute-done
  9.9 4.4 %collective-permute-done.1 = bf16[512,256]{1,0:T(8,128)(2,1)S(1)} collective-permute-done((bf16[512,256]{1,0:T(8,128)(2,1)S(1)}, bf16[512,256]{1,0:T(8,128)(2,1)S(1)}, u32[]{:S(2)}, u32[]{:S(2)}) %collective-permute-start.1) | collective-permute-done | bytes 262176 | tf_op jit(solution)/shard_map/ppermute | solution.py:23
  14.3 1.8 %pad_maximum_fusion.field_ref = bf16[5120,256]{1,0:T(8,128)(2,1)S(1)} fusion(bf16[512,256]{1,0:T(8,128)(2,1)S(1)} %collective-permute-done.1, bf16[4096,256]{1,0:T(8,128)(2,1)} %param.5, bf16[512,256]{1,0:T(8,128)(2,1)S(1)} %collective-permute-done), kind=kLoop, calls=%fused_computation.4 | loop fusion | flops 7864320 | bytes 5242880 | tf_op jit(solution)/shard_map/concatenate | solution.py:24
  16.1 0.0 copy-start
  16.1 3.4 %copy-done = bf16[16,4,256,256]{3,2,1,0:T(8,128)(2,1)S(1)} copy-done((bf16[16,4,256,256]{3,2,1,0:T(8,128)(2,1)S(1)}, bf16[16,4,256,256]{3,2,1,0:T(8,128)(2,1)}, u32[]{:S(2)}) %copy-start) | copy-done | bytes 8388632
  19.5 0.0 copy-start.1
  19.5 3.2 %shard_map.68 = bf16[4096,256]{1,0:T(8,128)(2,1)S(1)} custom-call(s32[16,4]{1,0:T(8,128)S(1)} %copy.7.off_ref, bf16[16,4,256,256]{3,2,1,0:T(8,128)(2,1)S(1)} %copy-done, bf16[5120,256]{1,0:T(8,128)(2,1)S(1)} %pad_maximum_fusion.field_ref), custom_call_target="tpu_custom_call" | custom-call | flops 2147483648 | bytes 13107200 | tf_op jit(solution)/shard_map/pallas_call | solution.py:46
  22.7 0.2 copy-done.1
  22.9 2.3 %convolution_bitcast_fusion.2 = f32[1024,256]{0,1:T(8,128)S(1)} fusion(bf16[4096,256]{1,0:T(8,128)(2,1)S(1)} %shard_map.68, bf16[4096,1024]{1,0:T(8,128)(2,1)S(1)} %copy-done.1), kind=kOutput, calls=%fused_computation.7 | convolution fusion | flops 2147483648 | bytes 11534336 | tf_op jit(solution)/shard_map/dot_general | solution.py:220
  25.2 0.3 copy.8
  25.6 0.0 slice-start
  25.6 19.7 %shard_map.69 = bf16[8,2,64,256]{3,2,1,0:T(8,128)(2,1)S(1)} custom-call(f32[8,2,64,256]{3,2,1,0:T(8,128)S(1)} %bitcast.21), custom_call_target="tpu_custom_call" | custom-call | bytes 16777216 | tf_op jit(solution)/shard_map/pallas_call | solution.py:164
  45.3 0.0 slice-start.1
  45.3 6.6 %multiply_reduce_fusion = (f32[256]{0:T(256)S(1)}, bf16[4096,256]{1,0:T(8,128)(2,1)S(1)}) fusion(bf16[4096,1024]{1,0:T(8,128)(2,1)} %param.6, bf16[1024,256]{1,0:T(8,128)(2,1)S(1)} %bitcast.22, bf16[4096,256]{1,0:T(8,128)(2,1)} %param.5), kind=kOutput, calls=%fused_computation.3 | convolution fusion | flops 2153774848 | bytes 13108224 | tf_op jit(solution)/shard_map/dot_general | solution.py:224
  51.9 0.0 copy-start.2
  52.0 2.5 %collective-permute-start.2 = (bf16[512,256]{1,0:T(8,128)(2,1)S(1)}, bf16[512,256]{1,0:T(8,128)(2,1)S(1)}, u32[]{:S(2)}, u32[]{:S(2)}) collective-permute-start(bf16[512,256]{1,0:T(8,128)(2,1)S(1)} %get-tuple-element.2), channel_id=1, source_target_pairs={{0,8},{8,16},{16,24},{24,32},{32,40},{40,48},{48,56},{56,64},{64,7... | collective-permute-start | bytes 786440 | tf_op jit(solution)/shard_map/ppermute | solution.py:20
  54.5 1.9 %collective-permute-start.3 = (bf16[512,256]{1,0:T(8,128)(2,1)S(1)}, bf16[512,256]{1,0:T(8,128)(2,1)S(1)}, u32[]{:S(2)}, u32[]{:S(2)}) collective-permute-start(bf16[512,256]{1,0:T(8,128)(2,1)S(1)} %get-tuple-element.3), channel_id=1, source_target_pairs={{8,0},{16,8},{24,16},{32,24},{40,32},{48,40},{56,48},{64,56},{72,6... | collective-permute-start | bytes 786440 | tf_op jit(solution)/shard_map/ppermute | solution.py:23
  56.4 1.4 %collective-permute-done.2 = bf16[512,256]{1,0:T(8,128)(2,1)S(1)} collective-permute-done((bf16[512,256]{1,0:T(8,128)(2,1)S(1)}, bf16[512,256]{1,0:T(8,128)(2,1)S(1)}, u32[]{:S(2)}, u32[]{:S(2)}) %collective-permute-start.2) | collective-permute-done | bytes 262176 | tf_op jit(solution)/shard_map/ppermute | solution.py:20
  57.8 4.4 %collective-permute-done.3 = bf16[512,256]{1,0:T(8,128)(2,1)S(1)} collective-permute-done((bf16[512,256]{1,0:T(8,128)(2,1)S(1)}, bf16[512,256]{1,0:T(8,128)(2,1)S(1)}, u32[]{:S(2)}, u32[]{:S(2)}) %collective-permute-start.3) | collective-permute-done | bytes 262176 | tf_op jit(solution)/shard_map/ppermute | solution.py:23
  62.2 0.0 copy-done.2
  62.2 0.0 slice-start.2
  62.2 0.2 pad_maximum_fusion.1.field_ref
  62.3 0.0 slice-done
  62.4 0.0 slice-done.1
  62.4 0.0 slice-start.3
  62.4 3.2 %shard_map.70 = bf16[4096,256]{1,0:T(8,128)(2,1)S(1)} custom-call(s32[16,4]{1,0:T(8,128)S(1)} %copy.7.off_ref, bf16[16,4,256,256]{3,2,1,0:T(8,128)(2,1)S(1)} %bitcast.20, bf16[5120,256]{1,0:T(8,128)(2,1)S(1)} %pad_maximum_fusion.1.field_ref), custom_call_target="tpu_custom_call" | custom-call | flops 2147483648 | bytes 13107200 | tf_op jit(solution)/shard_map/pallas_call | solution.py:46
  65.6 0.0 slice-done.2
  65.6 0.1 slice-done.3
  65.7 2.4 %convolution_bitcast_fusion.1 = f32[1024,256]{0,1:T(8,128)S(1)} fusion(bf16[4096,256]{1,0:T(8,128)(2,1)S(1)} %shard_map.70, bf16[4096,1024]{1,0:T(8,128)(2,1)S(1)} %bitcast.24), kind=kOutput, calls=%fused_computation.6 | convolution fusion | flops 2147483648 | bytes 11534336 | tf_op jit(solution)/shard_map/dot_general | solution.py:229
  68.1 0.3 copy.11
  68.4 0.1 pad_maximum_fusion.2.x_ref
  68.5 12.4 %shard_map.71 = bf16[64,256]{1,0:T(8,128)(2,1)S(1)} custom-call(f32[8,2,72,256]{3,2,1,0:T(8,128)S(1)} %pad_maximum_fusion.2.x_ref), custom_call_target="tpu_custom_call" | custom-call | bytes 9437184 | tf_op jit(solution)/shard_map/pallas_call | solution.py:201
  81.0 0.6 copy.14
  (4 shorter events, 0.0 us)
Async XLA Ops:
  1.7 8.2 %collective-permute-start = (bf16[512,256]{1,0:T(8,128)(2,1)S(1)}, bf16[512,256]{1,0:T(8,128)(2,1)S(1)}, u32[]{:S(2)}, u32[]{:S(2)}) collective-permute-start(bf16[512,256]{1,0:T(8,128)(2,1)S(1)} %get-tuple-element.4), channel_id=1, source_target_pairs={{0,8},{8,16},{16,24},{24,32},{32,40},{40,48},{48,56},{56,64},{64,7... | collective-permute-start | bytes 786440 | tf_op jit(solution)/shard_map/ppermute | solution.py:20
  6.6 7.7 %collective-permute-start.1 = (bf16[512,256]{1,0:T(8,128)(2,1)S(1)}, bf16[512,256]{1,0:T(8,128)(2,1)S(1)}, u32[]{:S(2)}, u32[]{:S(2)}) collective-permute-start(bf16[512,256]{1,0:T(8,128)(2,1)S(1)} %get-tuple-element.5), channel_id=1, source_target_pairs={{8,0},{16,8},{24,16},{32,24},{40,32},{48,40},{56,48},{64,56},{72,6... | collective-permute-start | bytes 786440 | tf_op jit(solution)/shard_map/ppermute | solution.py:23
  16.1 3.4 %copy-start = (bf16[16,4,256,256]{3,2,1,0:T(8,128)(2,1)S(1)}, bf16[16,4,256,256]{3,2,1,0:T(8,128)(2,1)}, u32[]{:S(2)}) copy-start(bf16[16,4,256,256]{3,2,1,0:T(8,128)(2,1)} %blk_ref.2) | copy-start | bytes 25165828
  19.5 3.4 %copy-start.1 = (bf16[4096,1024]{1,0:T(8,128)(2,1)S(1)}, bf16[4096,1024]{1,0:T(8,128)(2,1)}, u32[]{:S(2)}) copy-start(bf16[4096,1024]{1,0:T(8,128)(2,1)} %param.6) | copy-start | bytes 25165828
  25.6 36.8 %slice-start = ((s8[8388608]{0:T(1024)(128)(4,1)}), s8[4194304]{0:T(1024)(128)(4,1)S(1)}, s32[]{:S(2)}) async-start(s8[8388608]{0:T(1024)(128)(4,1)} %bitcast.19), calls=%async_computation | async-start | bytes 8388608
  45.3 17.1 %slice-start.1 = ((s8[8388608]{0:T(1024)(128)(4,1)}), s8[4194304]{0:T(1024)(128)(4,1)S(1)}, s32[]{:S(2)}) async-start(s8[8388608]{0:T(1024)(128)(4,1)} %bitcast.19), calls=%async_computation.1 | async-start | bytes 8388608
  51.9 10.3 %copy-start.2 = (bf16[4096,256]{1,0:T(8,128)(2,1)}, bf16[4096,256]{1,0:T(8,128)(2,1)S(1)}, u32[]{:S(2)}) copy-start(bf16[4096,256]{1,0:T(8,128)(2,1)S(1)} %get-tuple-element.10) | copy-start | bytes 6291460
  52.0 5.8 %collective-permute-start.2 = (bf16[512,256]{1,0:T(8,128)(2,1)S(1)}, bf16[512,256]{1,0:T(8,128)(2,1)S(1)}, u32[]{:S(2)}, u32[]{:S(2)}) collective-permute-start(bf16[512,256]{1,0:T(8,128)(2,1)S(1)} %get-tuple-element.2), channel_id=1, source_target_pairs={{0,8},{8,16},{16,24},{24,32},{32,40},{40,48},{48,56},{56,64},{64,7... | collective-permute-start | bytes 786440 | tf_op jit(solution)/shard_map/ppermute | solution.py:20
  54.5 7.7 %collective-permute-start.3 = (bf16[512,256]{1,0:T(8,128)(2,1)S(1)}, bf16[512,256]{1,0:T(8,128)(2,1)S(1)}, u32[]{:S(2)}, u32[]{:S(2)}) collective-permute-start(bf16[512,256]{1,0:T(8,128)(2,1)S(1)} %get-tuple-element.3), channel_id=1, source_target_pairs={{8,0},{16,8},{24,16},{32,24},{40,32},{48,40},{56,48},{64,56},{72,6... | collective-permute-start | bytes 786440 | tf_op jit(solution)/shard_map/ppermute | solution.py:23
  62.2 3.5 %slice-start.2 = ((s8[8388608]{0:T(1024)(128)(4,1)}), s8[4194304]{0:T(1024)(128)(4,1)S(1)}, s32[]{:S(2)}) async-start(s8[8388608]{0:T(1024)(128)(4,1)} %bitcast.23), calls=%async_computation.2 | async-start | bytes 8388608
  62.4 3.3 %slice-start.3 = ((s8[8388608]{0:T(1024)(128)(4,1)}), s8[4194304]{0:T(1024)(128)(4,1)S(1)}, s32[]{:S(2)}) async-start(s8[8388608]{0:T(1024)(128)(4,1)} %bitcast.23), calls=%async_computation.3 | async-start | bytes 8388608

commit v10 on v9

--- a/solution.py
+++ b/solution.py
@@ -23,6 +23,96 @@
         high = lax.ppermute(lax.slice_in_dim(block, 0, width, axis=dim), axis, backward)
         block = jnp.concatenate([low, block, high], axis=dim)
     return block
+
+
+def halo_kernel(n, field_ref, out_ref, low, high, send_sem, recv_sem, copy_sem):
+    rows, width = field_ref.shape
+    edge = 2 * BK
+    me = lax.axis_index("basis")
+    orb = lax.axis_index("orb")
+    has_low = me > 0
+    has_high = me < n - 1
+    middle = pltpu.make_async_copy(field_ref, out_ref.at[pl.ds(edge, rows)], copy_sem.at[0])
+    middle.start()
+    barrier = pltpu.get_barrier_semaphore()
+
+    @pl.when(has_low)
+    def _():
+        pl.semaphore_signal(barrier, inc=1, device_id=(me - 1, orb), device_id_type=MESH)
+
+    @pl.when(has_high)
+    def _():
+        pl.semaphore_signal(barrier, inc=1, device_id=(me + 1, orb), device_id_type=MESH)
+
+    pl.semaphore_wait(barrier, has_low.astype(jnp.int32) + has_high.astype(jnp.int32))
+    to_low = pltpu.make_async_remote_copy(
+        src_ref=field_ref.at[pl.ds(0, edge)], dst_ref=high,
+        send_sem=send_sem.at[0], recv_sem=recv_sem.at[0],
+        device_id=(jnp.maximum(me - 1, 0), orb), device_id_type=MESH,
+    )
+    to_high = pltpu.make_async_remote_copy(
+        src_ref=field_ref.at[pl.ds(rows - edge, edge)], dst_ref=low,
+        send_sem=send_sem.at[1], recv_sem=recv_sem.at[1],
+        device_id=(jnp.minimum(me + 1, n - 1), orb), device_id_type=MESH,
+    )
+
+    @pl.when(has_low)
+    def _():
+        to_low.start()
+
+    @pl.when(has_high)
+    def _():
+        to_high.start()
+
+    @pl.when(has_high)
+    def _():
+        to_low.wait_recv()
+        out_ref[pl.ds(rows + edge, edge), :] = high[...]
+
+    @pl.when(jnp.logical_not(has_high))
+    def _():
+        out_ref[pl.ds(rows + edge, edge), :] = jnp.zeros((edge, width), out_ref.dtype)
+
+    @pl.when(has_low)
+    def _():
+        to_high.wait_recv()
+        out_ref[pl.ds(0, edge), :] = low[...]
+
+    @pl.when(jnp.logical_not(has_low))
+    def _():
+        out_ref[pl.ds(0, edge), :] = jnp.zeros((edge, width), out_ref.dtype)
+
+    @pl.when(has_low)
+    def _():
+        to_low.wait_send()
+
+    @pl.when(has_high)
+    def _():
+        to_high.wait_send()
+
+    middle.wait()
+
+
+def with_halo(field, collective_id):
+    rows, width = field.shape
+    n = lax.axis_size("basis")
+    return pl.pallas_call(
+        functools.partial(halo_kernel, n),
+        out_shape=jax.ShapeDtypeStruct((rows + 4 * BK, width), field.dtype),
+        in_specs=[pl.BlockSpec(memory_space=pltpu.VMEM)],
+        out_specs=pl.BlockSpec(memory_space=pltpu.VMEM),
+        scratch_shapes=[
+            pltpu.VMEM((2 * BK, width), field.dtype),
+            pltpu.VMEM((2 * BK, width), field.dtype),
+            pltpu.SemaphoreType.DMA((2,)),
+            pltpu.SemaphoreType.DMA((2,)),
+            pltpu.SemaphoreType.DMA((1,)),
+        ],
+        cost_estimate=pl.CostEstimate(flops=0, bytes_accessed=4 * field.size * 2, transcendentals=0),
+        compiler_params=pltpu.CompilerParams(
+            collective_id=collective_id, has_side_effects=True, vmem_limit_bytes=8 * 1024 * 1024
+        ),
+    )(field)
 
 
 def band_kernel(rows_per_step, off_ref, blk_ref, field_ref, out_ref):
@@ -215,7 +305,7 @@
 def on_device(cont_orbitals, target_orbitals, margin_blocks, dipole_blocks, band_offsets):
     n = lax.axis_size("basis")
     count = band_offsets.shape[0] * BK * n
-    cont_padded = padded_2(cont_orbitals, (("basis", 0),), 2 * BK)
+    cont_padded = with_halo(cont_orbitals, 2)
     margin_cont = band_local(margin_blocks, band_offsets, cont_padded)
     partial_proj = lax.dot_general(
         target_orbitals, margin_cont, (((0,), (0,)), ((), ())), preferred_element_type=jnp.float32
@@ -224,7 +314,7 @@
     removed = jnp.dot(target_orbitals, projection_b, preferred_element_type=jnp.float32)
     cont_orth = (cont_orbitals.astype(jnp.float32) - removed).astype(jnp.bfloat16)
     squares = jnp.sum(jnp.square(cont_orth.astype(jnp.float32)), axis=0)
-    orth_padded = padded_2(cont_orth, (("basis", 0),), 2 * BK)
+    orth_padded = with_halo(cont_orth, 3)
     dipole_cont = band_local(dipole_blocks, band_offsets, orth_padded)
     partial_dip = lax.dot_general(
         target_orbitals,

time: 81.9 us -> 79.2 us (0.967)
  Pallas kernels: 38.6 us -> 57.7 us
  starting transfers between devices: 11.3 us -> 0 us
  waiting for transfers between devices: 10.8 us -> 0 us
  other arithmetic: 2.03 us -> 0.1 us
  local copies, waits for them, and re-layouts: 6.78 us -> 8.58 us
    pallas_call x0 -> x2, Pallas kernels: none -> 16.4 us  [with_halo(): pl.pallas_call(functools.partial(halo_kernel, n), out_shape=jax.ShapeDtyp...]
    ppermute x4 -> x0, starting transfers between devices: 11.3 us -> none  [the longest x2 7.44 us: padded_2(): lax.ppermute(lax.slice_in_dim(block, block.shape[dim] - width, None, axis...]
    ppermute x4 -> x0, waiting for transfers between devices: 10.8 us -> none  [the longest x2 8.79 us: padded_2(): lax.ppermute(lax.slice_in_dim(block, 0, width, axis=dim), axis, backward)]
    pallas_call x1, Pallas kernels: 19.7 us -> 22 us  [allreduce_to_bf16(): pl.pallas_call(functools.partial(allreduce_kernel, nchip), out_shape=jax....]
    concatenate x2 -> x0, other arithmetic: 1.93 us -> none  [padded_2(): block = jnp.concatenate([low, block, high], axis=dim)]
    unnamed x16 -> x20, local copies, waits for them, and re-layouts: 5 us -> 6.53 us
    dot_general x1, local copies, waits for them, and re-layouts: 0.33 us -> 1.7 us  [on_device(): lax.dot_general(target_orbitals, margin_cont, (((0,), (0,)), ((), ())), p...]
    slice x2 -> x0, local copies, waits for them, and re-layouts: 1.1 us -> none  [padded_2(): lax.slice_in_dim(block, block.shape[dim] - width, None, axis=dim)]
  transfers between devices with their start and end apart: 4 -> 0, of which waited for: 4 -> 0; matrix products, arithmetic and copies ran while one was open for 1% -> 0% of each run, Pallas kernels for 0% -> 0%
where the time goes in v10:
time: 79.2 us; the launch traced here: 79 us
  Pallas kernels  57.7 us (73%)
  matrix products  11.8 us (15%)
  local copies, waits for them, and re-layouts  8.58 us (11%)
  between operations  0.83 us (1%)
    pallas_call x1, Pallas kernels, allreduce_to_bf16(): pl.pallas_call(functools.partial(allreduce_kernel, nchip), out_shape=jax....  22 us
    pallas_call x2, Pallas kernels, with_halo(): pl.pallas_call(functools.partial(halo_kernel, n), out_shape=jax.ShapeDtyp...  16.4 us
    pallas_call x1, Pallas kernels, dipole_scatter(): pl.pallas_call(functools.partial(dipole_kernel, nchip, chunk, count), out...  12.8 us
    unnamed x20, local copies, waits for them, and re-layouts  6.53 us
    pallas_call x2, Pallas kernels, band_local(): pl.pallas_call(functools.partial(band_kernel, per), out_shape=jax.ShapeDt...  6.49 us
    dot_general x1, matrix products, on_device(): jnp.dot(target_orbitals, projection_b, preferred_element_type=jnp.float32)  6.07 us
    dot_general x1, matrix products, on_device(): lax.dot_general(target_orbitals, margin_cont, (((0,), (0,)), ((), ())), p...  3.31 us
    dot_general x1, matrix products, on_device(): lax.dot_general(target_orbitals, dipole_cont, (((0,), (0,)), ((), ())), p...  2.39 us

profile of v10, /device:TPU:1, one launch (start us, length us, event | category | flops | bytes accessed | tf_op | source)
XLA Modules:
  0.0 79.0 jit_solution(17304506392602741506)
XLA Ops:
  0.6 0.8 copy.7.off_ref
  1.4 0.0 copy-start.1
  1.4 1.6 %copy-done.1 = bf16[4096,256]{1,0:T(8,128)(2,1)S(1)} copy-done((bf16[4096,256]{1,0:T(8,128)(2,1)S(1)}, bf16[4096,256]{1,0:T(8,128)(2,1)}, u32[]{:S(2)}) %copy-start.1) | copy-done | bytes 2097176
  3.0 9.3 %shard_map.68.field_ref = bf16[5120,256]{1,0:T(8,128)(2,1)S(1)} custom-call(bf16[4096,256]{1,0:T(8,128)(2,1)S(1)} %copy-done.1), custom_call_target="tpu_custom_call" | custom-call | bytes 8388608 | tf_op jit(solution)/shard_map/pallas_call | solution.py:99
  12.3 0.0 copy-start
  12.3 3.4 %copy-done = bf16[16,4,256,256]{3,2,1,0:T(8,128)(2,1)S(1)} copy-done((bf16[16,4,256,256]{3,2,1,0:T(8,128)(2,1)S(1)}, bf16[16,4,256,256]{3,2,1,0:T(8,128)(2,1)}, u32[]{:S(2)}) %copy-start) | copy-done | bytes 8388632
  15.7 0.0 copy-start.4
  15.7 3.2 %shard_map.69 = bf16[4096,256]{1,0:T(8,128)(2,1)S(1)} custom-call(s32[16,4]{1,0:T(8,128)S(1)} %copy.7.off_ref, bf16[16,4,256,256]{3,2,1,0:T(8,128)(2,1)S(1)} %copy-done, bf16[5120,256]{1,0:T(8,128)(2,1)S(1)} %shard_map.68.field_ref), custom_call_target="tpu_custom_call" | custom-call | flops 2147483648 | bytes 13107200 | tf_op jit(solution)/shard_map/pallas_call | solution.py:136
  18.9 0.1 copy-done.4
  19.1 3.3 %convolution_bitcast_fusion.2 = f32[1024,256]{0,1:T(8,128)} fusion(bf16[4096,256]{1,0:T(8,128)(2,1)S(1)} %shard_map.69, bf16[4096,1024]{1,0:T(8,128)(2,1)S(1)} %copy-done.4), kind=kOutput, calls=%fused_computation.5 | convolution fusion | flops 2147483648 | bytes 11534336 | tf_op jit(solution)/shard_map/dot_general | solution.py:310
  22.4 0.0 copy-start.2
  22.4 1.7 %copy.8 = f32[1024,256]{1,0:T(8,128)S(1)} copy(f32[1024,256]{0,1:T(8,128)} %convolution_bitcast_fusion.2) | data formatting | bytes 2097152 | tf_op jit(solution)/shard_map/dot_general | solution.py:310
  24.1 22.0 %shard_map.70 = bf16[8,2,64,256]{3,2,1,0:T(8,128)(2,1)S(1)} custom-call(f32[8,2,64,256]{3,2,1,0:T(8,128)S(1)} %bitcast.21), custom_call_target="tpu_custom_call" | custom-call | bytes 16777216 | tf_op jit(solution)/shard_map/pallas_call | solution.py:254
  46.1 0.0 slice-start
  46.2 0.0 copy-done.2
  46.2 0.0 slice-start.1
  46.2 6.1 %multiply_reduce_fusion = (f32[256]{0:T(256)S(1)}, bf16[4096,256]{1,0:T(8,128)(2,1)S(1)}) fusion(bf16[4096,1024]{1,0:T(8,128)(2,1)} %param.6, bf16[1024,256]{1,0:T(8,128)(2,1)S(1)} %bitcast.22, bf16[4096,256]{1,0:T(8,128)(2,1)S(1)} %copy-done.2), kind=kOutput, calls=%fused_computation.3 | convolution fusion | flops 2153774848 | bytes 13108224 | tf_op jit(solution)/shard_map/dot_general | solution.py:314
  52.2 0.0 copy-start.3
  52.3 0.0 slice-start.2
  52.3 7.1 %shard_map.71.field_ref = bf16[5120,256]{1,0:T(8,128)(2,1)S(1)} custom-call(bf16[4096,256]{1,0:T(8,128)(2,1)S(1)} %get-tuple-element.6.field_ref), custom_call_target="tpu_custom_call" | custom-call | bytes 8388608 | tf_op jit(solution)/shard_map/pallas_call | solution.py:99
  59.3 0.0 slice-done
  59.4 0.0 slice-done.1
  59.4 0.0 slice-start.3
  59.4 3.3 %shard_map.72 = bf16[4096,256]{1,0:T(8,128)(2,1)S(1)} custom-call(s32[16,4]{1,0:T(8,128)S(1)} %copy.7.off_ref, bf16[16,4,256,256]{3,2,1,0:T(8,128)(2,1)S(1)} %bitcast.20, bf16[5120,256]{1,0:T(8,128)(2,1)S(1)} %shard_map.71.field_ref), custom_call_target="tpu_custom_call" | custom-call | flops 2147483648 | bytes 13107200 | tf_op jit(solution)/shard_map/pallas_call | solution.py:136
  62.7 0.0 copy-done.3
  62.7 0.0 slice-done.2
  62.7 0.0 slice-done.3
  62.7 2.4 %convolution_bitcast_fusion.1 = f32[1024,256]{0,1:T(8,128)S(1)} fusion(bf16[4096,256]{1,0:T(8,128)(2,1)S(1)} %shard_map.72, bf16[4096,1024]{1,0:T(8,128)(2,1)S(1)} %bitcast.24), kind=kOutput, calls=%fused_computation.4 | convolution fusion | flops 2147483648 | bytes 11534336 | tf_op jit(solution)/shard_map/dot_general | solution.py:319
  65.1 0.3 copy.11
  65.5 0.1 pad_maximum_fusion.x_ref
  65.6 12.8 %shard_map.73 = bf16[64,256]{1,0:T(8,128)(2,1)S(1)} custom-call(f32[8,2,72,256]{3,2,1,0:T(8,128)S(1)} %pad_maximum_fusion.x_ref), custom_call_target="tpu_custom_call" | custom-call | bytes 9437184 | tf_op jit(solution)/shard_map/pallas_call | solution.py:291
  78.4 0.6 copy.14
  (3 shorter events, 0.0 us)
Async XLA Ops:
  1.4 1.6 %copy-start.1 = (bf16[4096,256]{1,0:T(8,128)(2,1)S(1)}, bf16[4096,256]{1,0:T(8,128)(2,1)}, u32[]{:S(2)}) copy-start(bf16[4096,256]{1,0:T(8,128)(2,1)} %field_ref.1) | copy-start | bytes 6291460
  12.3 3.4 %copy-start = (bf16[16,4,256,256]{3,2,1,0:T(8,128)(2,1)S(1)}, bf16[16,4,256,256]{3,2,1,0:T(8,128)(2,1)}, u32[]{:S(2)}) copy-start(bf16[16,4,256,256]{3,2,1,0:T(8,128)(2,1)} %blk_ref.2) | copy-start | bytes 25165828
  15.7 3.4 %copy-start.4 = (bf16[4096,1024]{1,0:T(8,128)(2,1)S(1)}, bf16[4096,1024]{1,0:T(8,128)(2,1)}, u32[]{:S(2)}) copy-start(bf16[4096,1024]{1,0:T(8,128)(2,1)} %param.6) | copy-start | bytes 25165828
  22.4 23.7 %copy-start.2 = (bf16[4096,256]{1,0:T(8,128)(2,1)S(1)}, bf16[4096,256]{1,0:T(8,128)(2,1)}, u32[]{:S(2)}) copy-start(bf16[4096,256]{1,0:T(8,128)(2,1)} %field_ref.1) | copy-start | bytes 6291460
  46.1 13.2 %slice-start = ((s8[8388608]{0:T(1024)(128)(4,1)}), s8[4194304]{0:T(1024)(128)(4,1)S(1)}, s32[]{:S(2)}) async-start(s8[8388608]{0:T(1024)(128)(4,1)} %bitcast.19), calls=%async_computation | async-start | bytes 8388608
  46.2 13.2 %slice-start.1 = ((s8[8388608]{0:T(1024)(128)(4,1)}), s8[4194304]{0:T(1024)(128)(4,1)S(1)}, s32[]{:S(2)}) async-start(s8[8388608]{0:T(1024)(128)(4,1)} %bitcast.19), calls=%async_computation.1 | async-start | bytes 8388608
  52.2 10.4 %copy-start.3 = (bf16[4096,256]{1,0:T(8,128)(2,1)}, bf16[4096,256]{1,0:T(8,128)(2,1)S(1)}, u32[]{:S(2)}) copy-start(bf16[4096,256]{1,0:T(8,128)(2,1)S(1)} %get-tuple-element.6.field_ref) | copy-start | bytes 6291460
  52.3 10.4 %slice-start.2 = ((s8[8388608]{0:T(1024)(128)(4,1)}), s8[4194304]{0:T(1024)(128)(4,1)S(1)}, s32[]{:S(2)}) async-start(s8[8388608]{0:T(1024)(128)(4,1)} %bitcast.23), calls=%async_computation.2 | async-start | bytes 8388608
  59.4 3.3 %slice-start.3 = ((s8[8388608]{0:T(1024)(128)(4,1)}), s8[4194304]{0:T(1024)(128)(4,1)S(1)}, s32[]{:S(2)}) async-start(s8[8388608]{0:T(1024)(128)(4,1)} %bitcast.23), calls=%async_computation.3 | async-start | bytes 8388608

commit v11 on v10

--- a/solution.py
+++ b/solution.py
@@ -113,6 +113,115 @@
             collective_id=collective_id, has_side_effects=True, vmem_limit_bytes=8 * 1024 * 1024
         ),
     )(field)
+
+
+def orth_halo_kernel(n, tgt_ref, proj_ref, cont_ref, orth_ref, pad_ref, sq_ref, low, high, send_sem, recv_sem):
+    rows, width = cont_ref.shape
+    edge = 2 * BK
+    me = lax.axis_index("basis")
+    orb = lax.axis_index("orb")
+    has_low = me > 0
+    has_high = me < n - 1
+    barrier = pltpu.get_barrier_semaphore()
+
+    @pl.when(has_low)
+    def _():
+        pl.semaphore_signal(barrier, inc=1, device_id=(me - 1, orb), device_id_type=MESH)
+
+    @pl.when(has_high)
+    def _():
+        pl.semaphore_signal(barrier, inc=1, device_id=(me + 1, orb), device_id_type=MESH)
+
+    def tile(start):
+        removed = jnp.dot(tgt_ref[pl.ds(start, edge), :], proj_ref[...], preferred_element_type=jnp.float32)
+        orth = (cont_ref[pl.ds(start, edge), :].astype(jnp.float32) - removed).astype(orth_ref.dtype)
+        orth_ref[pl.ds(start, edge), :] = orth
+        pad_ref[pl.ds(start + edge, edge), :] = orth
+        wide = orth.astype(jnp.float32)
+        return jnp.sum(wide * wide, axis=0, keepdims=True)
+
+    squares = tile(0) + tile(rows - edge)
+    pl.semaphore_wait(barrier, has_low.astype(jnp.int32) + has_high.astype(jnp.int32))
+    to_low = pltpu.make_async_remote_copy(
+        src_ref=orth_ref.at[pl.ds(0, edge)], dst_ref=high,
+        send_sem=send_sem.at[0], recv_sem=recv_sem.at[0],
+        device_id=(jnp.maximum(me - 1, 0), orb), device_id_type=MESH,
+    )
+    to_high = pltpu.make_async_remote_copy(
+        src_ref=orth_ref.at[pl.ds(rows - edge, edge)], dst_ref=low,
+        send_sem=send_sem.at[1], recv_sem=recv_sem.at[1],
+        device_id=(jnp.minimum(me + 1, n - 1), orb), device_id_type=MESH,
+    )
+
+    @pl.when(has_low)
+    def _():
+        to_low.start()
+
+    @pl.when(has_high)
+    def _():
+        to_high.start()
+
+    for start in range(edge, rows - edge, edge):
+        squares = squares + tile(start)
+    sq_ref[...] = squares
+
+    @pl.when(has_high)
+    def _():
+        to_low.wait_recv()
+        pad_ref[pl.ds(rows + edge, edge), :] = high[...]
+
+    @pl.when(jnp.logical_not(has_high))
+    def _():
+        pad_ref[pl.ds(rows + edge, edge), :] = jnp.zeros((edge, width), pad_ref.dtype)
+
+    @pl.when(has_low)
+    def _():
+        to_high.wait_recv()
+        pad_ref[pl.ds(0, edge), :] = low[...]
+
+    @pl.when(jnp.logical_not(has_low))
+    def _():
+        pad_ref[pl.ds(0, edge), :] = jnp.zeros((edge, width), pad_ref.dtype)
+
+    @pl.when(has_low)
+    def _():
+        to_low.wait_send()
+
+    @pl.when(has_high)
+    def _():
+        to_high.wait_send()
+
+
+def orthogonalize_with_halo(target, projection_b, cont, collective_id):
+    rows, nt = target.shape
+    width = cont.shape[1]
+    n = lax.axis_size("basis")
+    vmem = pl.BlockSpec(memory_space=pltpu.VMEM)
+    orth, padded, squares = pl.pallas_call(
+        functools.partial(orth_halo_kernel, n),
+        out_shape=(
+            jax.ShapeDtypeStruct((rows, width), jnp.bfloat16),
+            jax.ShapeDtypeStruct((rows + 4 * BK, width), jnp.bfloat16),
+            jax.ShapeDtypeStruct((1, width), jnp.float32),
+        ),
+        in_specs=[vmem, vmem, vmem],
+        out_specs=(vmem, vmem, vmem),
+        scratch_shapes=[
+            pltpu.VMEM((2 * BK, width), jnp.bfloat16),
+            pltpu.VMEM((2 * BK, width), jnp.bfloat16),
+            pltpu.SemaphoreType.DMA((2,)),
+            pltpu.SemaphoreType.DMA((2,)),
+        ],
+        cost_estimate=pl.CostEstimate(
+            flops=2 * rows * nt * width,
+            bytes_accessed=target.size * 2 + projection_b.size * 2 + 3 * cont.size * 2,
+            transcendentals=0,
+        ),
+        compiler_params=pltpu.CompilerParams(
+            collective_id=collective_id, has_side_effects=True, vmem_limit_bytes=24 * 1024 * 1024
+        ),
+    )(target, projection_b, cont)
+    return orth, padded, squares[0]
 
 
 def band_kernel(rows_per_step, off_ref, blk_ref, field_ref, out_ref):
@@ -311,10 +420,9 @@
         target_orbitals, margin_cont, (((0,), (0,)), ((), ())), preferred_element_type=jnp.float32
     )
     projection_b = allreduce_to_bf16(partial_proj, n)
-    removed = jnp.dot(target_orbitals, projection_b, preferred_element_type=jnp.float32)
-    cont_orth = (cont_orbitals.astype(jnp.float32) - removed).astype(jnp.bfloat16)
-    squares = jnp.sum(jnp.square(cont_orth.astype(jnp.float32)), axis=0)
-    orth_padded = with_halo(cont_orth, 3)
+    cont_orth, orth_padded, squares = orthogonalize_with_halo(
+        target_orbitals, projection_b, cont_orbitals, 3
+    )
     dipole_cont = band_local(dipole_blocks, band_offsets, orth_padded)
     partial_dip = lax.dot_general(
         target_orbitals,

time: 79.2 us -> 82.2 us (1.038)
  local copies, waits for them, and re-layouts: 8.58 us -> 17.8 us
  matrix products: 11.8 us -> 5.67 us
    unnamed x20 -> x25, local copies, waits for them, and re-layouts: 6.53 us -> 15.8 us
    pallas_call x2 -> x1, Pallas kernels: 16.4 us -> 9.34 us  [with_halo(): pl.pallas_call(functools.partial(halo_kernel, n), out_shape=jax.ShapeDtyp...]
    pallas_call x0 -> x1, Pallas kernels: none -> 6.97 us  [orthogonalize_with_halo(): pl.pallas_call(functools.partial(orth_halo_kernel, n), out_shape=(jax.Sha...]
    dot_general x1 -> x0, matrix products: 6.07 us -> none  [on_device(): jnp.dot(target_orbitals, projection_b, preferred_element_type=jnp.float32)]
where the time goes in v11:
time: 82.2 us; the launch traced here: 82 us
  Pallas kernels  57.6 us (70%)
  local copies, waits for them, and re-layouts  17.8 us (22%)
  matrix products  5.67 us (7%)
    pallas_call x1, Pallas kernels, allreduce_to_bf16(): pl.pallas_call(functools.partial(allreduce_kernel, nchip), out_shape=jax....  22 us
    unnamed x25, local copies, waits for them, and re-layouts  15.8 us
    pallas_call x1, Pallas kernels, dipole_scatter(): pl.pallas_call(functools.partial(dipole_kernel, nchip, chunk, count), out...  12.8 us
    pallas_call x1, Pallas kernels, with_halo(): pl.pallas_call(functools.partial(halo_kernel, n), out_shape=jax.ShapeDtyp...  9.34 us
    pallas_call x1, Pallas kernels, orthogonalize_with_halo(): pl.pallas_call(functools.partial(orth_halo_kernel, n), out_shape=(jax.Sha...  6.97 us
    pallas_call x2, Pallas kernels, band_local(): pl.pallas_call(functools.partial(band_kernel, per), out_shape=jax.ShapeDt...  6.43 us
    dot_general x1, matrix products, on_device(): lax.dot_general(target_orbitals, margin_cont, (((0,), (0,)), ((), ())), p...  3.32 us
    dot_general x1, matrix products, on_device(): lax.dot_general(target_orbitals, dipole_cont, (((0,), (0,)), ((), ())), p...  2.35 us

profile of v11, /device:TPU:1, one launch (start us, length us, event | category | flops | bytes accessed | tf_op | source)
XLA Modules:
  0.0 82.0 jit_solution(9820977667540306636)
XLA Ops:
  0.6 0.8 copy.7.off_ref
  1.4 0.0 copy-start.3
  1.4 1.6 %copy-done.3 = bf16[4096,256]{1,0:T(8,128)(2,1)S(1)} copy-done((bf16[4096,256]{1,0:T(8,128)(2,1)S(1)}, bf16[4096,256]{1,0:T(8,128)(2,1)}, u32[]{:S(2)}) %copy-start.3) | copy-done | bytes 2097176
  3.0 0.0 slice-start
  3.0 9.3 %shard_map.68.field_ref = bf16[5120,256]{1,0:T(8,128)(2,1)S(1)} custom-call(bf16[4096,256]{1,0:T(8,128)(2,1)S(1)} %copy-done.3), custom_call_target="tpu_custom_call" | custom-call | bytes 8388608 | tf_op jit(solution)/shard_map/pallas_call | solution.py:99
  12.3 0.0 copy-start.1
  12.3 3.4 %copy-done.1 = bf16[16,4,256,256]{3,2,1,0:T(8,128)(2,1)S(1)} copy-done((bf16[16,4,256,256]{3,2,1,0:T(8,128)(2,1)S(1)}, bf16[16,4,256,256]{3,2,1,0:T(8,128)(2,1)}, u32[]{:S(2)}) %copy-start.1) | copy-done | bytes 8388632
  15.7 0.0 slice-start.1
  15.7 3.2 %shard_map.69 = bf16[4096,256]{1,0:T(8,128)(2,1)S(1)} custom-call(s32[16,4]{1,0:T(8,128)S(1)} %copy.7.off_ref, bf16[16,4,256,256]{3,2,1,0:T(8,128)(2,1)S(1)} %copy-done.1, bf16[5120,256]{1,0:T(8,128)(2,1)S(1)} %shard_map.68.field_ref), custom_call_target="tpu_custom_call" | custom-call | flops 2147483648 | bytes 13107200 | tf_op jit(solution)/shard_map/pallas_call | solution.py:245
  18.9 0.0 slice-done
  19.0 0.0 slice-done.1
  19.0 3.3 %convolution_bitcast_fusion.1 = f32[1024,256]{0,1:T(8,128)} fusion(bf16[4096,256]{1,0:T(8,128)(2,1)S(1)} %shard_map.69, bf16[4096,1024]{1,0:T(8,128)(2,1)S(1)} %bitcast.13), kind=kOutput, calls=%fused_computation.1 | convolution fusion | flops 2147483648 | bytes 11534336 | tf_op jit(solution)/shard_map/dot_general | solution.py:419
  22.3 0.0 copy-start.4
  22.3 1.7 %copy.8 = f32[1024,256]{1,0:T(8,128)S(1)} copy(f32[1024,256]{0,1:T(8,128)} %convolution_bitcast_fusion.1) | data formatting | bytes 2097152 | tf_op jit(solution)/shard_map/dot_general | solution.py:419
  24.0 22.0 %shard_map.70 = bf16[8,2,64,256]{3,2,1,0:T(8,128)(2,1)S(1)} custom-call(f32[8,2,64,256]{3,2,1,0:T(8,128)S(1)} %bitcast.16), custom_call_target="tpu_custom_call" | custom-call | bytes 16777216 | tf_op jit(solution)/shard_map/pallas_call | solution.py:363
  46.0 0.0 copy-done.4
  46.0 0.0 copy-start
  46.0 3.4 %copy-done = bf16[4096,1024]{1,0:T(8,128)(2,1)S(1)} copy-done((bf16[4096,1024]{1,0:T(8,128)(2,1)S(1)}, bf16[4096,1024]{1,0:T(8,128)(2,1)}, u32[]{:S(2)}) %copy-start) | copy-done | bytes 8388632
  49.4 0.0 slice-start.2
  49.4 7.0 %shard_map.71 = (bf16[4096,256]{1,0:T(8,128)(2,1)S(1)}, bf16[5120,256]{1,0:T(8,128)(2,1)S(1)}, f32[1,256]{1,0:T(1,128)S(1)}) custom-call(bf16[4096,1024]{1,0:T(8,128)(2,1)S(1)} %copy-done, bf16[1024,256]{1,0:T(8,128)(2,1)S(1)} %bitcast.17, bf16[4096,256]{1,0:T(8,128)(2,1)S(1)} %copy-done.4), custom_call_target="tpu_custom_call" | custom-call | flops 2147483648 | bytes 15204352 | tf_op jit(solution)/shard_map/pallas_call | solution.py:200
  56.4 0.0 copy-start.5
  56.4 1.3 %copy-done.5 = bf16[4096,256]{1,0:T(8,128)(2,1)} copy-done((bf16[4096,256]{1,0:T(8,128)(2,1)}, bf16[4096,256]{1,0:T(8,128)(2,1)S(1)}, u32[]{:S(2)}) %copy-start.5) | copy-done | bytes 2097176
  57.7 0.0 copy-start.2
  57.7 3.4 %copy-done.2 = bf16[16,4,256,256]{3,2,1,0:T(8,128)(2,1)S(1)} copy-done((bf16[16,4,256,256]{3,2,1,0:T(8,128)(2,1)S(1)}, bf16[16,4,256,256]{3,2,1,0:T(8,128)(2,1)}, u32[]{:S(2)}) %copy-start.2) | copy-done | bytes 8388632
  61.1 0.0 slice-start.3
  61.1 3.2 %shard_map.72 = bf16[4096,256]{1,0:T(8,128)(2,1)S(1)} custom-call(s32[16,4]{1,0:T(8,128)S(1)} %copy.7.off_ref, bf16[16,4,256,256]{3,2,1,0:T(8,128)(2,1)S(1)} %copy-done.2, bf16[5120,256]{1,0:T(8,128)(2,1)S(1)} %get-tuple-element.6.field_ref), custom_call_target="tpu_custom_call" | custom-call | flops 2147483648 | bytes 13107200 | tf_op jit(solution)/shard_map/pallas_call | solution.py:245
  64.3 0.0 slice-done.2
  64.3 0.0 slice-done.3
  64.3 2.4 %convolution_bitcast_fusion = f32[1024,256]{0,1:T(8,128)S(1)} fusion(bf16[4096,256]{1,0:T(8,128)(2,1)S(1)} %shard_map.72, bf16[4096,1024]{1,0:T(8,128)(2,1)S(1)} %bitcast.15), kind=kOutput, calls=%fused_computation | convolution fusion | flops 2147483648 | bytes 11534336 | tf_op jit(solution)/shard_map/dot_general | solution.py:427
  66.7 0.3 copy.10
  67.0 0.0 copy-start.6
  67.1 0.1 pad_maximum_fusion.x_ref
  67.1 12.8 %shard_map.73 = bf16[64,256]{1,0:T(8,128)(2,1)S(1)} custom-call(f32[8,2,72,256]{3,2,1,0:T(8,128)S(1)} %pad_maximum_fusion.x_ref), custom_call_target="tpu_custom_call" | custom-call | bytes 9437184 | tf_op jit(solution)/shard_map/pallas_call | solution.py:400
  80.0 0.0 copy-done.6
  80.0 1.3 %copy.13 = bf16[4096,256]{1,0:T(8,128)(2,1)} copy(bf16[4096,256]{1,0:T(8,128)(2,1)S(1)} %copy-done.6) | data formatting | bytes 4194304
  81.3 0.6 copy.14
  (3 shorter events, 0.0 us)
Async XLA Ops:
  1.4 1.6 %copy-start.3 = (bf16[4096,256]{1,0:T(8,128)(2,1)S(1)}, bf16[4096,256]{1,0:T(8,128)(2,1)}, u32[]{:S(2)}) copy-start(bf16[4096,256]{1,0:T(8,128)(2,1)} %cont_ref.1) | copy-start | bytes 6291460
  3.0 16.0 %slice-start = ((s8[8388608]{0:T(1024)(128)(4,1)}), s8[4194304]{0:T(1024)(128)(4,1)S(1)}, s32[]{:S(2)}) async-start(s8[8388608]{0:T(1024)(128)(4,1)} %bitcast.12), calls=%async_computation | async-start | bytes 8388608
  12.3 3.4 %copy-start.1 = (bf16[16,4,256,256]{3,2,1,0:T(8,128)(2,1)S(1)}, bf16[16,4,256,256]{3,2,1,0:T(8,128)(2,1)}, u32[]{:S(2)}) copy-start(bf16[16,4,256,256]{3,2,1,0:T(8,128)(2,1)} %blk_ref.2) | copy-start | bytes 25165828
  15.7 3.2 %slice-start.1 = ((s8[8388608]{0:T(1024)(128)(4,1)}), s8[4194304]{0:T(1024)(128)(4,1)S(1)}, s32[]{:S(2)}) async-start(s8[8388608]{0:T(1024)(128)(4,1)} %bitcast.12), calls=%async_computation.1 | async-start | bytes 8388608
  22.3 23.7 %copy-start.4 = (bf16[4096,256]{1,0:T(8,128)(2,1)S(1)}, bf16[4096,256]{1,0:T(8,128)(2,1)}, u32[]{:S(2)}) copy-start(bf16[4096,256]{1,0:T(8,128)(2,1)} %cont_ref.1) | copy-start | bytes 6291460
  46.0 3.4 %copy-start = (bf16[4096,1024]{1,0:T(8,128)(2,1)S(1)}, bf16[4096,1024]{1,0:T(8,128)(2,1)}, u32[]{:S(2)}) copy-start(bf16[4096,1024]{1,0:T(8,128)(2,1)} %tgt_ref.1) | copy-start | bytes 25165828
  49.4 14.9 %slice-start.2 = ((s8[8388608]{0:T(1024)(128)(4,1)}), s8[4194304]{0:T(1024)(128)(4,1)S(1)}, s32[]{:S(2)}) async-start(s8[8388608]{0:T(1024)(128)(4,1)} %bitcast.14), calls=%async_computation.2 | async-start | bytes 8388608
  56.4 1.3 %copy-start.5 = (bf16[4096,256]{1,0:T(8,128)(2,1)}, bf16[4096,256]{1,0:T(8,128)(2,1)S(1)}, u32[]{:S(2)}) copy-start(bf16[4096,256]{1,0:T(8,128)(2,1)S(1)} %get-tuple-element.10) | copy-start | bytes 6291460
  57.7 3.4 %copy-start.2 = (bf16[16,4,256,256]{3,2,1,0:T(8,128)(2,1)S(1)}, bf16[16,4,256,256]{3,2,1,0:T(8,128)(2,1)}, u32[]{:S(2)}) copy-start(bf16[16,4,256,256]{3,2,1,0:T(8,128)(2,1)} %blk_ref.3) | copy-start | bytes 25165828
  61.1 3.2 %slice-start.3 = ((s8[8388608]{0:T(1024)(128)(4,1)}), s8[4194304]{0:T(1024)(128)(4,1)S(1)}, s32[]{:S(2)}) async-start(s8[8388608]{0:T(1024)(128)(4,1)} %bitcast.14), calls=%async_computation.3 | async-start | bytes 8388608
  67.0 13.0 %copy-start.6 = (bf16[4096,256]{1,0:T(8,128)(2,1)S(1)}, bf16[4096,256]{1,0:T(8,128)(2,1)}, u32[]{:S(2)}) copy-start(bf16[4096,256]{1,0:T(8,128)(2,1)} %copy-done.5) | copy-start | bytes 6291460

commit v12 on v10

--- a/solution.py
+++ b/solution.py
@@ -307,11 +307,13 @@
     count = band_offsets.shape[0] * BK * n
     cont_padded = with_halo(cont_orbitals, 2)
     margin_cont = band_local(margin_blocks, band_offsets, cont_padded)
-    partial_proj = lax.dot_general(
-        target_orbitals, margin_cont, (((0,), (0,)), ((), ())), preferred_element_type=jnp.float32
-    )
-    projection_b = allreduce_to_bf16(partial_proj, n)
-    removed = jnp.dot(target_orbitals, projection_b, preferred_element_type=jnp.float32)
+    partial_proj_t = lax.dot_general(
+        margin_cont, target_orbitals, (((0,), (0,)), ((), ())), preferred_element_type=jnp.float32
+    )
+    projection_b_t = allreduce_to_bf16(partial_proj_t, n)
+    removed = lax.dot_general(
+        target_orbitals, projection_b_t, (((1,), (1,)), ((), ())), preferred_element_type=jnp.float32
+    )
     cont_orth = (cont_orbitals.astype(jnp.float32) - removed).astype(jnp.bfloat16)
     squares = jnp.sum(jnp.square(cont_orth.astype(jnp.float32)), axis=0)
     orth_padded = with_halo(cont_orth, 3)

time: 79.2 us -> 73.1 us (0.923)
  matrix products: 11.8 us -> 7.47 us
  local copies, waits for them, and re-layouts: 8.58 us -> 6.83 us
    dot_general x2, matrix products: 9.39 us -> 5.12 us  [the longest x1 2.78 us: on_device(): lax.dot_general(target_orbitals, projection_b_t, (((1,), (1,)), ((), ()))...]
    dot_general x1 -> x0, local copies, waits for them, and re-layouts: 1.7 us -> none  [on_device(): lax.dot_general(target_orbitals, margin_cont, (((0,), (0,)), ((), ())), p...]
    unnamed x20 -> x16, local copies, waits for them, and re-layouts: 6.53 us -> 6.49 us
where the time goes in v12:
time: 73.1 us; the launch traced here: 72.9 us
  Pallas kernels  57.7 us (79%)
  matrix products  7.47 us (10%)
  local copies, waits for them, and re-layouts  6.83 us (9%)
  between operations  0.78 us (1%)
    pallas_call x1, Pallas kernels, allreduce_to_bf16(): pl.pallas_call(functools.partial(allreduce_kernel, nchip), out_shape=jax....  22 us
    pallas_call x2, Pallas kernels, with_halo(): pl.pallas_call(functools.partial(halo_kernel, n), out_shape=jax.ShapeDtyp...  16.4 us
    pallas_call x1, Pallas kernels, dipole_scatter(): pl.pallas_call(functools.partial(dipole_kernel, nchip, chunk, count), out...  12.8 us
    unnamed x16, local copies, waits for them, and re-layouts  6.49 us
    pallas_call x2, Pallas kernels, band_local(): pl.pallas_call(functools.partial(band_kernel, per), out_shape=jax.ShapeDt...  6.47 us
    dot_general x1, matrix products, on_device(): lax.dot_general(target_orbitals, projection_b_t, (((1,), (1,)), ((), ()))...  2.78 us
    dot_general x1, matrix products, on_device(): lax.dot_general(target_orbitals, dipole_cont, (((0,), (0,)), ((), ())), p...  2.35 us
    dot_general x1, matrix products, on_device(): lax.dot_general(margin_cont, target_orbitals, (((0,), (0,)), ((), ())), p...  2.34 us

profile of v12, /device:TPU:1, one launch (start us, length us, event | category | flops | bytes accessed | tf_op | source)
XLA Modules:
  0.0 72.9 jit_solution(17381258613990038921)
XLA Ops:
  0.6 0.8 %copy.7.off_ref = s32[16,4]{1,0:T(8,128)S(1)} copy(s32[16,4]{0,1:T(4,128)} %param.9) | data formatting | bytes 512 | tf_op args[4]
  1.4 0.0 copy-start.1
  1.4 1.6 %copy-done.1 = bf16[4096,256]{1,0:T(8,128)(2,1)S(1)} copy-done((bf16[4096,256]{1,0:T(8,128)(2,1)S(1)}, bf16[4096,256]{1,0:T(8,128)(2,1)}, u32[]{:S(2)}) %copy-start.1) | copy-done | bytes 2097176
  3.0 9.3 %shard_map.68.field_ref = bf16[5120,256]{1,0:T(8,128)(2,1)S(1)} custom-call(bf16[4096,256]{1,0:T(8,128)(2,1)S(1)} %copy-done.1), custom_call_target="tpu_custom_call" | custom-call | bytes 8388608 | tf_op jit(solution)/shard_map/pallas_call | solution.py:99
  12.3 0.0 copy-start
  12.3 3.4 %copy-done = bf16[16,4,256,256]{3,2,1,0:T(8,128)(2,1)S(1)} copy-done((bf16[16,4,256,256]{3,2,1,0:T(8,128)(2,1)S(1)}, bf16[16,4,256,256]{3,2,1,0:T(8,128)(2,1)}, u32[]{:S(2)}) %copy-start) | copy-done | bytes 8388632
  15.7 0.0 copy-start.4
  15.7 3.3 %shard_map.69 = bf16[4096,256]{1,0:T(8,128)(2,1)S(1)} custom-call(s32[16,4]{1,0:T(8,128)S(1)} %copy.7.off_ref, bf16[16,4,256,256]{3,2,1,0:T(8,128)(2,1)S(1)} %copy-done, bf16[5120,256]{1,0:T(8,128)(2,1)S(1)} %shard_map.68.field_ref), custom_call_target="tpu_custom_call" | custom-call | flops 2147483648 | bytes 13107200 | tf_op jit(solution)/shard_map/pallas_call | solution.py:136
  19.0 0.1 copy-done.4
  19.1 0.0 copy-start.2
  19.1 2.3 %fusion.2 = f32[256,1024]{1,0:T(8,128)S(1)} fusion(bf16[4096,256]{1,0:T(8,128)(2,1)S(1)} %shard_map.69, bf16[4096,1024]{1,0:T(8,128)(2,1)S(1)} %copy-done.4), kind=kOutput, calls=%fused_computation.6 | convolution fusion | flops 2147483648 | bytes 11534336 | tf_op jit(solution)/shard_map/dot_general | solution.py:310
  21.4 22.0 %shard_map.70 = bf16[8,2,16,1024]{3,2,1,0:T(8,128)(2,1)S(1)} custom-call(f32[8,2,16,1024]{3,2,1,0:T(8,128)S(1)} %bitcast.19), custom_call_target="tpu_custom_call" | custom-call | bytes 16777216 | tf_op jit(solution)/shard_map/pallas_call | solution.py:254
  43.4 0.0 slice-start
  43.5 0.0 copy-done.2
  43.5 0.0 slice-start.1
  43.5 2.8 %multiply_reduce_fusion = (f32[256]{0:T(256)S(1)}, bf16[4096,256]{1,0:T(8,128)(2,1)S(1)}) fusion(bf16[256,1024]{1,0:T(8,128)(2,1)S(1)} %bitcast.20, bf16[4096,1024]{1,0:T(8,128)(2,1)S(1)} %copy-done.4, bf16[4096,256]{1,0:T(8,128)(2,1)S(1)} %copy-done.2), kind=kOutput, calls=%fused_computation.3 | convolution fusion | flops 2153774848 | bytes 13108224 | tf_op jit(solution)/shard_map/dot_general | solution.py:314
  46.3 0.0 copy-start.3
  46.3 7.1 %shard_map.71.field_ref = bf16[5120,256]{1,0:T(8,128)(2,1)S(1)} custom-call(bf16[4096,256]{1,0:T(8,128)(2,1)S(1)} %get-tuple-element.6.field_ref), custom_call_target="tpu_custom_call" | custom-call | bytes 8388608 | tf_op jit(solution)/shard_map/pallas_call | solution.py:99
  53.4 0.0 slice-done
  53.4 0.0 slice-done.1
  53.4 3.2 %shard_map.72 = bf16[4096,256]{1,0:T(8,128)(2,1)S(1)} custom-call(s32[16,4]{1,0:T(8,128)S(1)} %copy.7.off_ref, bf16[16,4,256,256]{3,2,1,0:T(8,128)(2,1)S(1)} %bitcast.18, bf16[5120,256]{1,0:T(8,128)(2,1)S(1)} %shard_map.71.field_ref), custom_call_target="tpu_custom_call" | custom-call | flops 2147483648 | bytes 13107200 | tf_op jit(solution)/shard_map/pallas_call | solution.py:136
  56.6 0.0 copy-done.3
  56.6 2.3 %convolution_bitcast_fusion.1 = f32[1024,256]{0,1:T(8,128)S(1)} fusion(bf16[4096,256]{1,0:T(8,128)(2,1)S(1)} %shard_map.72, bf16[4096,1024]{1,0:T(8,128)(2,1)S(1)} %copy-done.4), kind=kOutput, calls=%fused_computation.4 | convolution fusion | flops 2147483648 | bytes 11534336 | tf_op jit(solution)/shard_map/dot_general | solution.py:321
  59.0 0.3 copy.10
  59.3 0.1 pad_maximum_fusion.x_ref
  59.4 12.8 %shard_map.73 = bf16[64,256]{1,0:T(8,128)(2,1)S(1)} custom-call(f32[8,2,72,256]{3,2,1,0:T(8,128)S(1)} %pad_maximum_fusion.x_ref), custom_call_target="tpu_custom_call" | custom-call | bytes 9437184 | tf_op jit(solution)/shard_map/pallas_call | solution.py:291
  72.3 0.6 copy.13
  (2 shorter events, 0.0 us)
Async XLA Ops:
  1.4 1.6 %copy-start.1 = (bf16[4096,256]{1,0:T(8,128)(2,1)S(1)}, bf16[4096,256]{1,0:T(8,128)(2,1)}, u32[]{:S(2)}) copy-start(bf16[4096,256]{1,0:T(8,128)(2,1)} %field_ref.1) | copy-start | bytes 6291460
  12.3 3.4 %copy-start = (bf16[16,4,256,256]{3,2,1,0:T(8,128)(2,1)S(1)}, bf16[16,4,256,256]{3,2,1,0:T(8,128)(2,1)}, u32[]{:S(2)}) copy-start(bf16[16,4,256,256]{3,2,1,0:T(8,128)(2,1)} %blk_ref.2) | copy-start | bytes 25165828
  15.7 3.4 %copy-start.4 = (bf16[4096,1024]{1,0:T(8,128)(2,1)S(1)}, bf16[4096,1024]{1,0:T(8,128)(2,1)}, u32[]{:S(2)}) copy-start(bf16[4096,1024]{1,0:T(8,128)(2,1)} %param.6) | copy-start | bytes 25165828
  19.1 24.4 %copy-start.2 = (bf16[4096,256]{1,0:T(8,128)(2,1)S(1)}, bf16[4096,256]{1,0:T(8,128)(2,1)}, u32[]{:S(2)}) copy-start(bf16[4096,256]{1,0:T(8,128)(2,1)} %field_ref.1) | copy-start | bytes 6291460
  43.4 9.9 %slice-start = ((s8[8388608]{0:T(1024)(128)(4,1)}), s8[4194304]{0:T(1024)(128)(4,1)S(1)}, s32[]{:S(2)}) async-start(s8[8388608]{0:T(1024)(128)(4,1)} %bitcast.17), calls=%async_computation | async-start | bytes 8388608
  43.5 9.9 %slice-start.1 = ((s8[8388608]{0:T(1024)(128)(4,1)}), s8[4194304]{0:T(1024)(128)(4,1)S(1)}, s32[]{:S(2)}) async-start(s8[8388608]{0:T(1024)(128)(4,1)} %bitcast.17), calls=%async_computation.1 | async-start | bytes 8388608
  46.3 10.4 %copy-start.3 = (bf16[4096,256]{1,0:T(8,128)(2,1)}, bf16[4096,256]{1,0:T(8,128)(2,1)S(1)}, u32[]{:S(2)}) copy-start(bf16[4096,256]{1,0:T(8,128)(2,1)S(1)} %get-tuple-element.6.field_ref) | copy-start | bytes 6291460

commit v13 on v11

--- a/solution.py
+++ b/solution.py
@@ -133,7 +133,10 @@
         pl.semaphore_signal(barrier, inc=1, device_id=(me + 1, orb), device_id_type=MESH)
 
     def tile(start):
-        removed = jnp.dot(tgt_ref[pl.ds(start, edge), :], proj_ref[...], preferred_element_type=jnp.float32)
+        removed = lax.dot_general(
+            tgt_ref[pl.ds(start, edge), :], proj_ref[...], (((1,), (1,)), ((), ())),
+            preferred_element_type=jnp.float32,
+        )
         orth = (cont_ref[pl.ds(start, edge), :].astype(jnp.float32) - removed).astype(orth_ref.dtype)
         orth_ref[pl.ds(start, edge), :] = orth
         pad_ref[pl.ds(start + edge, edge), :] = orth
@@ -416,12 +419,12 @@
     count = band_offsets.shape[0] * BK * n
     cont_padded = with_halo(cont_orbitals, 2)
     margin_cont = band_local(margin_blocks, band_offsets, cont_padded)
-    partial_proj = lax.dot_general(
-        target_orbitals, margin_cont, (((0,), (0,)), ((), ())), preferred_element_type=jnp.float32
-    )
-    projection_b = allreduce_to_bf16(partial_proj, n)
+    partial_proj_t = lax.dot_general(
+        margin_cont, target_orbitals, (((0,), (0,)), ((), ())), preferred_element_type=jnp.float32
+    )
+    projection_b_t = allreduce_to_bf16(partial_proj_t, n)
     cont_orth, orth_padded, squares = orthogonalize_with_halo(
-        target_orbitals, projection_b, cont_orbitals, 3
+        target_orbitals, projection_b_t, cont_orbitals, 3
     )
     dipole_cont = band_local(dipole_blocks, band_offsets, orth_padded)
     partial_dip = lax.dot_general(

time: 82.2 us -> 73.8 us (0.90)
  local copies, waits for them, and re-layouts: 17.8 us -> 9.01 us
  other arithmetic: 0.08 us -> 1.33 us
  matrix products: 5.67 us -> 4.7 us
    unnamed x25 -> x17, local copies, waits for them, and re-layouts: 15.8 us -> 7.69 us
    dot_general x1 -> x0, local copies, waits for them, and re-layouts: 1.7 us -> none  [on_device(): lax.dot_general(target_orbitals, margin_cont, (((0,), (0,)), ((), ())), p...]
    concatenate x1, other arithmetic: 0.08 us -> 1.33 us  [dipole_scatter(): jnp.concatenate([partial.reshape(nchip, 2, chunk, cols), jnp.broadcast_to...]
    dot_general x1, local copies, waits for them, and re-layouts: 0.33 us -> 1.31 us  [on_device(): lax.dot_general(target_orbitals, dipole_cont, (((0,), (0,)), ((), ())), p...]
    dot_general x1, matrix products: 3.32 us -> 2.36 us  [on_device(): lax.dot_general(margin_cont, target_orbitals, (((0,), (0,)), ((), ())), p...]
where the time goes in v13:
time: 73.8 us; the launch traced here: 73.5 us
  Pallas kernels  57.7 us (78%)
  local copies, waits for them, and re-layouts  9.01 us (12%)
  matrix products  4.7 us (6%)
  other arithmetic  1.33 us (2%)
  between operations  0.78 us (1%)
    pallas_call x1, Pallas kernels, allreduce_to_bf16(): pl.pallas_call(functools.partial(allreduce_kernel, nchip), out_shape=jax....  22 us
    pallas_call x1, Pallas kernels, dipole_scatter(): pl.pallas_call(functools.partial(dipole_kernel, nchip, chunk, count), out...  12.9 us
    pallas_call x1, Pallas kernels, with_halo(): pl.pallas_call(functools.partial(halo_kernel, n), out_shape=jax.ShapeDtyp...  9.34 us
    unnamed x17, local copies, waits for them, and re-layouts  7.69 us
    pallas_call x1, Pallas kernels, orthogonalize_with_halo(): pl.pallas_call(functools.partial(orth_halo_kernel, n), out_shape=(jax.Sha...  7.1 us
    pallas_call x2, Pallas kernels, band_local(): pl.pallas_call(functools.partial(band_kernel, per), out_shape=jax.ShapeDt...  6.43 us
    dot_general x1, matrix products, on_device(): lax.dot_general(margin_cont, target_orbitals, (((0,), (0,)), ((), ())), p...  2.36 us
    dot_general x1, matrix products, on_device(): lax.dot_general(target_orbitals, dipole_cont, (((0,), (0,)), ((), ())), p...  2.34 us

profile of v13, /device:TPU:1, one launch (start us, length us, event | category | flops | bytes accessed | tf_op | source)
XLA Modules:
  0.0 73.5 jit_solution(4064321205229681007)
XLA Ops:
  0.6 0.8 %copy.7.off_ref = s32[16,4]{1,0:T(8,128)S(1)} copy(s32[16,4]{0,1:T(4,128)} %param.9) | data formatting | bytes 512 | tf_op args[4]
  1.4 0.0 copy-start.1
  1.4 1.6 %copy-done.1 = bf16[4096,256]{1,0:T(8,128)(2,1)S(1)} copy-done((bf16[4096,256]{1,0:T(8,128)(2,1)S(1)}, bf16[4096,256]{1,0:T(8,128)(2,1)}, u32[]{:S(2)}) %copy-start.1) | copy-done | bytes 2097176
  3.0 0.0 slice-start
  3.0 9.3 %shard_map.68.field_ref = bf16[5120,256]{1,0:T(8,128)(2,1)S(1)} custom-call(bf16[4096,256]{1,0:T(8,128)(2,1)S(1)} %copy-done.1), custom_call_target="tpu_custom_call" | custom-call | bytes 8388608 | tf_op jit(solution)/shard_map/pallas_call | solution.py:99
  12.3 0.0 copy-start
  12.3 3.4 %copy-done = bf16[16,4,256,256]{3,2,1,0:T(8,128)(2,1)S(1)} copy-done((bf16[16,4,256,256]{3,2,1,0:T(8,128)(2,1)S(1)}, bf16[16,4,256,256]{3,2,1,0:T(8,128)(2,1)}, u32[]{:S(2)}) %copy-start) | copy-done | bytes 8388632
  15.7 0.0 slice-start.1
  15.7 0.0 slice-start.2
  15.7 3.2 %shard_map.69 = bf16[4096,256]{1,0:T(8,128)(2,1)S(1)} custom-call(s32[16,4]{1,0:T(8,128)S(1)} %copy.7.off_ref, bf16[16,4,256,256]{3,2,1,0:T(8,128)(2,1)S(1)} %copy-done, bf16[5120,256]{1,0:T(8,128)(2,1)S(1)} %shard_map.68.field_ref), custom_call_target="tpu_custom_call" | custom-call | flops 2147483648 | bytes 13107200 | tf_op jit(solution)/shard_map/pallas_call | solution.py:248
  18.9 0.0 slice-done
  19.0 0.0 slice-done.1
  19.0 0.0 copy-start.2
  19.0 0.0 slice-start.3
  19.0 2.4 %fusion = f32[256,1024]{1,0:T(8,128)S(1)} fusion(bf16[4096,256]{1,0:T(8,128)(2,1)S(1)} %shard_map.69, bf16[4096,1024]{1,0:T(8,128)(2,1)S(1)} %bitcast.11), kind=kOutput, calls=%fused_computation.2 | convolution fusion | flops 2147483648 | bytes 11534336 | tf_op jit(solution)/shard_map/dot_general | solution.py:422
  21.4 22.0 %shard_map.70 = bf16[8,2,16,1024]{3,2,1,0:T(8,128)(2,1)S(1)} custom-call(f32[8,2,16,1024]{3,2,1,0:T(8,128)S(1)} %bitcast.14), custom_call_target="tpu_custom_call" | custom-call | bytes 16777216 | tf_op jit(solution)/shard_map/pallas_call | solution.py:366
  43.3 0.0 copy-done.2
  43.3 7.1 %shard_map.71 = (bf16[4096,256]{1,0:T(8,128)(2,1)S(1)}, bf16[5120,256]{1,0:T(8,128)(2,1)S(1)}, f32[1,256]{1,0:T(1,128)S(1)}) custom-call(bf16[4096,1024]{1,0:T(8,128)(2,1)S(1)} %bitcast.11, bf16[256,1024]{1,0:T(8,128)(2,1)S(1)} %bitcast.15, bf16[4096,256]{1,0:T(8,128)(2,1)S(1)} %copy-done.2), custom_call_target="tpu_custom_call" | custom-call | flops 2147483648 | bytes 15204352 | tf_op jit(solution)/shard_map/pallas_call | solution.py:203
  50.5 0.0 slice-done.2
  50.5 0.0 slice-done.3
  50.5 3.2 %shard_map.72 = bf16[4096,256]{1,0:T(8,128)(2,1)S(1)} custom-call(s32[16,4]{1,0:T(8,128)S(1)} %copy.7.off_ref, bf16[16,4,256,256]{3,2,1,0:T(8,128)(2,1)S(1)} %bitcast.13, bf16[5120,256]{1,0:T(8,128)(2,1)S(1)} %get-tuple-element.6.field_ref), custom_call_target="tpu_custom_call" | custom-call | flops 2147483648 | bytes 13107200 | tf_op jit(solution)/shard_map/pallas_call | solution.py:248
  53.7 2.3 %convolution_bitcast_fusion = f32[1024,256]{0,1:T(8,128)S(1)} fusion(bf16[4096,256]{1,0:T(8,128)(2,1)S(1)} %shard_map.72, bf16[4096,1024]{1,0:T(8,128)(2,1)S(1)} %bitcast.11), kind=kOutput, calls=%fused_computation | convolution fusion | flops 2147483648 | bytes 11534336 | tf_op jit(solution)/shard_map/dot_general | solution.py:430
  56.1 1.3 %copy.9 = f32[1024,256]{1,0:T(8,128)} copy(f32[1024,256]{0,1:T(8,128)S(1)} %convolution_bitcast_fusion) | data formatting | bytes 2097152 | tf_op jit(solution)/shard_map/dot_general | solution.py:430
  57.4 1.3 %pad_maximum_fusion.x_ref = f32[8,2,72,256]{3,2,1,0:T(8,128)S(1)} fusion(f32[8,2,8,256]{3,2,1,0:T(8,128)S(1)} %broadcast_in_dim.8, f32[8,2,64,256]{3,2,1,0:T(8,128)} %bitcast.17), kind=kLoop, calls=%fused_computation.1 | loop fusion | flops 294912 | bytes 2359296 | tf_op jit(solution)/shard_map/concatenate | solution.py:396
  58.7 12.9 %shard_map.73 = bf16[64,256]{1,0:T(8,128)(2,1)S(1)} custom-call(f32[8,2,72,256]{3,2,1,0:T(8,128)S(1)} %pad_maximum_fusion.x_ref), custom_call_target="tpu_custom_call" | custom-call | bytes 9437184 | tf_op jit(solution)/shard_map/pallas_call | solution.py:403
  71.6 1.3 %copy.12 = bf16[4096,256]{1,0:T(8,128)(2,1)} copy(bf16[4096,256]{1,0:T(8,128)(2,1)S(1)} %get-tuple-element.10) | data formatting | bytes 4194304
  72.9 0.6 copy.13
  (3 shorter events, 0.0 us)
Async XLA Ops:
  1.4 1.6 %copy-start.1 = (bf16[4096,256]{1,0:T(8,128)(2,1)S(1)}, bf16[4096,256]{1,0:T(8,128)(2,1)}, u32[]{:S(2)}) copy-start(bf16[4096,256]{1,0:T(8,128)(2,1)} %cont_ref.1) | copy-start | bytes 6291460
  3.0 16.0 %slice-start = ((s8[8388608]{0:T(1024)(128)(4,1)}), s8[4194304]{0:T(1024)(128)(4,1)S(1)}, s32[]{:S(2)}) async-start(s8[8388608]{0:T(1024)(128)(4,1)} %bitcast.10), calls=%async_computation | async-start | bytes 8388608
  12.3 3.4 %copy-start = (bf16[16,4,256,256]{3,2,1,0:T(8,128)(2,1)S(1)}, bf16[16,4,256,256]{3,2,1,0:T(8,128)(2,1)}, u32[]{:S(2)}) copy-start(bf16[16,4,256,256]{3,2,1,0:T(8,128)(2,1)} %blk_ref.2) | copy-start | bytes 25165828
  15.7 3.2 %slice-start.1 = ((s8[8388608]{0:T(1024)(128)(4,1)}), s8[4194304]{0:T(1024)(128)(4,1)S(1)}, s32[]{:S(2)}) async-start(s8[8388608]{0:T(1024)(128)(4,1)} %bitcast.10), calls=%async_computation.1 | async-start | bytes 8388608
  15.7 34.7 %slice-start.2 = ((s8[8388608]{0:T(1024)(128)(4,1)}), s8[4194304]{0:T(1024)(128)(4,1)S(1)}, s32[]{:S(2)}) async-start(s8[8388608]{0:T(1024)(128)(4,1)} %bitcast.12), calls=%async_computation.2 | async-start | bytes 8388608
  19.0 24.4 %copy-start.2 = (bf16[4096,256]{1,0:T(8,128)(2,1)S(1)}, bf16[4096,256]{1,0:T(8,128)(2,1)}, u32[]{:S(2)}) copy-start(bf16[4096,256]{1,0:T(8,128)(2,1)} %cont_ref.1) | copy-start | bytes 6291460
  19.0 31.5 %slice-start.3 = ((s8[8388608]{0:T(1024)(128)(4,1)}), s8[4194304]{0:T(1024)(128)(4,1)S(1)}, s32[]{:S(2)}) async-start(s8[8388608]{0:T(1024)(128)(4,1)} %bitcast.12), calls=%async_computation.3 | async-start | bytes 8388608

commit v14 on v13

--- a/solution.py
+++ b/solution.py
@@ -115,7 +115,7 @@
     )(field)
 
 
-def orth_halo_kernel(n, tgt_ref, proj_ref, cont_ref, orth_ref, pad_ref, sq_ref, low, high, send_sem, recv_sem):
+def orth_halo_kernel(n, tgt_ref, proj_ref, cont_ref, pad_ref, sq_ref, orth_ref, low, high, send_sem, recv_sem):
     rows, width = cont_ref.shape
     edge = 2 * BK
     me = lax.axis_index("basis")
@@ -200,16 +200,16 @@
     width = cont.shape[1]
     n = lax.axis_size("basis")
     vmem = pl.BlockSpec(memory_space=pltpu.VMEM)
-    orth, padded, squares = pl.pallas_call(
+    padded, squares = pl.pallas_call(
         functools.partial(orth_halo_kernel, n),
         out_shape=(
-            jax.ShapeDtypeStruct((rows, width), jnp.bfloat16),
             jax.ShapeDtypeStruct((rows + 4 * BK, width), jnp.bfloat16),
             jax.ShapeDtypeStruct((1, width), jnp.float32),
         ),
         in_specs=[vmem, vmem, vmem],
-        out_specs=(vmem, vmem, vmem),
+        out_specs=(vmem, vmem),
         scratch_shapes=[
+            pltpu.VMEM((rows, width), jnp.bfloat16),
             pltpu.VMEM((2 * BK, width), jnp.bfloat16),
             pltpu.VMEM((2 * BK, width), jnp.bfloat16),
             pltpu.SemaphoreType.DMA((2,)),
@@ -224,11 +224,14 @@
             collective_id=collective_id, has_side_effects=True, vmem_limit_bytes=24 * 1024 * 1024
         ),
     )(target, projection_b, cont)
-    return orth, padded, squares[0]
-
-
-def band_kernel(rows_per_step, off_ref, blk_ref, field_ref, out_ref):
+    return padded, squares[0]
+
+
+def band_kernel(rows_per_step, off_ref, blk_ref, field_ref, out_ref, *mid):
     g = pl.program_id(0)
+    if mid:
+        start = pl.multiple_of((g * rows_per_step + 2) * BK, BK)
+        mid[0][...] = field_ref[pl.ds(start, rows_per_step * BK), :]
     for r in range(rows_per_step):
         b = g * rows_per_step + r
         acc = None
@@ -241,13 +244,15 @@
         out_ref[pl.ds(r * BK, BK), :] = acc.astype(out_ref.dtype)
 
 
-def band_local(blocks, offsets, padded):
+def band_local(blocks, offsets, padded, with_middle=False):
     nblk = blocks.shape[0]
     rows, width = padded.shape
     per = 8 if nblk % 8 == 0 else 1
+    field = jax.ShapeDtypeStruct((nblk * BK, width), jnp.bfloat16)
+    spec = pl.BlockSpec((per * BK, width), lambda g, off: (g, 0))
     return pl.pallas_call(
         functools.partial(band_kernel, per),
-        out_shape=jax.ShapeDtypeStruct((nblk * BK, width), jnp.bfloat16),
+        out_shape=(field, field) if with_middle else field,
         grid_spec=pltpu.PrefetchScalarGridSpec(
             num_scalar_prefetch=1,
             grid=(nblk // per,),
@@ -255,7 +260,7 @@
                 pl.BlockSpec((per, KB, BK, BK), lambda g, off: (g, 0, 0, 0)),
                 pl.BlockSpec((rows, width), lambda g, off: (0, 0)),
             ],
-            out_specs=pl.BlockSpec((per * BK, width), lambda g, off: (g, 0)),
+            out_specs=(spec, spec) if with_middle else spec,
         ),
         cost_estimate=pl.CostEstimate(
             flops=2 * nblk * KB * BK * BK * width,
@@ -423,10 +428,10 @@
         margin_cont, target_orbitals, (((0,), (0,)), ((), ())), preferred_element_type=jnp.float32
     )
     projection_b_t = allreduce_to_bf16(partial_proj_t, n)
-    cont_orth, orth_padded, squares = orthogonalize_with_halo(
+    orth_padded, squares = orthogonalize_with_halo(
         target_orbitals, projection_b_t, cont_orbitals, 3
     )
-    dipole_cont = band_local(dipole_blocks, band_offsets, orth_padded)
+    dipole_cont, cont_orth = band_local(dipole_blocks, band_offsets, orth_padded, True)
     partial_dip = lax.dot_general(
         target_orbitals,
         dipole_cont,

time: 73.8 us -> 71.4 us (0.967)
  local copies, waits for them, and re-layouts: 9.01 us -> 6.71 us
  other arithmetic: 1.33 us -> 0.08 us
  Pallas kernels: 57.7 us -> 58.9 us
    unnamed x17 -> x16, local copies, waits for them, and re-layouts: 7.69 us -> 6.37 us
    concatenate x1, other arithmetic: 1.33 us -> 0.08 us  [dipole_scatter(): jnp.concatenate([partial.reshape(nchip, 2, chunk, cols), jnp.broadcast_to...]
    pallas_call x2, Pallas kernels: 6.43 us -> 7.49 us  [band_local(): pl.pallas_call(functools.partial(band_kernel, per), out_shape=(field, fie...]
    dot_general x1, local copies, waits for them, and re-layouts: 1.31 us -> 0.33 us  [on_device(): lax.dot_general(target_orbitals, dipole_cont, (((0,), (0,)), ((), ())), p...]
where the time goes in v14:
time: 71.4 us; the launch traced here: 71.2 us
  Pallas kernels  58.9 us (82%)
  local copies, waits for them, and re-layouts  6.71 us (9%)
  matrix products  4.74 us (7%)
  between operations  0.78 us (1%)
    pallas_call x1, Pallas kernels, allreduce_to_bf16(): pl.pallas_call(functools.partial(allreduce_kernel, nchip), out_shape=jax....  22 us
    pallas_call x1, Pallas kernels, dipole_scatter(): pl.pallas_call(functools.partial(dipole_kernel, nchip, chunk, count), out...  12.9 us
    pallas_call x1, Pallas kernels, with_halo(): pl.pallas_call(functools.partial(halo_kernel, n), out_shape=jax.ShapeDtyp...  9.34 us
    pallas_call x2, Pallas kernels, band_local(): pl.pallas_call(functools.partial(band_kernel, per), out_shape=(field, fie...  7.49 us
    pallas_call x1, Pallas kernels, orthogonalize_with_halo(): pl.pallas_call(functools.partial(orth_halo_kernel, n), out_shape=(jax.Sha...  7.11 us
    unnamed x16, local copies, waits for them, and re-layouts  6.37 us
    dot_general x1, matrix products, on_device(): lax.dot_general(margin_cont, target_orbitals, (((0,), (0,)), ((), ())), p...  2.37 us
    dot_general x1, matrix products, on_device(): lax.dot_general(target_orbitals, dipole_cont, (((0,), (0,)), ((), ())), p...  2.37 us

profile of v14, /device:TPU:1, one launch (start us, length us, event | category | flops | bytes accessed | tf_op | source)
XLA Modules:
  0.0 71.2 jit_solution(10052068558976835649)
XLA Ops:
  0.6 0.8 %copy.8.off_ref = s32[16,4]{1,0:T(8,128)S(1)} copy(s32[16,4]{0,1:T(4,128)} %param.9) | data formatting | bytes 512 | tf_op args[4]
  1.4 0.0 copy-start.1
  1.4 1.6 %copy-done.1 = bf16[4096,256]{1,0:T(8,128)(2,1)S(1)} copy-done((bf16[4096,256]{1,0:T(8,128)(2,1)S(1)}, bf16[4096,256]{1,0:T(8,128)(2,1)}, u32[]{:S(2)}) %copy-start.1) | copy-done | bytes 2097176
  3.0 0.0 slice-start
  3.0 9.3 %shard_map.68.field_ref = bf16[5120,256]{1,0:T(8,128)(2,1)S(1)} custom-call(bf16[4096,256]{1,0:T(8,128)(2,1)S(1)} %copy-done.1), custom_call_target="tpu_custom_call" | custom-call | bytes 8388608 | tf_op jit(solution)/shard_map/pallas_call | solution.py:99
  12.3 0.0 copy-start
  12.3 3.4 %copy-done = bf16[16,4,256,256]{3,2,1,0:T(8,128)(2,1)S(1)} copy-done((bf16[16,4,256,256]{3,2,1,0:T(8,128)(2,1)S(1)}, bf16[16,4,256,256]{3,2,1,0:T(8,128)(2,1)}, u32[]{:S(2)}) %copy-start) | copy-done | bytes 8388632
  15.7 0.0 slice-start.1
  15.7 0.0 slice-start.2
  15.7 3.3 %shard_map.69 = bf16[4096,256]{1,0:T(8,128)(2,1)S(1)} custom-call(s32[16,4]{1,0:T(8,128)S(1)} %copy.8.off_ref, bf16[16,4,256,256]{3,2,1,0:T(8,128)(2,1)S(1)} %copy-done, bf16[5120,256]{1,0:T(8,128)(2,1)S(1)} %shard_map.68.field_ref), custom_call_target="tpu_custom_call" | custom-call | flops 2147483648 | bytes 13107200 | tf_op jit(solution)/shard_map/pallas_call | solution.py:253
  19.0 0.0 slice-done
  19.0 0.0 slice-done.1
  19.0 0.0 copy-start.2
  19.0 0.0 slice-start.3
  19.1 2.4 %fusion = f32[256,1024]{1,0:T(8,128)S(1)} fusion(bf16[4096,256]{1,0:T(8,128)(2,1)S(1)} %shard_map.69, bf16[4096,1024]{1,0:T(8,128)(2,1)S(1)} %bitcast.11), kind=kOutput, calls=%fused_computation.2 | convolution fusion | flops 2147483648 | bytes 11534336 | tf_op jit(solution)/shard_map/dot_general | solution.py:427
  21.4 22.0 %shard_map.70 = bf16[8,2,16,1024]{3,2,1,0:T(8,128)(2,1)S(1)} custom-call(f32[8,2,16,1024]{3,2,1,0:T(8,128)S(1)} %bitcast.14), custom_call_target="tpu_custom_call" | custom-call | bytes 16777216 | tf_op jit(solution)/shard_map/pallas_call | solution.py:371
  43.4 0.0 copy-done.2
  43.4 7.1 %shard_map.71 = (bf16[5120,256]{1,0:T(8,128)(2,1)S(1)}, f32[1,256]{1,0:T(1,128)S(1)}) custom-call(bf16[4096,1024]{1,0:T(8,128)(2,1)S(1)} %bitcast.11, bf16[256,1024]{1,0:T(8,128)(2,1)S(1)} %bitcast.15, bf16[4096,256]{1,0:T(8,128)(2,1)S(1)} %copy-done.2), custom_call_target="tpu_custom_call" | custom-call | flops 2147483648 | bytes 15204352 | tf_op jit(solution)/shard_map/pallas_call | solution.py:203
  50.6 0.0 slice-done.2
  50.6 0.0 slice-done.3
  50.6 4.2 %shard_map.72 = (bf16[4096,256]{1,0:T(8,128)(2,1)S(1)}, bf16[4096,256]{1,0:T(8,128)(2,1)}) custom-call(s32[16,4]{1,0:T(8,128)S(1)} %copy.8.off_ref, bf16[16,4,256,256]{3,2,1,0:T(8,128)(2,1)S(1)} %bitcast.13, bf16[5120,256]{1,0:T(8,128)(2,1)S(1)} %get-tuple-element.6.field_ref), custom_call_target="tpu_custom_call" | custom-call | flops 2147483648 | bytes 13107200 | tf_op jit(solution)/shard_map/pallas_call | solution.py:253
  54.8 2.4 %convolution_bitcast_fusion = f32[1024,256]{0,1:T(8,128)S(1)} fusion(bf16[4096,256]{1,0:T(8,128)(2,1)S(1)} %get-tuple-element.8, bf16[4096,1024]{1,0:T(8,128)(2,1)S(1)} %bitcast.11), kind=kOutput, calls=%fused_computation | convolution fusion | flops 2147483648 | bytes 11534336 | tf_op jit(solution)/shard_map/dot_general | solution.py:435
  57.2 0.3 copy.9
  57.5 0.1 pad_maximum_fusion.x_ref
  57.6 12.9 %shard_map.73 = bf16[64,256]{1,0:T(8,128)(2,1)S(1)} custom-call(f32[8,2,72,256]{3,2,1,0:T(8,128)S(1)} %pad_maximum_fusion.x_ref), custom_call_target="tpu_custom_call" | custom-call | bytes 9437184 | tf_op jit(solution)/shard_map/pallas_call | solution.py:408
  70.6 0.6 copy.11
  (3 shorter events, 0.0 us)
Async XLA Ops:
  1.4 1.6 %copy-start.1 = (bf16[4096,256]{1,0:T(8,128)(2,1)S(1)}, bf16[4096,256]{1,0:T(8,128)(2,1)}, u32[]{:S(2)}) copy-start(bf16[4096,256]{1,0:T(8,128)(2,1)} %cont_ref.1) | copy-start | bytes 6291460
  3.0 16.0 %slice-start = ((s8[8388608]{0:T(1024)(128)(4,1)}), s8[4194304]{0:T(1024)(128)(4,1)S(1)}, s32[]{:S(2)}) async-start(s8[8388608]{0:T(1024)(128)(4,1)} %bitcast.10), calls=%async_computation | async-start | bytes 8388608
  12.3 3.4 %copy-start = (bf16[16,4,256,256]{3,2,1,0:T(8,128)(2,1)S(1)}, bf16[16,4,256,256]{3,2,1,0:T(8,128)(2,1)}, u32[]{:S(2)}) copy-start(bf16[16,4,256,256]{3,2,1,0:T(8,128)(2,1)} %blk_ref.2) | copy-start | bytes 25165828
  15.7 3.3 %slice-start.1 = ((s8[8388608]{0:T(1024)(128)(4,1)}), s8[4194304]{0:T(1024)(128)(4,1)S(1)}, s32[]{:S(2)}) async-start(s8[8388608]{0:T(1024)(128)(4,1)} %bitcast.10), calls=%async_computation.1 | async-start | bytes 8388608
  15.7 34.8 %slice-start.2 = ((s8[8388608]{0:T(1024)(128)(4,1)}), s8[4194304]{0:T(1024)(128)(4,1)S(1)}, s32[]{:S(2)}) async-start(s8[8388608]{0:T(1024)(128)(4,1)} %bitcast.12), calls=%async_computation.2 | async-start | bytes 8388608
  19.0 24.4 %copy-start.2 = (bf16[4096,256]{1,0:T(8,128)(2,1)S(1)}, bf16[4096,256]{1,0:T(8,128)(2,1)}, u32[]{:S(2)}) copy-start(bf16[4096,256]{1,0:T(8,128)(2,1)} %cont_ref.1) | copy-start | bytes 6291460
  19.0 31.5 %slice-start.3 = ((s8[8388608]{0:T(1024)(128)(4,1)}), s8[4194304]{0:T(1024)(128)(4,1)S(1)}, s32[]{:S(2)}) async-start(s8[8388608]{0:T(1024)(128)(4,1)} %bitcast.12), calls=%async_computation.3 | async-start | bytes 8388608

commit v15 on v14

--- a/solution.py
+++ b/solution.py
@@ -236,7 +236,7 @@
         b = g * rows_per_step + r
         acc = None
         for k in range(KB):
-            start = pl.multiple_of((b + 2 + off_ref[b, k]) * BK, BK)
+            start = pl.multiple_of((b + 2 + off_ref[k, b]) * BK, BK)
             term = jnp.dot(
                 blk_ref[r, k], field_ref[pl.ds(start, BK), :], preferred_element_type=jnp.float32
             )
@@ -268,7 +268,7 @@
             transcendentals=0,
         ),
         compiler_params=pltpu.CompilerParams(vmem_limit_bytes=24 * 1024 * 1024),
-    )(offsets, blocks, padded)
+    )(offsets.T, blocks, padded)
 
 
 def _place():

time: 71.4 us -> 70.3 us (0.985)
  local copies, waits for them, and re-layouts: 6.71 us -> 5.95 us
    unnamed x16 -> x17, local copies, waits for them, and re-layouts: 6.37 us -> 5.61 us
where the time goes in v15:
time: 70.3 us; the launch traced here: 70.2 us
  Pallas kernels  58.6 us (83%)
  local copies, waits for them, and re-layouts  5.95 us (8%)
  matrix products  4.69 us (7%)
  between operations  0.8 us (1%)
    pallas_call x1, Pallas kernels, allreduce_to_bf16(): pl.pallas_call(functools.partial(allreduce_kernel, nchip), out_shape=jax....  22 us
    pallas_call x1, Pallas kernels, dipole_scatter(): pl.pallas_call(functools.partial(dipole_kernel, nchip, chunk, count), out...  12.9 us
    pallas_call x1, Pallas kernels, with_halo(): pl.pallas_call(functools.partial(halo_kernel, n), out_shape=jax.ShapeDtyp...  9.34 us
    pallas_call x2, Pallas kernels, band_local(): pl.pallas_call(functools.partial(band_kernel, per), out_shape=(field, fie...  7.25 us
    pallas_call x1, Pallas kernels, orthogonalize_with_halo(): pl.pallas_call(functools.partial(orth_halo_kernel, n), out_shape=(jax.Sha...  7.11 us
    unnamed x17, local copies, waits for them, and re-layouts  5.61 us
    dot_general x1, matrix products, on_device(): lax.dot_general(margin_cont, target_orbitals, (((0,), (0,)), ((), ())), p...  2.35 us
    dot_general x1, matrix products, on_device(): lax.dot_general(target_orbitals, dipole_cont, (((0,), (0,)), ((), ())), p...  2.34 us

profile of v15, /device:TPU:1, one launch (start us, length us, event | category | flops | bytes accessed | tf_op | source)
XLA Modules:
  0.0 70.2 jit_solution(8960496023328048886)
XLA Ops:
  0.6 0.0 copy-start.1
  0.6 1.6 %copy-done.1 = bf16[4096,256]{1,0:T(8,128)(2,1)S(1)} copy-done((bf16[4096,256]{1,0:T(8,128)(2,1)S(1)}, bf16[4096,256]{1,0:T(8,128)(2,1)}, u32[]{:S(2)}) %copy-start.1) | copy-done | bytes 2097176
  2.2 0.0 copy-start.3
  2.2 0.0 slice-start
  2.2 9.3 %shard_map.68.field_ref = bf16[5120,256]{1,0:T(8,128)(2,1)S(1)} custom-call(bf16[4096,256]{1,0:T(8,128)(2,1)S(1)} %copy-done.1), custom_call_target="tpu_custom_call" | custom-call | bytes 8388608 | tf_op jit(solution)/shard_map/pallas_call | solution.py:99
  11.6 0.0 copy-done.3
  11.6 0.0 copy-start
  11.6 3.4 %copy-done = bf16[16,4,256,256]{3,2,1,0:T(8,128)(2,1)S(1)} copy-done((bf16[16,4,256,256]{3,2,1,0:T(8,128)(2,1)S(1)}, bf16[16,4,256,256]{3,2,1,0:T(8,128)(2,1)}, u32[]{:S(2)}) %copy-start) | copy-done | bytes 8388632
  15.0 0.0 slice-start.1
  15.0 0.0 slice-start.2
  15.0 3.2 %shard_map.69 = bf16[4096,256]{1,0:T(8,128)(2,1)S(1)} custom-call(s32[4,16]{1,0:T(4,128)S(1)} %bitcast.17, bf16[16,4,256,256]{3,2,1,0:T(8,128)(2,1)S(1)} %copy-done, bf16[5120,256]{1,0:T(8,128)(2,1)S(1)} %shard_map.68.field_ref), custom_call_target="tpu_custom_call" | custom-call | flops 2147483648 | bytes 13107200 | tf_op jit(solution)/shard_map/pallas_call | solution.py:253
  18.2 0.0 slice-done
  18.2 0.0 slice-done.1
  18.2 0.0 copy-start.2
  18.2 0.0 slice-start.3
  18.2 2.4 %fusion = f32[256,1024]{1,0:T(8,128)S(1)} fusion(bf16[4096,256]{1,0:T(8,128)(2,1)S(1)} %shard_map.69, bf16[4096,1024]{1,0:T(8,128)(2,1)S(1)} %bitcast.12), kind=kOutput, calls=%fused_computation.2 | convolution fusion | flops 2147483648 | bytes 11534336 | tf_op jit(solution)/shard_map/dot_general | solution.py:427
  20.6 22.0 %shard_map.70 = bf16[8,2,16,1024]{3,2,1,0:T(8,128)(2,1)S(1)} custom-call(f32[8,2,16,1024]{3,2,1,0:T(8,128)S(1)} %bitcast.15), custom_call_target="tpu_custom_call" | custom-call | bytes 16777216 | tf_op jit(solution)/shard_map/pallas_call | solution.py:371
  42.6 0.0 copy-done.2
  42.6 7.1 %shard_map.71 = (bf16[5120,256]{1,0:T(8,128)(2,1)S(1)}, f32[1,256]{1,0:T(1,128)S(1)}) custom-call(bf16[4096,1024]{1,0:T(8,128)(2,1)S(1)} %bitcast.12, bf16[256,1024]{1,0:T(8,128)(2,1)S(1)} %bitcast.16, bf16[4096,256]{1,0:T(8,128)(2,1)S(1)} %copy-done.2), custom_call_target="tpu_custom_call" | custom-call | flops 2147483648 | bytes 15204352 | tf_op jit(solution)/shard_map/pallas_call | solution.py:203
  49.7 0.0 slice-done.2
  49.7 0.0 slice-done.3
  49.7 4.1 %shard_map.72 = (bf16[4096,256]{1,0:T(8,128)(2,1)S(1)}, bf16[4096,256]{1,0:T(8,128)(2,1)}) custom-call(s32[4,16]{1,0:T(4,128)S(1)} %bitcast.18, bf16[16,4,256,256]{3,2,1,0:T(8,128)(2,1)S(1)} %bitcast.14, bf16[5120,256]{1,0:T(8,128)(2,1)S(1)} %get-tuple-element.6.field_ref), custom_call_target="tpu_custom_call" | custom-call | flops 2147483648 | bytes 13107200 | tf_op jit(solution)/shard_map/pallas_call | solution.py:253
  53.8 2.3 %convolution_bitcast_fusion = f32[1024,256]{0,1:T(8,128)S(1)} fusion(bf16[4096,256]{1,0:T(8,128)(2,1)S(1)} %get-tuple-element.8, bf16[4096,1024]{1,0:T(8,128)(2,1)S(1)} %bitcast.12), kind=kOutput, calls=%fused_computation | convolution fusion | flops 2147483648 | bytes 11534336 | tf_op jit(solution)/shard_map/dot_general | solution.py:435
  56.1 0.3 copy.7
  56.5 0.1 pad_maximum_fusion.x_ref
  56.6 12.9 %shard_map.73 = bf16[64,256]{1,0:T(8,128)(2,1)S(1)} custom-call(f32[8,2,72,256]{3,2,1,0:T(8,128)S(1)} %pad_maximum_fusion.x_ref), custom_call_target="tpu_custom_call" | custom-call | bytes 9437184 | tf_op jit(solution)/shard_map/pallas_call | solution.py:408
  69.5 0.6 copy.9
  (3 shorter events, 0.0 us)
Async XLA Ops:
  0.6 1.6 %copy-start.1 = (bf16[4096,256]{1,0:T(8,128)(2,1)S(1)}, bf16[4096,256]{1,0:T(8,128)(2,1)}, u32[]{:S(2)}) copy-start(bf16[4096,256]{1,0:T(8,128)(2,1)} %cont_ref.1) | copy-start | bytes 6291460
  2.2 9.4 %copy-start.3 = (s32[16,4]{0,1:T(4,128)S(1)}, s32[16,4]{0,1:T(4,128)}, u32[]{:S(2)}) copy-start(s32[16,4]{0,1:T(4,128)} %param.9) | copy-start | bytes 772
  2.2 15.9 %slice-start = ((s8[8388608]{0:T(1024)(128)(4,1)}), s8[4194304]{0:T(1024)(128)(4,1)S(1)}, s32[]{:S(2)}) async-start(s8[8388608]{0:T(1024)(128)(4,1)} %bitcast.11), calls=%async_computation | async-start | bytes 8388608
  11.6 3.4 %copy-start = (bf16[16,4,256,256]{3,2,1,0:T(8,128)(2,1)S(1)}, bf16[16,4,256,256]{3,2,1,0:T(8,128)(2,1)}, u32[]{:S(2)}) copy-start(bf16[16,4,256,256]{3,2,1,0:T(8,128)(2,1)} %blk_ref.2) | copy-start | bytes 25165828
  15.0 3.2 %slice-start.1 = ((s8[8388608]{0:T(1024)(128)(4,1)}), s8[4194304]{0:T(1024)(128)(4,1)S(1)}, s32[]{:S(2)}) async-start(s8[8388608]{0:T(1024)(128)(4,1)} %bitcast.11), calls=%async_computation.1 | async-start | bytes 8388608
  15.0 34.7 %slice-start.2 = ((s8[8388608]{0:T(1024)(128)(4,1)}), s8[4194304]{0:T(1024)(128)(4,1)S(1)}, s32[]{:S(2)}) async-start(s8[8388608]{0:T(1024)(128)(4,1)} %bitcast.13), calls=%async_computation.2 | async-start | bytes 8388608
  18.2 24.4 %copy-start.2 = (bf16[4096,256]{1,0:T(8,128)(2,1)S(1)}, bf16[4096,256]{1,0:T(8,128)(2,1)}, u32[]{:S(2)}) copy-start(bf16[4096,256]{1,0:T(8,128)(2,1)} %cont_ref.1) | copy-start | bytes 6291460
  18.2 31.5 %slice-start.3 = ((s8[8388608]{0:T(1024)(128)(4,1)}), s8[4194304]{0:T(1024)(128)(4,1)S(1)}, s32[]{:S(2)}) async-start(s8[8388608]{0:T(1024)(128)(4,1)} %bitcast.13), calls=%async_computation.3 | async-start | bytes 8388608

commit v16 on v15

--- a/solution.py
+++ b/solution.py
@@ -388,10 +388,7 @@
 
 def dipole_kernel(nchip, chunk, count, x_ref, out_ref, pair_recv, part, chip_recv,
                   p_send, p_recv, c_send, c_recv):
-    total = _two_level_sum(nchip, x_ref, pair_recv, part, chip_recv, p_send, p_recv, c_send, c_recv)
-    squares = total[chunk:chunk + 1, :]
-    col_norm = 1.0 / jnp.sqrt(squares / count + 1e-06)
-    out_ref[...] = (total[:chunk, :] * col_norm).astype(out_ref.dtype)
+    out_ref[...] = _two_level_sum(nchip, x_ref, pair_recv, part, chip_recv, p_send, p_recv, c_send, c_recv)
 
 
 def dipole_scatter(partial, squares, n, count):
@@ -405,9 +402,9 @@
         ],
         axis=2,
     )
-    return pl.pallas_call(
+    total = pl.pallas_call(
         functools.partial(dipole_kernel, nchip, chunk, count),
-        out_shape=jax.ShapeDtypeStruct((chunk, cols), jnp.bfloat16),
+        out_shape=jax.ShapeDtypeStruct((chunk + 8, cols), jnp.float32),
         in_specs=[pl.BlockSpec(memory_space=pltpu.VMEM)],
         out_specs=pl.BlockSpec(memory_space=pltpu.VMEM),
         scratch_shapes=_two_level_scratch(nchip, chunk + 8, cols)
@@ -417,6 +414,8 @@
         ),
         cost_estimate=pl.CostEstimate(flops=0, bytes_accessed=32 * x.size, transcendentals=0),
     )(x)
+    col_norm = 1.0 / jnp.sqrt(total[chunk] / count + 1e-06)
+    return (total[:chunk] * col_norm[None, :]).astype(jnp.bfloat16)
 
 
 def on_device(cont_orbitals, target_orbitals, margin_blocks, dipole_blocks, band_offsets):

time: 70.3 us -> 70.3 us (level)
    unnamed x17 -> x16, local copies, waits for them, and re-layouts: 5.61 us -> 4.99 us
where the time goes in v16:
time: 70.3 us; the launch traced here: 70.2 us
  Pallas kernels  58.6 us (83%)
  local copies, waits for them, and re-layouts  5.34 us (8%)
  matrix products  4.69 us (7%)
  between operations  0.8 us (1%)
  other arithmetic  0.71 us (1%)
    pallas_call x1, Pallas kernels, allreduce_to_bf16(): pl.pallas_call(functools.partial(allreduce_kernel, nchip), out_shape=jax....  22 us
    pallas_call x1, Pallas kernels, dipole_scatter(): pl.pallas_call(functools.partial(dipole_kernel, nchip, chunk, count), out...  12.9 us
    pallas_call x1, Pallas kernels, with_halo(): pl.pallas_call(functools.partial(halo_kernel, n), out_shape=jax.ShapeDtyp...  9.34 us
    pallas_call x2, Pallas kernels, band_local(): pl.pallas_call(functools.partial(band_kernel, per), out_shape=(field, fie...  7.25 us
    pallas_call x1, Pallas kernels, orthogonalize_with_halo(): pl.pallas_call(functools.partial(orth_halo_kernel, n), out_shape=(jax.Sha...  7.11 us
    unnamed x16, local copies, waits for them, and re-layouts  4.99 us
    dot_general x1, matrix products, on_device(): lax.dot_general(margin_cont, target_orbitals, (((0,), (0,)), ((), ())), p...  2.35 us
    dot_general x1, matrix products, on_device(): lax.dot_general(target_orbitals, dipole_cont, (((0,), (0,)), ((), ())), p...  2.34 us

profile of v16, /device:TPU:1, one launch (start us, length us, event | category | flops | bytes accessed | tf_op | source)
XLA Modules:
  0.0 70.2 jit_solution(17496896430438851395)
XLA Ops:
  0.6 0.0 copy-start.1
  0.6 1.6 %copy-done.1 = bf16[4096,256]{1,0:T(8,128)(2,1)S(1)} copy-done((bf16[4096,256]{1,0:T(8,128)(2,1)S(1)}, bf16[4096,256]{1,0:T(8,128)(2,1)}, u32[]{:S(2)}) %copy-start.1) | copy-done | bytes 2097176
  2.2 0.0 copy-start.3
  2.2 0.0 slice-start
  2.2 9.3 %shard_map.68.field_ref = bf16[5120,256]{1,0:T(8,128)(2,1)S(1)} custom-call(bf16[4096,256]{1,0:T(8,128)(2,1)S(1)} %copy-done.1), custom_call_target="tpu_custom_call" | custom-call | bytes 8388608 | tf_op jit(solution)/shard_map/pallas_call | solution.py:99
  11.6 0.0 copy-done.3
  11.6 0.0 copy-start
  11.6 3.4 %copy-done = bf16[16,4,256,256]{3,2,1,0:T(8,128)(2,1)S(1)} copy-done((bf16[16,4,256,256]{3,2,1,0:T(8,128)(2,1)S(1)}, bf16[16,4,256,256]{3,2,1,0:T(8,128)(2,1)}, u32[]{:S(2)}) %copy-start) | copy-done | bytes 8388632
  15.0 0.0 slice-start.1
  15.0 0.0 slice-start.2
  15.0 3.2 %shard_map.69 = bf16[4096,256]{1,0:T(8,128)(2,1)S(1)} custom-call(s32[4,16]{1,0:T(4,128)S(1)} %bitcast.18, bf16[16,4,256,256]{3,2,1,0:T(8,128)(2,1)S(1)} %copy-done, bf16[5120,256]{1,0:T(8,128)(2,1)S(1)} %shard_map.68.field_ref), custom_call_target="tpu_custom_call" | custom-call | flops 2147483648 | bytes 13107200 | tf_op jit(solution)/shard_map/pallas_call | solution.py:253
  18.2 0.0 slice-done
  18.2 0.0 slice-done.1
  18.2 0.0 copy-start.2
  18.2 0.0 slice-start.3
  18.2 2.4 %fusion = f32[256,1024]{1,0:T(8,128)S(1)} fusion(bf16[4096,256]{1,0:T(8,128)(2,1)S(1)} %shard_map.69, bf16[4096,1024]{1,0:T(8,128)(2,1)S(1)} %bitcast.13), kind=kOutput, calls=%fused_computation.4 | convolution fusion | flops 2147483648 | bytes 11534336 | tf_op jit(solution)/shard_map/dot_general | solution.py:426
  20.6 22.0 %shard_map.70 = bf16[8,2,16,1024]{3,2,1,0:T(8,128)(2,1)S(1)} custom-call(f32[8,2,16,1024]{3,2,1,0:T(8,128)S(1)} %bitcast.16), custom_call_target="tpu_custom_call" | custom-call | bytes 16777216 | tf_op jit(solution)/shard_map/pallas_call | solution.py:371
  42.6 0.0 copy-done.2
  42.6 7.1 %shard_map.71 = (bf16[5120,256]{1,0:T(8,128)(2,1)S(1)}, f32[1,256]{1,0:T(1,128)S(1)}) custom-call(bf16[4096,1024]{1,0:T(8,128)(2,1)S(1)} %bitcast.13, bf16[256,1024]{1,0:T(8,128)(2,1)S(1)} %bitcast.17, bf16[4096,256]{1,0:T(8,128)(2,1)S(1)} %copy-done.2), custom_call_target="tpu_custom_call" | custom-call | flops 2147483648 | bytes 15204352 | tf_op jit(solution)/shard_map/pallas_call | solution.py:203
  49.7 0.0 slice-done.2
  49.7 0.0 slice-done.3
  49.7 4.1 %shard_map.72 = (bf16[4096,256]{1,0:T(8,128)(2,1)S(1)}, bf16[4096,256]{1,0:T(8,128)(2,1)}) custom-call(s32[4,16]{1,0:T(4,128)S(1)} %bitcast.19, bf16[16,4,256,256]{3,2,1,0:T(8,128)(2,1)S(1)} %bitcast.15, bf16[5120,256]{1,0:T(8,128)(2,1)S(1)} %get-tuple-element.6.field_ref), custom_call_target="tpu_custom_call" | custom-call | flops 2147483648 | bytes 13107200 | tf_op jit(solution)/shard_map/pallas_call | solution.py:253
  53.8 2.3 %convolution_bitcast_fusion = f32[1024,256]{0,1:T(8,128)S(1)} fusion(bf16[4096,256]{1,0:T(8,128)(2,1)S(1)} %get-tuple-element.8, bf16[4096,1024]{1,0:T(8,128)(2,1)S(1)} %bitcast.13), kind=kOutput, calls=%fused_computation | convolution fusion | flops 2147483648 | bytes 11534336 | tf_op jit(solution)/shard_map/dot_general | solution.py:434
  56.1 0.3 copy.7
  56.5 0.1 pad_maximum_fusion.x_ref
  56.6 12.9 %shard_map.73 = f32[72,256]{1,0:T(8,128)S(1)} custom-call(f32[8,2,72,256]{3,2,1,0:T(8,128)S(1)} %pad_maximum_fusion.x_ref), custom_call_target="tpu_custom_call" | custom-call | bytes 9437184 | tf_op jit(solution)/shard_map/pallas_call | solution.py:405
  69.5 0.6 multiply_convert_fusion
  (4 shorter events, 0.0 us)
Async XLA Ops:
  0.6 1.6 %copy-start.1 = (bf16[4096,256]{1,0:T(8,128)(2,1)S(1)}, bf16[4096,256]{1,0:T(8,128)(2,1)}, u32[]{:S(2)}) copy-start(bf16[4096,256]{1,0:T(8,128)(2,1)} %cont_ref.1) | copy-start | bytes 6291460
  2.2 9.4 %copy-start.3 = (s32[16,4]{0,1:T(4,128)S(1)}, s32[16,4]{0,1:T(4,128)}, u32[]{:S(2)}) copy-start(s32[16,4]{0,1:T(4,128)} %param.9) | copy-start | bytes 772
  2.2 15.9 %slice-start = ((s8[8388608]{0:T(1024)(128)(4,1)}), s8[4194304]{0:T(1024)(128)(4,1)S(1)}, s32[]{:S(2)}) async-start(s8[8388608]{0:T(1024)(128)(4,1)} %bitcast.12), calls=%async_computation | async-start | bytes 8388608
  11.6 3.4 %copy-start = (bf16[16,4,256,256]{3,2,1,0:T(8,128)(2,1)S(1)}, bf16[16,4,256,256]{3,2,1,0:T(8,128)(2,1)}, u32[]{:S(2)}) copy-start(bf16[16,4,256,256]{3,2,1,0:T(8,128)(2,1)} %blk_ref.2) | copy-start | bytes 25165828
  15.0 3.2 %slice-start.1 = ((s8[8388608]{0:T(1024)(128)(4,1)}), s8[4194304]{0:T(1024)(128)(4,1)S(1)}, s32[]{:S(2)}) async-start(s8[8388608]{0:T(1024)(128)(4,1)} %bitcast.12), calls=%async_computation.1 | async-start | bytes 8388608
  15.0 34.7 %slice-start.2 = ((s8[8388608]{0:T(1024)(128)(4,1)}), s8[4194304]{0:T(1024)(128)(4,1)S(1)}, s32[]{:S(2)}) async-start(s8[8388608]{0:T(1024)(128)(4,1)} %bitcast.14), calls=%async_computation.2 | async-start | bytes 8388608
  18.2 24.4 %copy-start.2 = (bf16[4096,256]{1,0:T(8,128)(2,1)S(1)}, bf16[4096,256]{1,0:T(8,128)(2,1)}, u32[]{:S(2)}) copy-start(bf16[4096,256]{1,0:T(8,128)(2,1)} %cont_ref.1) | copy-start | bytes 6291460
  18.2 31.5 %slice-start.3 = ((s8[8388608]{0:T(1024)(128)(4,1)}), s8[4194304]{0:T(1024)(128)(4,1)S(1)}, s32[]{:S(2)}) async-start(s8[8388608]{0:T(1024)(128)(4,1)} %bitcast.14), calls=%async_computation.3 | async-start | bytes 8388608

commit v17 on v16

--- a/solution.py
+++ b/solution.py
@@ -242,6 +242,37 @@
             )
             acc = term if acc is None else acc + term
         out_ref[pl.ds(r * BK, BK), :] = acc.astype(out_ref.dtype)
+
+
+def band_whole_kernel(off_ref, blk_ref, field_ref, out_ref):
+    for b in range(blk_ref.shape[0]):
+        acc = None
+        for k in range(KB):
+            start = pl.multiple_of((b + 2 + off_ref[k, b]) * BK, BK)
+            term = jnp.dot(blk_ref[b, k], field_ref[pl.ds(start, BK), :], preferred_element_type=jnp.float32)
+            acc = term if acc is None else acc + term
+        out_ref[pl.ds(b * BK, BK), :] = acc.astype(out_ref.dtype)
+
+
+def band_whole(blocks, offsets, padded):
+    nblk = blocks.shape[0]
+    rows, width = padded.shape
+    return pl.pallas_call(
+        band_whole_kernel,
+        out_shape=jax.ShapeDtypeStruct((nblk * BK, width), jnp.bfloat16),
+        in_specs=[
+            pl.BlockSpec(memory_space=pltpu.SMEM),
+            pl.BlockSpec(memory_space=pltpu.VMEM),
+            pl.BlockSpec(memory_space=pltpu.VMEM),
+        ],
+        out_specs=pl.BlockSpec(memory_space=pltpu.VMEM),
+        cost_estimate=pl.CostEstimate(
+            flops=2 * nblk * KB * BK * BK * width,
+            bytes_accessed=blocks.size * 2 + padded.size * 2 + nblk * BK * width * 2,
+            transcendentals=0,
+        ),
+        compiler_params=pltpu.CompilerParams(vmem_limit_bytes=8 * 1024 * 1024),
+    )(offsets.T, blocks, padded)
 
 
 def band_local(blocks, offsets, padded, with_middle=False):
@@ -422,7 +453,7 @@
     n = lax.axis_size("basis")
     count = band_offsets.shape[0] * BK * n
     cont_padded = with_halo(cont_orbitals, 2)
-    margin_cont = band_local(margin_blocks, band_offsets, cont_padded)
+    margin_cont = band_whole(margin_blocks, band_offsets, cont_padded)
     partial_proj_t = lax.dot_general(
         margin_cont, target_orbitals, (((0,), (0,)), ((), ())), preferred_element_type=jnp.float32
     )

time: 70.3 us -> 70 us (level)
    pallas_call x2 -> x1, Pallas kernels: 7.25 us -> 4.07 us  [band_local(): pl.pallas_call(functools.partial(band_kernel, per), out_shape=(field, fie...]
    pallas_call x0 -> x1, Pallas kernels: none -> 2.9 us  [band_whole(): pl.pallas_call(band_whole_kernel, out_shape=jax.ShapeDtypeStruct((nblk *...]
where the time goes in v17:
time: 70 us; the launch traced here: 69.8 us
  Pallas kernels  58.3 us (83%)
  local copies, waits for them, and re-layouts  5.34 us (8%)
  matrix products  4.7 us (7%)
  between operations  0.8 us (1%)
  other arithmetic  0.71 us (1%)
    pallas_call x1, Pallas kernels, allreduce_to_bf16(): pl.pallas_call(functools.partial(allreduce_kernel, nchip), out_shape=jax....  22 us
    pallas_call x1, Pallas kernels, dipole_scatter(): pl.pallas_call(functools.partial(dipole_kernel, nchip, chunk, count), out...  12.8 us
    pallas_call x1, Pallas kernels, with_halo(): pl.pallas_call(functools.partial(halo_kernel, n), out_shape=jax.ShapeDtyp...  9.34 us
    pallas_call x1, Pallas kernels, orthogonalize_with_halo(): pl.pallas_call(functools.partial(orth_halo_kernel, n), out_shape=(jax.Sha...  7.11 us
    unnamed x16, local copies, waits for them, and re-layouts  4.99 us
    pallas_call x1, Pallas kernels, band_local(): pl.pallas_call(functools.partial(band_kernel, per), out_shape=(field, fie...  4.07 us
    pallas_call x1, Pallas kernels, band_whole(): pl.pallas_call(band_whole_kernel, out_shape=jax.ShapeDtypeStruct((nblk *...  2.9 us
    dot_general x1, matrix products, on_device(): lax.dot_general(target_orbitals, dipole_cont, (((0,), (0,)), ((), ())), p...  2.35 us

profile of v17, /device:TPU:1, one launch (start us, length us, event | category | flops | bytes accessed | tf_op | source)
XLA Modules:
  0.0 69.8 jit_solution(9906992473872765534)
XLA Ops:
  0.6 0.0 copy-start.1
  0.6 1.6 %copy-done.1 = bf16[4096,256]{1,0:T(8,128)(2,1)S(1)} copy-done((bf16[4096,256]{1,0:T(8,128)(2,1)S(1)}, bf16[4096,256]{1,0:T(8,128)(2,1)}, u32[]{:S(2)}) %copy-start.1) | copy-done | bytes 2097176
  2.2 0.0 copy-start.3
  2.2 0.0 slice-start
  2.2 9.3 %shard_map.68.field_ref = bf16[5120,256]{1,0:T(8,128)(2,1)S(1)} custom-call(bf16[4096,256]{1,0:T(8,128)(2,1)S(1)} %copy-done.1), custom_call_target="tpu_custom_call" | custom-call | bytes 8388608 | tf_op jit(solution)/shard_map/pallas_call | solution.py:99
  11.6 0.0 copy-done.3
  11.6 0.0 copy-start
  11.6 3.4 %copy-done = bf16[16,4,256,256]{3,2,1,0:T(8,128)(2,1)S(1)} copy-done((bf16[16,4,256,256]{3,2,1,0:T(8,128)(2,1)S(1)}, bf16[16,4,256,256]{3,2,1,0:T(8,128)(2,1)}, u32[]{:S(2)}) %copy-start) | copy-done | bytes 8388632
  15.0 0.0 slice-start.1
  15.0 0.0 slice-start.2
  15.0 2.9 %shard_map.69 = bf16[4096,256]{1,0:T(8,128)(2,1)S(1)} custom-call(s32[4,16]{1,0:T(4,128)S(1)} %bitcast.18, bf16[16,4,256,256]{3,2,1,0:T(8,128)(2,1)S(1)} %copy-done, bf16[5120,256]{1,0:T(8,128)(2,1)S(1)} %shard_map.68.field_ref), custom_call_target="tpu_custom_call" | custom-call | flops 2147483648 | bytes 13107200 | tf_op jit(solution)/shard_map/pallas_call | solution.py:260
  17.9 0.0 slice-done
  17.9 0.0 slice-done.1
  17.9 0.0 copy-start.2
  17.9 0.0 slice-start.3
  17.9 2.3 %fusion = f32[256,1024]{1,0:T(8,128)S(1)} fusion(bf16[4096,256]{1,0:T(8,128)(2,1)S(1)} %shard_map.69, bf16[4096,1024]{1,0:T(8,128)(2,1)S(1)} %bitcast.13), kind=kOutput, calls=%fused_computation.4 | convolution fusion | flops 2147483648 | bytes 11534336 | tf_op jit(solution)/shard_map/dot_general | solution.py:457
  20.3 22.0 %shard_map.70 = bf16[8,2,16,1024]{3,2,1,0:T(8,128)(2,1)S(1)} custom-call(f32[8,2,16,1024]{3,2,1,0:T(8,128)S(1)} %bitcast.16), custom_call_target="tpu_custom_call" | custom-call | bytes 16777216 | tf_op jit(solution)/shard_map/pallas_call | solution.py:402
  42.3 0.0 copy-done.2
  42.3 7.1 %shard_map.71 = (bf16[5120,256]{1,0:T(8,128)(2,1)S(1)}, f32[1,256]{1,0:T(1,128)S(1)}) custom-call(bf16[4096,1024]{1,0:T(8,128)(2,1)S(1)} %bitcast.13, bf16[256,1024]{1,0:T(8,128)(2,1)S(1)} %bitcast.17, bf16[4096,256]{1,0:T(8,128)(2,1)S(1)} %copy-done.2), custom_call_target="tpu_custom_call" | custom-call | flops 2147483648 | bytes 15204352 | tf_op jit(solution)/shard_map/pallas_call | solution.py:203
  49.4 0.0 slice-done.2
  49.4 0.0 slice-done.3
  49.4 4.1 %shard_map.72 = (bf16[4096,256]{1,0:T(8,128)(2,1)S(1)}, bf16[4096,256]{1,0:T(8,128)(2,1)}) custom-call(s32[4,16]{1,0:T(4,128)S(1)} %bitcast.19, bf16[16,4,256,256]{3,2,1,0:T(8,128)(2,1)S(1)} %bitcast.15, bf16[5120,256]{1,0:T(8,128)(2,1)S(1)} %get-tuple-element.6.field_ref), custom_call_target="tpu_custom_call" | custom-call | flops 2147483648 | bytes 13107200 | tf_op jit(solution)/shard_map/pallas_call | solution.py:284
  53.5 2.4 %convolution_bitcast_fusion = f32[1024,256]{0,1:T(8,128)S(1)} fusion(bf16[4096,256]{1,0:T(8,128)(2,1)S(1)} %get-tuple-element.8, bf16[4096,1024]{1,0:T(8,128)(2,1)S(1)} %bitcast.13), kind=kOutput, calls=%fused_computation | convolution fusion | flops 2147483648 | bytes 11534336 | tf_op jit(solution)/shard_map/dot_general | solution.py:465
  55.9 0.3 copy.7
  56.2 0.1 pad_maximum_fusion.x_ref
  56.3 12.8 %shard_map.73 = f32[72,256]{1,0:T(8,128)S(1)} custom-call(f32[8,2,72,256]{3,2,1,0:T(8,128)S(1)} %pad_maximum_fusion.x_ref), custom_call_target="tpu_custom_call" | custom-call | bytes 9437184 | tf_op jit(solution)/shard_map/pallas_call | solution.py:436
  69.2 0.6 multiply_convert_fusion
  (4 shorter events, 0.0 us)
Async XLA Ops:
  0.6 1.6 %copy-start.1 = (bf16[4096,256]{1,0:T(8,128)(2,1)S(1)}, bf16[4096,256]{1,0:T(8,128)(2,1)}, u32[]{:S(2)}) copy-start(bf16[4096,256]{1,0:T(8,128)(2,1)} %cont_ref.1) | copy-start | bytes 6291460
  2.2 9.4 %copy-start.3 = (s32[16,4]{0,1:T(4,128)S(1)}, s32[16,4]{0,1:T(4,128)}, u32[]{:S(2)}) copy-start(s32[16,4]{0,1:T(4,128)} %param.9) | copy-start | bytes 772
  2.2 15.7 %slice-start = ((s8[8388608]{0:T(1024)(128)(4,1)}), s8[4194304]{0:T(1024)(128)(4,1)S(1)}, s32[]{:S(2)}) async-start(s8[8388608]{0:T(1024)(128)(4,1)} %bitcast.12), calls=%async_computation | async-start | bytes 8388608
  11.6 3.4 %copy-start = (bf16[16,4,256,256]{3,2,1,0:T(8,128)(2,1)S(1)}, bf16[16,4,256,256]{3,2,1,0:T(8,128)(2,1)}, u32[]{:S(2)}) copy-start(bf16[16,4,256,256]{3,2,1,0:T(8,128)(2,1)} %blk_ref.2) | copy-start | bytes 25165828
  15.0 2.9 %slice-start.1 = ((s8[8388608]{0:T(1024)(128)(4,1)}), s8[4194304]{0:T(1024)(128)(4,1)S(1)}, s32[]{:S(2)}) async-start(s8[8388608]{0:T(1024)(128)(4,1)} %bitcast.12), calls=%async_computation.1 | async-start | bytes 8388608
  15.0 34.4 %slice-start.2 = ((s8[8388608]{0:T(1024)(128)(4,1)}), s8[4194304]{0:T(1024)(128)(4,1)S(1)}, s32[]{:S(2)}) async-start(s8[8388608]{0:T(1024)(128)(4,1)} %bitcast.14), calls=%async_computation.2 | async-start | bytes 8388608
  17.9 24.4 %copy-start.2 = (bf16[4096,256]{1,0:T(8,128)(2,1)S(1)}, bf16[4096,256]{1,0:T(8,128)(2,1)}, u32[]{:S(2)}) copy-start(bf16[4096,256]{1,0:T(8,128)(2,1)} %cont_ref.1) | copy-start | bytes 6291460
  17.9 31.5 %slice-start.3 = ((s8[8388608]{0:T(1024)(128)(4,1)}), s8[4194304]{0:T(1024)(128)(4,1)S(1)}, s32[]{:S(2)}) async-start(s8[8388608]{0:T(1024)(128)(4,1)} %bitcast.14), calls=%async_computation.3 | async-start | bytes 8388608

commit v18 on v16

--- a/solution.py
+++ b/solution.py
@@ -242,6 +242,131 @@
             )
             acc = term if acc is None else acc + term
         out_ref[pl.ds(r * BK, BK), :] = acc.astype(out_ref.dtype)
+
+
+def band_whole_kernel(off_ref, blk_ref, field_ref, low_ref, high_ref, out_ref):
+    nblk = blk_ref.shape[0]
+    for b in range(nblk):
+        if b < 2:
+            src, base = low_ref, 2
+        elif b >= nblk - 2:
+            src, base = high_ref, 4 - nblk
+        else:
+            src, base = field_ref, 0
+        acc = None
+        for k in range(KB):
+            start = pl.multiple_of((b + base + off_ref[k, b]) * BK, BK)
+            term = jnp.dot(blk_ref[b, k], src[pl.ds(start, BK), :], preferred_element_type=jnp.float32)
+            acc = term if acc is None else acc + term
+        out_ref[pl.ds(b * BK, BK), :] = acc.astype(out_ref.dtype)
+
+
+def band_whole(blocks, offsets, field, edges):
+    nblk = blocks.shape[0]
+    rows, width = field.shape
+    vmem = pl.BlockSpec(memory_space=pltpu.VMEM)
+    return pl.pallas_call(
+        band_whole_kernel,
+        out_shape=jax.ShapeDtypeStruct((nblk * BK, width), jnp.bfloat16),
+        in_specs=[pl.BlockSpec(memory_space=pltpu.SMEM), vmem, vmem, vmem, vmem],
+        out_specs=vmem,
+        cost_estimate=pl.CostEstimate(
+            flops=2 * nblk * KB * BK * BK * width,
+            bytes_accessed=blocks.size * 2 + 2 * field.size * 2,
+            transcendentals=0,
+        ),
+        compiler_params=pltpu.CompilerParams(vmem_limit_bytes=8 * 1024 * 1024),
+    )(offsets.T, blocks, field, *edges)
+
+
+def edge_kernel(n, field_ref, low_out, high_out, low, high, send_sem, recv_sem):
+    rows, width = field_ref.shape
+    edge = 2 * BK
+    me = lax.axis_index("basis")
+    orb = lax.axis_index("orb")
+    has_low = me > 0
+    has_high = me < n - 1
+    barrier = pltpu.get_barrier_semaphore()
+
+    @pl.when(has_low)
+    def _():
+        pl.semaphore_signal(barrier, inc=1, device_id=(me - 1, orb), device_id_type=MESH)
+
+    @pl.when(has_high)
+    def _():
+        pl.semaphore_signal(barrier, inc=1, device_id=(me + 1, orb), device_id_type=MESH)
+
+    pl.semaphore_wait(barrier, has_low.astype(jnp.int32) + has_high.astype(jnp.int32))
+    to_low = pltpu.make_async_remote_copy(
+        src_ref=field_ref.at[pl.ds(0, edge)], dst_ref=high,
+        send_sem=send_sem.at[0], recv_sem=recv_sem.at[0],
+        device_id=(jnp.maximum(me - 1, 0), orb), device_id_type=MESH,
+    )
+    to_high = pltpu.make_async_remote_copy(
+        src_ref=field_ref.at[pl.ds(rows - edge, edge)], dst_ref=low,
+        send_sem=send_sem.at[1], recv_sem=recv_sem.at[1],
+        device_id=(jnp.minimum(me + 1, n - 1), orb), device_id_type=MESH,
+    )
+
+    @pl.when(has_low)
+    def _():
+        to_low.start()
+
+    @pl.when(has_high)
+    def _():
+        to_high.start()
+
+    low_out[pl.ds(edge, 2 * edge), :] = field_ref[pl.ds(0, 2 * edge), :]
+    high_out[pl.ds(0, 2 * edge), :] = field_ref[pl.ds(rows - 2 * edge, 2 * edge), :]
+
+    @pl.when(has_high)
+    def _():
+        to_low.wait_recv()
+        high_out[pl.ds(2 * edge, edge), :] = high[...]
+
+    @pl.when(jnp.logical_not(has_high))
+    def _():
+        high_out[pl.ds(2 * edge, edge), :] = jnp.zeros((edge, width), high_out.dtype)
+
+    @pl.when(has_low)
+    def _():
+        to_high.wait_recv()
+        low_out[pl.ds(0, edge), :] = low[...]
+
+    @pl.when(jnp.logical_not(has_low))
+    def _():
+        low_out[pl.ds(0, edge), :] = jnp.zeros((edge, width), low_out.dtype)
+
+    @pl.when(has_low)
+    def _():
+        to_low.wait_send()
+
+    @pl.when(has_high)
+    def _():
+        to_high.wait_send()
+
+
+def edges_of(field, collective_id):
+    rows, width = field.shape
+    n = lax.axis_size("basis")
+    part = jax.ShapeDtypeStruct((6 * BK, width), field.dtype)
+    vmem = pl.BlockSpec(memory_space=pltpu.VMEM)
+    return pl.pallas_call(
+        functools.partial(edge_kernel, n),
+        out_shape=(part, part),
+        in_specs=[vmem],
+        out_specs=(vmem, vmem),
+        scratch_shapes=[
+            pltpu.VMEM((2 * BK, width), field.dtype),
+            pltpu.VMEM((2 * BK, width), field.dtype),
+            pltpu.SemaphoreType.DMA((2,)),
+            pltpu.SemaphoreType.DMA((2,)),
+        ],
+        cost_estimate=pl.CostEstimate(flops=0, bytes_accessed=12 * BK * width * 2, transcendentals=0),
+        compiler_params=pltpu.CompilerParams(
+            collective_id=collective_id, has_side_effects=True, vmem_limit_bytes=8 * 1024 * 1024
+        ),
+    )(field)
 
 
 def band_local(blocks, offsets, padded, with_middle=False):
@@ -421,8 +546,8 @@
 def on_device(cont_orbitals, target_orbitals, margin_blocks, dipole_blocks, band_offsets):
     n = lax.axis_size("basis")
     count = band_offsets.shape[0] * BK * n
-    cont_padded = with_halo(cont_orbitals, 2)
-    margin_cont = band_local(margin_blocks, band_offsets, cont_padded)
+    cont_edges = edges_of(cont_orbitals, 2)
+    margin_cont = band_whole(margin_blocks, band_offsets, cont_orbitals, cont_edges)
     partial_proj_t = lax.dot_general(
         margin_cont, target_orbitals, (((0,), (0,)), ((), ())), preferred_element_type=jnp.float32
     )

time: 70.3 us -> 70.6 us (level)
    pallas_call x2 -> x1, Pallas kernels: 7.25 us -> 4.07 us  [band_local(): pl.pallas_call(functools.partial(band_kernel, per), out_shape=(field, fie...]
    pallas_call x1 -> x2, Pallas kernels: 9.34 us -> 12.1 us  [the longest x1 9.19 us: edges_of(): pl.pallas_call(functools.partial(edge_kernel, n), out_shape=(part, part),...]
where the time goes in v18:
time: 70.6 us; the launch traced here: 70.4 us
  Pallas kernels  58.2 us (82%)
  local copies, waits for them, and re-layouts  6.01 us (9%)
  matrix products  4.71 us (7%)
  between operations  0.8 us (1%)
  other arithmetic  0.71 us (1%)
    pallas_call x1, Pallas kernels, allreduce_to_bf16(): pl.pallas_call(functools.partial(allreduce_kernel, nchip), out_shape=jax....  22 us
    pallas_call x1, Pallas kernels, dipole_scatter(): pl.pallas_call(functools.partial(dipole_kernel, nchip, chunk, count), out...  12.9 us
    pallas_call x1, Pallas kernels, edges_of(): pl.pallas_call(functools.partial(edge_kernel, n), out_shape=(part, part),...  9.19 us
    pallas_call x1, Pallas kernels, orthogonalize_with_halo(): pl.pallas_call(functools.partial(orth_halo_kernel, n), out_shape=(jax.Sha...  7.11 us
    unnamed x16, local copies, waits for them, and re-layouts  5.67 us
    pallas_call x1, Pallas kernels, band_local(): pl.pallas_call(functools.partial(band_kernel, per), out_shape=(field, fie...  4.07 us
    pallas_call x1, Pallas kernels, band_whole(): pl.pallas_call(band_whole_kernel, out_shape=jax.ShapeDtypeStruct((nblk *...  2.9 us
    dot_general x1, matrix products, on_device(): lax.dot_general(margin_cont, target_orbitals, (((0,), (0,)), ((), ())), p...  2.36 us

profile of v18, /device:TPU:1, one launch (start us, length us, event | category | flops | bytes accessed | tf_op | source)
XLA Modules:
  0.0 70.4 jit_solution(9450520298873611231)
XLA Ops:
  0.6 0.0 copy-start
  0.6 1.6 %copy-done = bf16[4096,256]{1,0:T(8,128)(2,1)S(1)} copy-done((bf16[4096,256]{1,0:T(8,128)(2,1)S(1)}, bf16[4096,256]{1,0:T(8,128)(2,1)}, u32[]{:S(2)}) %copy-start) | copy-done | bytes 2097176
  2.2 0.0 slice-start
  2.2 9.2 %shard_map.68 = (bf16[1536,256]{1,0:T(8,128)(2,1)S(1)}, bf16[1536,256]{1,0:T(8,128)(2,1)S(1)}) custom-call(bf16[4096,256]{1,0:T(8,128)(2,1)S(1)} %copy-done), custom_call_target="tpu_custom_call" | custom-call | bytes 1572864 | tf_op jit(solution)/shard_map/pallas_call | solution.py:354
  11.4 0.0 copy-start.2
  11.4 3.4 %copy-done.2 = bf16[16,4,256,256]{3,2,1,0:T(8,128)(2,1)S(1)} copy-done((bf16[16,4,256,256]{3,2,1,0:T(8,128)(2,1)S(1)}, bf16[16,4,256,256]{3,2,1,0:T(8,128)(2,1)}, u32[]{:S(2)}) %copy-start.2) | copy-done | bytes 8388632
  14.8 0.0 copy-start.3
  14.8 0.7 copy-done.3
  15.5 0.0 slice-start.1
  15.5 0.0 slice-start.2
  15.5 2.9 %shard_map.69 = bf16[4096,256]{1,0:T(8,128)(2,1)S(1)} custom-call(s32[4,16]{1,0:T(4,128)S(1)} %bitcast.18, bf16[16,4,256,256]{3,2,1,0:T(8,128)(2,1)S(1)} %copy-done.2, bf16[4096,256]{1,0:T(8,128)(2,1)S(1)} %copy-done, bf16[1536,256]{1,0:T(8,128)(2,1)S(1)} %get-tuple-element.8.low_ref, bf16[1536,256]{1,0:T(8,128)(2,1)S(1)} %get-tuple-element.9.high_ref), custom_call_target="tpu_custom_call" | custom-call | flops 2147483648 | bytes 12582912 | tf_op jit(solution)/shard_map/pallas_call | solution.py:268
  18.4 0.0 slice-done
  18.4 0.0 slice-done.1
  18.4 0.0 copy-start.1
  18.4 0.0 slice-start.3
  18.5 2.4 %fusion = f32[256,1024]{1,0:T(8,128)S(1)} fusion(bf16[4096,256]{1,0:T(8,128)(2,1)S(1)} %shard_map.69, bf16[4096,1024]{1,0:T(8,128)(2,1)S(1)} %bitcast.13), kind=kOutput, calls=%fused_computation.4 | convolution fusion | flops 2147483648 | bytes 11534336 | tf_op jit(solution)/shard_map/dot_general | solution.py:551
  20.8 22.0 %shard_map.70 = bf16[8,2,16,1024]{3,2,1,0:T(8,128)(2,1)S(1)} custom-call(f32[8,2,16,1024]{3,2,1,0:T(8,128)S(1)} %bitcast.16), custom_call_target="tpu_custom_call" | custom-call | bytes 16777216 | tf_op jit(solution)/shard_map/pallas_call | solution.py:496
  42.8 0.0 copy-done.1
  42.8 7.1 %shard_map.71 = (bf16[5120,256]{1,0:T(8,128)(2,1)S(1)}, f32[1,256]{1,0:T(1,128)S(1)}) custom-call(bf16[4096,1024]{1,0:T(8,128)(2,1)S(1)} %bitcast.13, bf16[256,1024]{1,0:T(8,128)(2,1)S(1)} %bitcast.17, bf16[4096,256]{1,0:T(8,128)(2,1)S(1)} %copy-done.1), custom_call_target="tpu_custom_call" | custom-call | flops 2147483648 | bytes 15204352 | tf_op jit(solution)/shard_map/pallas_call | solution.py:203
  49.9 0.0 slice-done.2
  50.0 0.0 slice-done.3
  50.0 4.1 %shard_map.72 = (bf16[4096,256]{1,0:T(8,128)(2,1)S(1)}, bf16[4096,256]{1,0:T(8,128)(2,1)}) custom-call(s32[4,16]{1,0:T(4,128)S(1)} %bitcast.19, bf16[16,4,256,256]{3,2,1,0:T(8,128)(2,1)S(1)} %bitcast.15, bf16[5120,256]{1,0:T(8,128)(2,1)S(1)} %get-tuple-element.10.field_ref), custom_call_target="tpu_custom_call" | custom-call | flops 2147483648 | bytes 13107200 | tf_op jit(solution)/shard_map/pallas_call | solution.py:378
  54.1 2.4 %convolution_bitcast_fusion = f32[1024,256]{0,1:T(8,128)S(1)} fusion(bf16[4096,256]{1,0:T(8,128)(2,1)S(1)} %get-tuple-element.12, bf16[4096,1024]{1,0:T(8,128)(2,1)S(1)} %bitcast.13), kind=kOutput, calls=%fused_computation | convolution fusion | flops 2147483648 | bytes 11534336 | tf_op jit(solution)/shard_map/dot_general | solution.py:559
  56.4 0.3 copy.7
  56.8 0.1 pad_maximum_fusion.x_ref
  56.9 12.9 %shard_map.73 = f32[72,256]{1,0:T(8,128)S(1)} custom-call(f32[8,2,72,256]{3,2,1,0:T(8,128)S(1)} %pad_maximum_fusion.x_ref), custom_call_target="tpu_custom_call" | custom-call | bytes 9437184 | tf_op jit(solution)/shard_map/pallas_call | solution.py:530
  69.8 0.6 multiply_convert_fusion
  (4 shorter events, 0.0 us)
Async XLA Ops:
  0.6 1.6 %copy-start = (bf16[4096,256]{1,0:T(8,128)(2,1)S(1)}, bf16[4096,256]{1,0:T(8,128)(2,1)}, u32[]{:S(2)}) copy-start(bf16[4096,256]{1,0:T(8,128)(2,1)} %cont_ref.1) | copy-start | bytes 6291460
  2.2 16.2 %slice-start = ((s8[8388608]{0:T(1024)(128)(4,1)}), s8[4194304]{0:T(1024)(128)(4,1)S(1)}, s32[]{:S(2)}) async-start(s8[8388608]{0:T(1024)(128)(4,1)} %bitcast.12), calls=%async_computation | async-start | bytes 8388608
  11.4 3.4 %copy-start.2 = (bf16[16,4,256,256]{3,2,1,0:T(8,128)(2,1)S(1)}, bf16[16,4,256,256]{3,2,1,0:T(8,128)(2,1)}, u32[]{:S(2)}) copy-start(bf16[16,4,256,256]{3,2,1,0:T(8,128)(2,1)} %blk_ref.2) | copy-start | bytes 25165828
  14.8 0.7 copy-start.3
  15.5 2.9 %slice-start.1 = ((s8[8388608]{0:T(1024)(128)(4,1)}), s8[4194304]{0:T(1024)(128)(4,1)S(1)}, s32[]{:S(2)}) async-start(s8[8388608]{0:T(1024)(128)(4,1)} %bitcast.12), calls=%async_computation.1 | async-start | bytes 8388608
  15.5 34.5 %slice-start.2 = ((s8[8388608]{0:T(1024)(128)(4,1)}), s8[4194304]{0:T(1024)(128)(4,1)S(1)}, s32[]{:S(2)}) async-start(s8[8388608]{0:T(1024)(128)(4,1)} %bitcast.14), calls=%async_computation.2 | async-start | bytes 8388608
  18.4 24.4 %copy-start.1 = (bf16[4096,256]{1,0:T(8,128)(2,1)S(1)}, bf16[4096,256]{1,0:T(8,128)(2,1)}, u32[]{:S(2)}) copy-start(bf16[4096,256]{1,0:T(8,128)(2,1)} %cont_ref.1) | copy-start | bytes 6291460
  18.4 31.5 %slice-start.3 = ((s8[8388608]{0:T(1024)(128)(4,1)}), s8[4194304]{0:T(1024)(128)(4,1)S(1)}, s32[]{:S(2)}) async-start(s8[8388608]{0:T(1024)(128)(4,1)} %bitcast.14), calls=%async_computation.3 | async-start | bytes 8388608

commit v19 on v17

--- a/solution.py
+++ b/solution.py
@@ -269,6 +269,37 @@
         cost_estimate=pl.CostEstimate(
             flops=2 * nblk * KB * BK * BK * width,
             bytes_accessed=blocks.size * 2 + padded.size * 2 + nblk * BK * width * 2,
+            transcendentals=0,
+        ),
+        compiler_params=pltpu.CompilerParams(vmem_limit_bytes=8 * 1024 * 1024),
+    )(offsets.T, blocks, padded)
+
+
+def band_mid_kernel(off_ref, blk_ref, field_ref, out_ref, mid_ref, sem):
+    nblk = blk_ref.shape[0]
+    copy = pltpu.make_async_copy(field_ref.at[pl.ds(2 * BK, nblk * BK)], mid_ref, sem.at[0])
+    copy.start()
+    band_whole_kernel(off_ref, blk_ref, field_ref, out_ref)
+    copy.wait()
+
+
+def band_with_middle(blocks, offsets, padded):
+    nblk = blocks.shape[0]
+    rows, width = padded.shape
+    field = jax.ShapeDtypeStruct((nblk * BK, width), jnp.bfloat16)
+    return pl.pallas_call(
+        band_mid_kernel,
+        out_shape=(field, field),
+        in_specs=[
+            pl.BlockSpec(memory_space=pltpu.SMEM),
+            pl.BlockSpec(memory_space=pltpu.VMEM),
+            pl.BlockSpec(memory_space=pltpu.VMEM),
+        ],
+        out_specs=(pl.BlockSpec(memory_space=pltpu.VMEM), pl.BlockSpec(memory_space=pl.ANY)),
+        scratch_shapes=[pltpu.SemaphoreType.DMA((1,))],
+        cost_estimate=pl.CostEstimate(
+            flops=2 * nblk * KB * BK * BK * width,
+            bytes_accessed=blocks.size * 2 + padded.size * 2 + 2 * nblk * BK * width * 2,
             transcendentals=0,
         ),
         compiler_params=pltpu.CompilerParams(vmem_limit_bytes=8 * 1024 * 1024),
@@ -461,7 +492,7 @@
     orth_padded, squares = orthogonalize_with_halo(
         target_orbitals, projection_b_t, cont_orbitals, 3
     )
-    dipole_cont, cont_orth = band_local(dipole_blocks, band_offsets, orth_padded, True)
+    dipole_cont, cont_orth = band_with_middle(dipole_blocks, band_offsets, orth_padded)
     partial_dip = lax.dot_general(
         target_orbitals,
         dipole_cont,

time: 70 us -> 70 us (level)
  no operation moved by 1% of the time
where the time goes in v19:
time: 70 us; the launch traced here: 69.8 us
  Pallas kernels  58.3 us (83%)
  local copies, waits for them, and re-layouts  5.34 us (8%)
  matrix products  4.7 us (7%)
  between operations  0.81 us (1%)
  other arithmetic  0.71 us (1%)
    pallas_call x1, Pallas kernels, allreduce_to_bf16(): pl.pallas_call(functools.partial(allreduce_kernel, nchip), out_shape=jax....  22 us
    pallas_call x1, Pallas kernels, dipole_scatter(): pl.pallas_call(functools.partial(dipole_kernel, nchip, chunk, count), out...  12.9 us
    pallas_call x1, Pallas kernels, with_halo(): pl.pallas_call(functools.partial(halo_kernel, n), out_shape=jax.ShapeDtyp...  9.34 us
    pallas_call x1, Pallas kernels, orthogonalize_with_halo(): pl.pallas_call(functools.partial(orth_halo_kernel, n), out_shape=(jax.Sha...  7.12 us
    unnamed x16, local copies, waits for them, and re-layouts  4.99 us
    pallas_call x1, Pallas kernels, band_with_middle(): pl.pallas_call(band_mid_kernel, out_shape=(field, field), in_specs=[pl.Bl...  3.99 us
    pallas_call x1, Pallas kernels, band_whole(): pl.pallas_call(band_whole_kernel, out_shape=jax.ShapeDtypeStruct((nblk *...  2.9 us
    dot_general x1, matrix products, on_device(): lax.dot_general(target_orbitals, dipole_cont, (((0,), (0,)), ((), ())), p...  2.36 us

profile of v19, /device:TPU:1, one launch (start us, length us, event | category | flops | bytes accessed | tf_op | source)
XLA Modules:
  0.0 69.8 jit_solution(8916097351361138241)
XLA Ops:
  0.6 0.0 copy-start.1
  0.6 1.6 %copy-done.1 = bf16[4096,256]{1,0:T(8,128)(2,1)S(1)} copy-done((bf16[4096,256]{1,0:T(8,128)(2,1)S(1)}, bf16[4096,256]{1,0:T(8,128)(2,1)}, u32[]{:S(2)}) %copy-start.1) | copy-done | bytes 2097176
  2.2 0.0 copy-start.3
  2.2 0.0 slice-start
  2.2 9.3 %shard_map.68.field_ref = bf16[5120,256]{1,0:T(8,128)(2,1)S(1)} custom-call(bf16[4096,256]{1,0:T(8,128)(2,1)S(1)} %copy-done.1), custom_call_target="tpu_custom_call" | custom-call | bytes 8388608 | tf_op jit(solution)/shard_map/pallas_call | solution.py:99
  11.6 0.0 copy-done.3
  11.6 0.0 copy-start
  11.6 3.4 %copy-done = bf16[16,4,256,256]{3,2,1,0:T(8,128)(2,1)S(1)} copy-done((bf16[16,4,256,256]{3,2,1,0:T(8,128)(2,1)S(1)}, bf16[16,4,256,256]{3,2,1,0:T(8,128)(2,1)}, u32[]{:S(2)}) %copy-start) | copy-done | bytes 8388632
  15.0 0.0 slice-start.1
  15.0 0.0 slice-start.2
  15.0 2.9 %shard_map.69 = bf16[4096,256]{1,0:T(8,128)(2,1)S(1)} custom-call(s32[4,16]{1,0:T(4,128)S(1)} %bitcast.18, bf16[16,4,256,256]{3,2,1,0:T(8,128)(2,1)S(1)} %copy-done, bf16[5120,256]{1,0:T(8,128)(2,1)S(1)} %shard_map.68.field_ref), custom_call_target="tpu_custom_call" | custom-call | flops 2147483648 | bytes 13107200 | tf_op jit(solution)/shard_map/pallas_call | solution.py:260
  17.9 0.0 slice-done
  17.9 0.0 slice-done.1
  17.9 0.0 copy-start.2
  17.9 0.0 slice-start.3
  17.9 2.3 %fusion = f32[256,1024]{1,0:T(8,128)S(1)} fusion(bf16[4096,256]{1,0:T(8,128)(2,1)S(1)} %shard_map.69, bf16[4096,1024]{1,0:T(8,128)(2,1)S(1)} %bitcast.13), kind=kOutput, calls=%fused_computation.4 | convolution fusion | flops 2147483648 | bytes 11534336 | tf_op jit(solution)/shard_map/dot_general | solution.py:488
  20.3 22.0 %shard_map.70 = bf16[8,2,16,1024]{3,2,1,0:T(8,128)(2,1)S(1)} custom-call(f32[8,2,16,1024]{3,2,1,0:T(8,128)S(1)} %bitcast.16), custom_call_target="tpu_custom_call" | custom-call | bytes 16777216 | tf_op jit(solution)/shard_map/pallas_call | solution.py:433
  42.3 0.0 copy-done.2
  42.3 7.1 %shard_map.71 = (bf16[5120,256]{1,0:T(8,128)(2,1)S(1)}, f32[1,256]{1,0:T(1,128)S(1)}) custom-call(bf16[4096,1024]{1,0:T(8,128)(2,1)S(1)} %bitcast.13, bf16[256,1024]{1,0:T(8,128)(2,1)S(1)} %bitcast.17, bf16[4096,256]{1,0:T(8,128)(2,1)S(1)} %copy-done.2), custom_call_target="tpu_custom_call" | custom-call | flops 2147483648 | bytes 15204352 | tf_op jit(solution)/shard_map/pallas_call | solution.py:203
  49.4 0.0 slice-done.2
  49.4 0.0 slice-done.3
  49.4 4.0 %shard_map.72 = (bf16[4096,256]{1,0:T(8,128)(2,1)S(1)}, bf16[4096,256]{1,0:T(8,128)(2,1)}) custom-call(s32[4,16]{1,0:T(4,128)S(1)} %bitcast.19, bf16[16,4,256,256]{3,2,1,0:T(8,128)(2,1)S(1)} %bitcast.15, bf16[5120,256]{1,0:T(8,128)(2,1)S(1)} %get-tuple-element.6.field_ref), custom_call_target="tpu_custom_call" | custom-call | flops 2147483648 | bytes 15204352 | tf_op jit(solution)/shard_map/pallas_call | solution.py:290
  53.4 2.4 %convolution_bitcast_fusion = f32[1024,256]{0,1:T(8,128)S(1)} fusion(bf16[4096,256]{1,0:T(8,128)(2,1)S(1)} %get-tuple-element.8, bf16[4096,1024]{1,0:T(8,128)(2,1)S(1)} %bitcast.13), kind=kOutput, calls=%fused_computation | convolution fusion | flops 2147483648 | bytes 11534336 | tf_op jit(solution)/shard_map/dot_general | solution.py:496
  55.8 0.3 copy.7
  56.2 0.1 pad_maximum_fusion.x_ref
  56.3 12.9 %shard_map.73 = f32[72,256]{1,0:T(8,128)S(1)} custom-call(f32[8,2,72,256]{3,2,1,0:T(8,128)S(1)} %pad_maximum_fusion.x_ref), custom_call_target="tpu_custom_call" | custom-call | bytes 9437184 | tf_op jit(solution)/shard_map/pallas_call | solution.py:467
  69.2 0.6 multiply_convert_fusion
  (4 shorter events, 0.0 us)
Async XLA Ops:
  0.6 1.6 %copy-start.1 = (bf16[4096,256]{1,0:T(8,128)(2,1)S(1)}, bf16[4096,256]{1,0:T(8,128)(2,1)}, u32[]{:S(2)}) copy-start(bf16[4096,256]{1,0:T(8,128)(2,1)} %cont_ref.1) | copy-start | bytes 6291460
  2.2 9.4 %copy-start.3 = (s32[16,4]{0,1:T(4,128)S(1)}, s32[16,4]{0,1:T(4,128)}, u32[]{:S(2)}) copy-start(s32[16,4]{0,1:T(4,128)} %param.9) | copy-start | bytes 772
  2.2 15.7 %slice-start = ((s8[8388608]{0:T(1024)(128)(4,1)}), s8[4194304]{0:T(1024)(128)(4,1)S(1)}, s32[]{:S(2)}) async-start(s8[8388608]{0:T(1024)(128)(4,1)} %bitcast.12), calls=%async_computation | async-start | bytes 8388608
  11.6 3.4 %copy-start = (bf16[16,4,256,256]{3,2,1,0:T(8,128)(2,1)S(1)}, bf16[16,4,256,256]{3,2,1,0:T(8,128)(2,1)}, u32[]{:S(2)}) copy-start(bf16[16,4,256,256]{3,2,1,0:T(8,128)(2,1)} %blk_ref.2) | copy-start | bytes 25165828
  15.0 2.9 %slice-start.1 = ((s8[8388608]{0:T(1024)(128)(4,1)}), s8[4194304]{0:T(1024)(128)(4,1)S(1)}, s32[]{:S(2)}) async-start(s8[8388608]{0:T(1024)(128)(4,1)} %bitcast.12), calls=%async_computation.1 | async-start | bytes 8388608
  15.0 34.4 %slice-start.2 = ((s8[8388608]{0:T(1024)(128)(4,1)}), s8[4194304]{0:T(1024)(128)(4,1)S(1)}, s32[]{:S(2)}) async-start(s8[8388608]{0:T(1024)(128)(4,1)} %bitcast.14), calls=%async_computation.2 | async-start | bytes 8388608
  17.9 24.4 %copy-start.2 = (bf16[4096,256]{1,0:T(8,128)(2,1)S(1)}, bf16[4096,256]{1,0:T(8,128)(2,1)}, u32[]{:S(2)}) copy-start(bf16[4096,256]{1,0:T(8,128)(2,1)} %cont_ref.1) | copy-start | bytes 6291460
  17.9 31.5 %slice-start.3 = ((s8[8388608]{0:T(1024)(128)(4,1)}), s8[4194304]{0:T(1024)(128)(4,1)S(1)}, s32[]{:S(2)}) async-start(s8[8388608]{0:T(1024)(128)(4,1)} %bitcast.14), calls=%async_computation.3 | async-start | bytes 8388608

commit v20 on v17

--- a/solution.py
+++ b/solution.py
@@ -115,8 +115,10 @@
     )(field)
 
 
-def orth_halo_kernel(n, tgt_ref, proj_ref, cont_ref, pad_ref, sq_ref, orth_ref, low, high, send_sem, recv_sem):
+def orth_halo_kernel(n, tgt_ref, proj_ref, cont_ref, pad_ref, sq_ref, orth_ref, low, high, send_sem, recv_sem,
+                     proj_t):
     rows, width = cont_ref.shape
+    proj_t[...] = proj_ref[...].T
     edge = 2 * BK
     me = lax.axis_index("basis")
     orb = lax.axis_index("orb")
@@ -133,10 +135,7 @@
         pl.semaphore_signal(barrier, inc=1, device_id=(me + 1, orb), device_id_type=MESH)
 
     def tile(start):
-        removed = lax.dot_general(
-            tgt_ref[pl.ds(start, edge), :], proj_ref[...], (((1,), (1,)), ((), ())),
-            preferred_element_type=jnp.float32,
-        )
+        removed = jnp.dot(tgt_ref[pl.ds(start, edge), :], proj_t[...], preferred_element_type=jnp.float32)
         orth = (cont_ref[pl.ds(start, edge), :].astype(jnp.float32) - removed).astype(orth_ref.dtype)
         orth_ref[pl.ds(start, edge), :] = orth
         pad_ref[pl.ds(start + edge, edge), :] = orth
@@ -214,6 +213,7 @@
             pltpu.VMEM((2 * BK, width), jnp.bfloat16),
             pltpu.SemaphoreType.DMA((2,)),
             pltpu.SemaphoreType.DMA((2,)),
+            pltpu.VMEM((nt, width), jnp.bfloat16),
         ],
         cost_estimate=pl.CostEstimate(
             flops=2 * rows * nt * width,

time: 70 us -> 70 us (level)
  no operation moved by 1% of the time
where the time goes in v20:
time: 70 us; the launch traced here: 69.8 us
  Pallas kernels  58.3 us (83%)
  local copies, waits for them, and re-layouts  5.34 us (8%)
  matrix products  4.7 us (7%)
  between operations  0.8 us (1%)
  other arithmetic  0.71 us (1%)
    pallas_call x1, Pallas kernels, allreduce_to_bf16(): pl.pallas_call(functools.partial(allreduce_kernel, nchip), out_shape=jax....  22 us
    pallas_call x1, Pallas kernels, dipole_scatter(): pl.pallas_call(functools.partial(dipole_kernel, nchip, chunk, count), out...  12.8 us
    pallas_call x1, Pallas kernels, with_halo(): pl.pallas_call(functools.partial(halo_kernel, n), out_shape=jax.ShapeDtyp...  9.34 us
    pallas_call x1, Pallas kernels, orthogonalize_with_halo(): pl.pallas_call(functools.partial(orth_halo_kernel, n), out_shape=(jax.Sha...  7.16 us
    unnamed x16, local copies, waits for them, and re-layouts  4.99 us
    pallas_call x1, Pallas kernels, band_local(): pl.pallas_call(functools.partial(band_kernel, per), out_shape=(field, fie...  4.07 us
    pallas_call x1, Pallas kernels, band_whole(): pl.pallas_call(band_whole_kernel, out_shape=jax.ShapeDtypeStruct((nblk *...  2.9 us
    dot_general x1, matrix products, on_device(): lax.dot_general(target_orbitals, dipole_cont, (((0,), (0,)), ((), ())), p...  2.35 us

profile of v20, /device:TPU:1, one launch (start us, length us, event | category | flops | bytes accessed | tf_op | source)
XLA Modules:
  0.0 69.8 jit_solution(391155933667460090)
XLA Ops:
  0.6 0.0 copy-start.1
  0.6 1.6 %copy-done.1 = bf16[4096,256]{1,0:T(8,128)(2,1)S(1)} copy-done((bf16[4096,256]{1,0:T(8,128)(2,1)S(1)}, bf16[4096,256]{1,0:T(8,128)(2,1)}, u32[]{:S(2)}) %copy-start.1) | copy-done | bytes 2097176
  2.2 0.0 copy-start.3
  2.2 0.0 slice-start
  2.2 9.3 %shard_map.68.field_ref = bf16[5120,256]{1,0:T(8,128)(2,1)S(1)} custom-call(bf16[4096,256]{1,0:T(8,128)(2,1)S(1)} %copy-done.1), custom_call_target="tpu_custom_call" | custom-call | bytes 8388608 | tf_op jit(solution)/shard_map/pallas_call | solution.py:99
  11.6 0.0 copy-done.3
  11.6 0.0 copy-start
  11.6 3.4 %copy-done = bf16[16,4,256,256]{3,2,1,0:T(8,128)(2,1)S(1)} copy-done((bf16[16,4,256,256]{3,2,1,0:T(8,128)(2,1)S(1)}, bf16[16,4,256,256]{3,2,1,0:T(8,128)(2,1)}, u32[]{:S(2)}) %copy-start) | copy-done | bytes 8388632
  15.0 0.0 slice-start.1
  15.0 0.0 slice-start.2
  15.0 2.9 %shard_map.69 = bf16[4096,256]{1,0:T(8,128)(2,1)S(1)} custom-call(s32[4,16]{1,0:T(4,128)S(1)} %bitcast.18, bf16[16,4,256,256]{3,2,1,0:T(8,128)(2,1)S(1)} %copy-done, bf16[5120,256]{1,0:T(8,128)(2,1)S(1)} %shard_map.68.field_ref), custom_call_target="tpu_custom_call" | custom-call | flops 2147483648 | bytes 13107200 | tf_op jit(solution)/shard_map/pallas_call | solution.py:260
  17.9 0.0 slice-done
  17.9 0.0 slice-done.1
  17.9 0.0 copy-start.2
  17.9 0.0 slice-start.3
  17.9 2.3 %fusion = f32[256,1024]{1,0:T(8,128)S(1)} fusion(bf16[4096,256]{1,0:T(8,128)(2,1)S(1)} %shard_map.69, bf16[4096,1024]{1,0:T(8,128)(2,1)S(1)} %bitcast.13), kind=kOutput, calls=%fused_computation.4 | convolution fusion | flops 2147483648 | bytes 11534336 | tf_op jit(solution)/shard_map/dot_general | solution.py:457
  20.3 22.0 %shard_map.70 = bf16[8,2,16,1024]{3,2,1,0:T(8,128)(2,1)S(1)} custom-call(f32[8,2,16,1024]{3,2,1,0:T(8,128)S(1)} %bitcast.16), custom_call_target="tpu_custom_call" | custom-call | bytes 16777216 | tf_op jit(solution)/shard_map/pallas_call | solution.py:402
  42.3 0.0 copy-done.2
  42.3 7.2 %shard_map.71 = (bf16[5120,256]{1,0:T(8,128)(2,1)S(1)}, f32[1,256]{1,0:T(1,128)S(1)}) custom-call(bf16[4096,1024]{1,0:T(8,128)(2,1)S(1)} %bitcast.13, bf16[256,1024]{1,0:T(8,128)(2,1)S(1)} %bitcast.17, bf16[4096,256]{1,0:T(8,128)(2,1)S(1)} %copy-done.2), custom_call_target="tpu_custom_call" | custom-call | flops 2147483648 | bytes 15204352 | tf_op jit(solution)/shard_map/pallas_call | solution.py:202
  49.5 0.0 slice-done.2
  49.5 0.0 slice-done.3
  49.5 4.1 %shard_map.72 = (bf16[4096,256]{1,0:T(8,128)(2,1)S(1)}, bf16[4096,256]{1,0:T(8,128)(2,1)}) custom-call(s32[4,16]{1,0:T(4,128)S(1)} %bitcast.19, bf16[16,4,256,256]{3,2,1,0:T(8,128)(2,1)S(1)} %bitcast.15, bf16[5120,256]{1,0:T(8,128)(2,1)S(1)} %get-tuple-element.6.field_ref), custom_call_target="tpu_custom_call" | custom-call | flops 2147483648 | bytes 13107200 | tf_op jit(solution)/shard_map/pallas_call | solution.py:284
  53.6 2.4 %convolution_bitcast_fusion = f32[1024,256]{0,1:T(8,128)S(1)} fusion(bf16[4096,256]{1,0:T(8,128)(2,1)S(1)} %get-tuple-element.8, bf16[4096,1024]{1,0:T(8,128)(2,1)S(1)} %bitcast.13), kind=kOutput, calls=%fused_computation | convolution fusion | flops 2147483648 | bytes 11534336 | tf_op jit(solution)/shard_map/dot_general | solution.py:465
  55.9 0.3 copy.7
  56.3 0.1 pad_maximum_fusion.x_ref
  56.4 12.8 %shard_map.73 = f32[72,256]{1,0:T(8,128)S(1)} custom-call(f32[8,2,72,256]{3,2,1,0:T(8,128)S(1)} %pad_maximum_fusion.x_ref), custom_call_target="tpu_custom_call" | custom-call | bytes 9437184 | tf_op jit(solution)/shard_map/pallas_call | solution.py:436
  69.2 0.6 multiply_convert_fusion
  (4 shorter events, 0.0 us)
Async XLA Ops:
  0.6 1.6 %copy-start.1 = (bf16[4096,256]{1,0:T(8,128)(2,1)S(1)}, bf16[4096,256]{1,0:T(8,128)(2,1)}, u32[]{:S(2)}) copy-start(bf16[4096,256]{1,0:T(8,128)(2,1)} %cont_ref.1) | copy-start | bytes 6291460
  2.2 9.4 %copy-start.3 = (s32[16,4]{0,1:T(4,128)S(1)}, s32[16,4]{0,1:T(4,128)}, u32[]{:S(2)}) copy-start(s32[16,4]{0,1:T(4,128)} %param.9) | copy-start | bytes 772
  2.2 15.7 %slice-start = ((s8[8388608]{0:T(1024)(128)(4,1)}), s8[4194304]{0:T(1024)(128)(4,1)S(1)}, s32[]{:S(2)}) async-start(s8[8388608]{0:T(1024)(128)(4,1)} %bitcast.12), calls=%async_computation | async-start | bytes 8388608
  11.6 3.4 %copy-start = (bf16[16,4,256,256]{3,2,1,0:T(8,128)(2,1)S(1)}, bf16[16,4,256,256]{3,2,1,0:T(8,128)(2,1)}, u32[]{:S(2)}) copy-start(bf16[16,4,256,256]{3,2,1,0:T(8,128)(2,1)} %blk_ref.2) | copy-start | bytes 25165828
  15.0 2.9 %slice-start.1 = ((s8[8388608]{0:T(1024)(128)(4,1)}), s8[4194304]{0:T(1024)(128)(4,1)S(1)}, s32[]{:S(2)}) async-start(s8[8388608]{0:T(1024)(128)(4,1)} %bitcast.12), calls=%async_computation.1 | async-start | bytes 8388608
  15.0 34.5 %slice-start.2 = ((s8[8388608]{0:T(1024)(128)(4,1)}), s8[4194304]{0:T(1024)(128)(4,1)S(1)}, s32[]{:S(2)}) async-start(s8[8388608]{0:T(1024)(128)(4,1)} %bitcast.14), calls=%async_computation.2 | async-start | bytes 8388608
  17.9 24.4 %copy-start.2 = (bf16[4096,256]{1,0:T(8,128)(2,1)S(1)}, bf16[4096,256]{1,0:T(8,128)(2,1)}, u32[]{:S(2)}) copy-start(bf16[4096,256]{1,0:T(8,128)(2,1)} %cont_ref.1) | copy-start | bytes 6291460
  17.9 31.6 %slice-start.3 = ((s8[8388608]{0:T(1024)(128)(4,1)}), s8[4194304]{0:T(1024)(128)(4,1)S(1)}, s32[]{:S(2)}) async-start(s8[8388608]{0:T(1024)(128)(4,1)} %bitcast.14), calls=%async_computation.3 | async-start | bytes 8388608
